TPU v7x, 32 devices: a whole 2x2x4 slice. The times are simulated.
32 devices in a mesh: fsdp: 4 (over z), ctx: 2 (over x), tp: 4 (over y, core).
Axes of the slice: x: 2, y: 2, z: 4, core: 2. Of those that a mesh axis runs over, the one named last changes fastest.
Arguments:
- tokens: bfloat16 [4, 2048, 2048], P('fsdp', 'ctx'), may hold values from -6 to 6
- segments: int32 [4, 2048], P('fsdp'), may hold values from 0 to 7, never falling along the last dimension, each value on 1 to 1024 neighbouring positions
- cotangent: bfloat16 [4, 2048, 2048], P('fsdp', 'ctx'), may hold values from -6 to 6
- gain_mix: float32 [2048], replicated, may hold values from 0.5 to 1.5
- w_branch: bfloat16 [2048, 2560], P('fsdp', 'tp'), may hold values from -0.125 to 0.125
- w_input: bfloat16 [2048, 2560], P('fsdp', 'tp'), may hold values from -0.125 to 0.125
- conv_weight: float32 [4, 2560], P(None, 'tp'), may hold values from -3 to 3
- conv_bias: float32 [2560], P('tp'), may hold values from -1.75 to 1.75
- gate_a: bfloat16 [16, 160, 160], P('tp'), may hold values from -0.5 to 0.5
- bias_a: float32 [2560], P('tp'), may hold values from -3 to 3
- gate_x: bfloat16 [16, 160, 160], P('tp'), may hold values from -0.5 to 0.5
- bias_x: float32 [2560], P('tp'), may hold values from -3 to 3
- decay_param: float32 [2560], P('tp'), may hold values from 4 to 8
- w_out: bfloat16 [2560, 2048], P('tp', 'fsdp'), may hold values from -0.3125 to 0.3125
- gain_mlp: float32 [2048], replicated, may hold values from 0.5 to 1.5
- w_gate: bfloat16 [2048, 6144], P('fsdp', 'tp'), may hold values from -0.125 to 0.125
- w_up: bfloat16 [2048, 6144], P('fsdp', 'tp'), may hold values from -0.125 to 0.125
- w_down: bfloat16 [6144, 2048], P('tp', 'fsdp'), may hold values from -0.15625 to 0.15625
Outputs:
- output: bfloat16 [4, 2048, 2048], P('fsdp', 'ctx')
- grad_tokens: bfloat16 [4, 2048, 2048], P('fsdp', 'ctx')
- grad_gain_mix: float32 [2048], replicated
- grad_w_branch: float32 [2048, 2560], P('fsdp', 'tp')
- grad_w_input: float32 [2048, 2560], P('fsdp', 'tp')
- grad_conv_weight: float32 [4, 2560], P(None, 'tp')
- grad_conv_bias: float32 [2560], P('tp')
- grad_gate_a: float32 [16, 160, 160], P('tp')
- grad_bias_a: float32 [2560], P('tp')
- grad_gate_x: float32 [16, 160, 160], P('tp')
- grad_bias_x: float32 [2560], P('tp')
- grad_decay_param: float32 [2560], P('tp')
- grad_w_out: float32 [2560, 2048], P('tp', 'fsdp')
- grad_gain_mlp: float32 [2048], replicated
- grad_w_gate: float32 [2048, 6144], P('fsdp', 'tp')
- grad_w_up: float32 [2048, 6144], P('fsdp', 'tp')
- grad_w_down: float32 [6144, 2048], P('tp', 'fsdp')
Inputs may be any that keep to these rules, and one draw needn't show every extreme that they name: `segments`: within a sequence the document numbers never fall; every document has 1 to 1024 positions and one has exactly 1024.
All inputs are finite; a program needn't handle non-finite values.
Results may differ from a plain program's by a relative error of at most 0.012.
Values may be sent and summed in bfloat16 or wider, within the bound.
A program may use at most 256 MiB of HBM per device.

v0:
```python
import jax
import jax.numpy as jnp
from jax import lax
from jax.sharding import PartitionSpec as P

EPSILON = 1e-06
RATE_SCALE = 8.0


def passed_along(block, axis, distance):
    devices = range(lax.axis_size(axis))
    route = [(i - distance, i) for i in devices if i - distance in devices]
    return lax.ppermute(block, axis, route)


def entering_2(x, axis, combine, identity, reverse):
    length, place = (lax.axis_size(axis), lax.axis_index(axis))
    everything = jax.tree.map(lambda part: lax.all_gather(part, axis), x)
    start = jax.tree.map(
        lambda part, zero: jnp.broadcast_to(jnp.asarray(zero, part.dtype), part.shape), x, identity
    )

    def turn(k, before):
        at = length - 1 - k if reverse else k
        reached = at > place if reverse else at < place
        new = combine(before, jax.tree.map(lambda part: part[at], everything))
        return jax.tree.map(lambda a, b: jnp.where(reached, a, b), new, before)

    return lax.fori_loop(0, length, turn, start)


def linear_combine(earlier, later):
    return (earlier[0] * later[0], later[0] * earlier[1] + later[1])


def matmul(left, right):
    return jnp.dot(left, right, preferred_element_type=jnp.float32)


def left_inner(left, right):
    return lax.dot_general(
        left, right, (((0,), (0,)), ((), ())), preferred_element_type=jnp.float32
    )


def right_inner(left, right):
    return lax.dot_general(
        left, right, (((1,), (1,)), ((), ())), preferred_element_type=jnp.float32
    )


def gelu_slope(values):
    result, pull_back = jax.vjp(lambda inner_v: jax.nn.gelu(inner_v, approximate=True), values)
    return (result, pull_back(jnp.ones_like(values))[0])


def rms_rows(values):
    return lax.rsqrt(jnp.mean(values * values, axis=-1, keepdims=True) + EPSILON)


def norm_back(grad_norm, scaled, scale_row, gain):
    grad_scaled = grad_norm * gain
    return scale_row * (
        grad_scaled - scaled * jnp.mean(grad_scaled * scaled, axis=-1, keepdims=True)
    )


def shards(
    tokens,
    segments,
    cotangent,
    gain_mix,
    w_branch,
    w_input,
    conv_weight,
    conv_bias,
    gate_a,
    bias_a,
    gate_x,
    bias_x,
    decay_param,
    w_out,
    gain_mlp,
    w_gate,
    w_up,
    w_down,
):
    full_branch, full_input, full_gate, full_up, full_out, full_down = (
        lax.all_gather(w_branch, "fsdp", axis=0, tiled=True),
        lax.all_gather(w_input, "fsdp", axis=0, tiled=True),
        lax.all_gather(w_gate, "fsdp", axis=0, tiled=True),
        lax.all_gather(w_up, "fsdp", axis=0, tiled=True),
        lax.all_gather(w_out, "fsdp", axis=1, tiled=True),
        lax.all_gather(w_down, "fsdp", axis=1, tiled=True),
    )
    seq_count, tok_count, model_width = tokens.shape
    row_count = seq_count * tok_count
    kernel = conv_weight.shape[0]
    lag_rows = kernel - 1
    local_width = conv_bias.shape[0]
    head_count = gate_a.shape[0]
    block_width = gate_a.shape[1]
    inputs = tokens.reshape(row_count, model_width).astype(jnp.float32)
    scale_mix = rms_rows(inputs)
    scaled_mix = inputs * scale_mix
    normed = (scaled_mix * gain_mix).astype(jnp.bfloat16)
    branch_pre = matmul(normed, full_branch)
    branch, branch_slope = gelu_slope(branch_pre)
    conv_in = (
        matmul(normed, full_input).astype(jnp.bfloat16).reshape(seq_count, tok_count, local_width)
    )
    first_pos = lax.axis_index("ctx") * tok_count
    padded_seg = jnp.pad(segments, ((0, 0), (lag_rows, lag_rows)), constant_values=-1)
    near_seg = lax.dynamic_slice_in_dim(padded_seg, first_pos, tok_count + 2 * lag_rows, 1)
    own_seg = near_seg[:, lag_rows : lag_rows + tok_count]
    same_back = [
        near_seg[:, lag_rows - offset : lag_rows - offset + tok_count] == own_seg
        for offset in range(kernel)
    ]
    same_ahead = [
        near_seg[:, lag_rows + offset : lag_rows + offset + tok_count] == own_seg
        for offset in range(kernel)
    ]
    tail_rows = passed_along(conv_in[:, tok_count - lag_rows :], "ctx", 1)
    conv_ext = jnp.concatenate([tail_rows, conv_in], axis=1)
    conv_sum = jnp.zeros((seq_count, tok_count, local_width), jnp.float32) + conv_bias
    for offset in range(kernel):
        earlier_in = jnp.where(
            same_back[offset][..., None],
            conv_ext[:, lag_rows - offset : lag_rows - offset + tok_count],
            0.0,
        )
        conv_sum = conv_sum + conv_weight[offset] * earlier_in
    conv_out = conv_sum.astype(jnp.bfloat16)
    conv_heads = conv_out.reshape(seq_count, tok_count, head_count, block_width)
    pre_a = (
        jnp.einsum(
            "sthi,hij->sthj", conv_heads, gate_a, preferred_element_type=jnp.float32
        ).reshape(seq_count, tok_count, local_width)
        + bias_a
    )
    pre_x = (
        jnp.einsum(
            "sthi,hij->sthj", conv_heads, gate_x, preferred_element_type=jnp.float32
        ).reshape(seq_count, tok_count, local_width)
        + bias_x
    )
    recur_gate = jax.nn.sigmoid(pre_a)
    input_gate = jax.nn.sigmoid(pre_x)
    softened = jax.nn.softplus(-decay_param)
    log_decay = -RATE_SCALE * softened * recur_gate
    decay = jnp.exp(log_decay)
    root_term = jnp.sqrt(-jnp.expm1(2.0 * log_decay))
    starts = jnp.logical_not(same_back[1])[..., None]
    multiplier = jnp.where(starts, 1.0, root_term)
    carry_factor = jnp.where(starts, 0.0, decay)
    conv_float = conv_out.astype(jnp.float32)
    driven = input_gate * conv_float * multiplier
    decay_run, local_states = lax.associative_scan(linear_combine, (carry_factor, driven), axis=1)
    ones_state = jnp.ones((seq_count, local_width), jnp.float32)
    zero_state = jnp.zeros((seq_count, local_width), jnp.float32)
    entering = entering_2(
        (decay_run[:, -1], local_states[:, -1]),
        "ctx",
        linear_combine,
        (ones_state, zero_state),
        False,
    )[1]
    states = local_states + decay_run * entering[:, None]
    states_rows = states.reshape(row_count, local_width)
    mixed_out = (states_rows * branch).astype(jnp.bfloat16)
    mixer_term = matmul(mixed_out, full_out)
    resid_rows = inputs + lax.psum(mixer_term, "tp")
    scale_mlp = rms_rows(resid_rows)
    scaled_mlp = resid_rows * scale_mlp
    normed_mlp = (scaled_mlp * gain_mlp).astype(jnp.bfloat16)
    gate_pre = matmul(normed_mlp, full_gate)
    up_pre = matmul(normed_mlp, full_up)
    gate_act, gate_slope = gelu_slope(gate_pre)
    hidden = (gate_act * up_pre).astype(jnp.bfloat16)
    down_term = matmul(hidden, full_down)
    output = (resid_rows + lax.psum(down_term, "tp")).astype(jnp.bfloat16)
    grad_low = cotangent.reshape(row_count, model_width)
    grad_out = grad_low.astype(jnp.float32)
    grad_w_down = left_inner(hidden, grad_low)
    grad_hidden = right_inner(grad_low, full_down)
    grad_gate = (grad_hidden * up_pre * gate_slope).astype(jnp.bfloat16)
    grad_up = (grad_hidden * gate_act).astype(jnp.bfloat16)
    grad_w_gate = left_inner(normed_mlp, grad_gate)
    grad_w_up = left_inner(normed_mlp, grad_up)
    mlp_back_term = right_inner(grad_gate, full_gate) + right_inner(grad_up, full_up)
    grad_norm_mlp = lax.psum(mlp_back_term, "tp")
    grad_resid = grad_out + norm_back(grad_norm_mlp, scaled_mlp, scale_mlp, gain_mlp)
    grad_proj = grad_resid.astype(jnp.bfloat16)
    grad_gain_mlp = jnp.sum(grad_norm_mlp * scaled_mlp, axis=0)
    grad_w_out = left_inner(mixed_out, grad_proj)
    grad_mixed = right_inner(grad_proj, full_out)
    grad_branch = (grad_mixed * states_rows * branch_slope).astype(jnp.bfloat16)
    grad_states = (grad_mixed * branch).reshape(seq_count, tok_count, local_width)
    next_factor = jnp.concatenate(
        [carry_factor[:, 1:], jnp.ones((seq_count, 1, local_width), jnp.float32)], axis=1
    )
    run_back, local_back = lax.associative_scan(
        linear_combine, (jnp.flip(next_factor, 1), jnp.flip(grad_states, 1)), axis=1
    )
    run_back = jnp.flip(run_back, 1)
    local_back = jnp.flip(local_back, 1)
    leaving = (carry_factor[:, 0] * run_back[:, 0], carry_factor[:, 0] * local_back[:, 0])
    arriving = entering_2(leaving, "ctx", linear_combine, (ones_state, zero_state), True)[1]
    grad_total = local_back + run_back * arriving[:, None]
    prev_states = jnp.concatenate([entering[:, None], states[:, :-1]], axis=1)
    grad_mult = grad_total * input_gate * conv_float
    grad_log = jnp.where(
        starts, 0.0, grad_total * prev_states * decay - grad_mult * decay * decay / root_term
    )
    grad_decay_param = (
        RATE_SCALE * jax.nn.sigmoid(-decay_param) * jnp.sum(grad_log * recur_gate, axis=(0, 1))
    )
    grad_pre_a = (grad_log * (-RATE_SCALE * softened) * recur_gate * (1.0 - recur_gate)).astype(
        jnp.bfloat16
    )
    grad_pre_x = (grad_total * conv_float * multiplier * input_gate * (1.0 - input_gate)).astype(
        jnp.bfloat16
    )
    heads_a = grad_pre_a.reshape(seq_count, tok_count, head_count, block_width)
    heads_x = grad_pre_x.reshape(seq_count, tok_count, head_count, block_width)
    grad_gate_a = jnp.einsum(
        "sthi,sthj->hij", conv_heads, heads_a, preferred_element_type=jnp.float32
    )
    grad_gate_x = jnp.einsum(
        "sthi,sthj->hij", conv_heads, heads_x, preferred_element_type=jnp.float32
    )
    grad_bias_a = jnp.sum(grad_pre_a.astype(jnp.float32), axis=(0, 1))
    grad_bias_x = jnp.sum(grad_pre_x.astype(jnp.float32), axis=(0, 1))
    gate_back = jnp.einsum(
        "sthj,hij->sthi", heads_a, gate_a, preferred_element_type=jnp.float32
    ) + jnp.einsum("sthj,hij->sthi", heads_x, gate_x, preferred_element_type=jnp.float32)
    grad_conv = grad_total * input_gate * multiplier + gate_back.reshape(
        seq_count, tok_count, local_width
    )
    head_rows = passed_along(grad_conv[:, :lag_rows], "ctx", -1)
    grad_ext = jnp.concatenate([grad_conv, head_rows], axis=1)
    grad_conv_in = jnp.zeros((seq_count, tok_count, local_width), jnp.float32)
    weight_rows = []
    for offset in range(kernel):
        later_grad = jnp.where(
            same_ahead[offset][..., None], grad_ext[:, offset : offset + tok_count], 0.0
        )
        grad_conv_in = grad_conv_in + conv_weight[offset] * later_grad
        earlier_in = jnp.where(
            same_back[offset][..., None],
            conv_ext[:, lag_rows - offset : lag_rows - offset + tok_count],
            0.0,
        )
        weight_rows.append(jnp.sum(grad_conv * earlier_in, axis=(0, 1)))
    grad_conv_weight = jnp.stack(weight_rows)
    grad_conv_bias = jnp.sum(grad_conv, axis=(0, 1))
    grad_in_low = grad_conv_in.astype(jnp.bfloat16).reshape(row_count, local_width)
    grad_w_input = left_inner(normed, grad_in_low)
    grad_w_branch = left_inner(normed, grad_branch)
    mix_back_term = right_inner(grad_in_low, full_input) + right_inner(grad_branch, full_branch)
    grad_norm_mix = lax.psum(mix_back_term, "tp")
    grad_gain_mix = jnp.sum(grad_norm_mix * scaled_mix, axis=0)
    grad_tokens = (grad_resid + norm_back(grad_norm_mix, scaled_mix, scale_mix, gain_mix)).astype(
        jnp.bfloat16
    )
    owned = (
        lax.psum_scatter(grad_w_branch, "fsdp", scatter_dimension=0, tiled=True),
        lax.psum_scatter(grad_w_input, "fsdp", scatter_dimension=0, tiled=True),
        lax.psum_scatter(grad_w_gate, "fsdp", scatter_dimension=0, tiled=True),
        lax.psum_scatter(grad_w_up, "fsdp", scatter_dimension=0, tiled=True),
        lax.psum_scatter(grad_w_out, "fsdp", scatter_dimension=1, tiled=True),
        lax.psum_scatter(grad_w_down, "fsdp", scatter_dimension=1, tiled=True),
    )
    owned_branch, owned_input, owned_gate, owned_up, owned_out, owned_down = owned
    summed = lax.psum(
        (owned_branch, owned_input, owned_gate, owned_up, owned_out, owned_down), "ctx"
    )
    sum_branch, sum_input, sum_gate, sum_up, sum_out, sum_down = summed
    small_sums = lax.psum(
        (
            grad_gain_mix,
            grad_gain_mlp,
            grad_conv_weight,
            grad_conv_bias,
            grad_gate_a,
            grad_bias_a,
            grad_gate_x,
            grad_bias_x,
            grad_decay_param,
        ),
        ("fsdp", "ctx"),
    )
    (
        sum_gain_mix,
        sum_gain_mlp,
        sum_conv_weight,
        sum_conv_bias,
        sum_gate_a,
        sum_bias_a,
        sum_gate_x,
        sum_bias_x,
        sum_decay,
    ) = small_sums
    return (
        output.reshape(seq_count, tok_count, model_width),
        grad_tokens.reshape(seq_count, tok_count, model_width),
        sum_gain_mix,
        sum_branch,
        sum_input,
        sum_conv_weight,
        sum_conv_bias,
        sum_gate_a,
        sum_bias_a,
        sum_gate_x,
        sum_bias_x,
        sum_decay,
        sum_out,
        sum_gain_mlp,
        sum_gate,
        sum_up,
        sum_down,
    )


def solution(mesh):
    in_specs = (
        P("fsdp", "ctx", None),
        P("fsdp", None),
        P("fsdp", "ctx", None),
        P(),
        P("fsdp", "tp"),
        P("fsdp", "tp"),
        P(None, "tp"),
        P("tp"),
        P("tp", None, None),
        P("tp"),
        P("tp", None, None),
        P("tp"),
        P("tp"),
        P("tp", "fsdp"),
        P(),
        P("fsdp", "tp"),
        P("fsdp", "tp"),
        P("tp", "fsdp"),
    )
    out_specs = (
        P("fsdp", "ctx", None),
        P("fsdp", "ctx", None),
        P(),
        P("fsdp", "tp"),
        P("fsdp", "tp"),
        P(None, "tp"),
        P("tp"),
        P("tp", None, None),
        P("tp"),
        P("tp", None, None),
        P("tp"),
        P("tp"),
        P("tp", "fsdp"),
        P(),
        P("fsdp", "tp"),
        P("fsdp", "tp"),
        P("tp", "fsdp"),
    )
    return jax.shard_map(shards, mesh=mesh, in_specs=in_specs, out_specs=out_specs, check_vma=False)
```

profile of v0, /device:TPU:0, one launch (start us, length us, event | category | flops | bytes accessed | tf_op | source)
XLA Modules:
  0.0 3015.6 jit_solution(510944161602865288)
XLA Ops:
  13.5 53.5 %all-gather.7.cloned.1.call-done = bf16[2048,640]{1,0:T(8,128)(2,1)} async-done(((bf16[512,640]{1,0:T(8,128)(2,1)}), bf16[2048,640]{1,0:T(8,128)(2,1)}) %all-gather.7.cloned.1.call-update) | async-done | bytes 2621456 | tf_op jit(solution)/shard_map/all_gather | solution.py:90
  100.3 7.1 slice.691
  327.6 9.0 pad.269
  336.7 9.0 pad.270
  348.2 9.0 pad.289
  357.2 9.0 pad.290
  376.8 12.8 fusion.76
  389.7 8.9 fusion.138
  400.5 150.4 %all-reduce.93.cloned.1.call-done = f32[1024,2048]{1,0:T(8,128)} async-done(((f32[1024,2048]{1,0:T(8,128)}), f32[1024,2048]{1,0:T(8,128)}) %all-reduce.93.cloned.1.call-update) | async-done | bytes 8388624 | tf_op jit(solution)/shard_map/psum | solution.py:173
  562.8 105.0 %all-gather.13.cloned.1.call-done = bf16[2048,1536]{1,0:T(8,128)(2,1)} async-done(((bf16[512,1536]{1,0:T(8,128)(2,1)}), bf16[2048,1536]{1,0:T(8,128)(2,1)}) %all-gather.13.cloned.1.call-update) | async-done | bytes 6291472 | tf_op jit(solution)/shard_map/all_gather | solution.py:91
  667.8 12.2 fusion.139
  680.1 102.7 %all-gather.15.cloned.1.call-done = bf16[2048,1536]{1,0:T(8,128)(2,1)} async-done(((bf16[512,1536]{1,0:T(8,128)(2,1)}), bf16[2048,1536]{1,0:T(8,128)(2,1)}) %all-gather.15.cloned.1.call-update) | async-done | bytes 6291472 | tf_op jit(solution)/shard_map/all_gather | solution.py:92
  782.8 11.7 fusion.140
  794.5 103.4 %all-gather.17.cloned.1.call-done = bf16[1536,2048]{1,0:T(8,128)(2,1)} async-done(((bf16[1536,512]{1,0:T(8,128)(2,1)}), bf16[1536,2048]{1,0:T(8,128)(2,1)}) %all-gather.17.cloned.1.call-update) | async-done | bytes 6291472 | tf_op jit(solution)/shard_map/all_gather | solution.py:94
  897.9 18.2 multiply_convert_fusion.1
  916.2 10.0 fusion.142
  926.2 10.7 convolution_add_fusion.1
  936.9 151.2 %all-reduce.95.cloned.1.call-done = f32[1024,2048]{1,0:T(8,128)} async-done(((f32[1024,2048]{1,0:T(8,128)}), f32[1024,2048]{1,0:T(8,128)}) %all-reduce.95.cloned.1.call-update) | async-done | bytes 8388624 | tf_op jit(solution)/shard_map/psum | solution.py:192
  1088.1 7.6 multiply_reduce_fusion
  1112.0 7.1 slice.788
  1133.2 10.7 slice.789
  1143.9 10.7 slice.794
  1154.6 11.1 slice.787
  1165.7 12.5 fusion.54
  1178.1 20.8 reverse.9
  1333.1 8.7 fusion.115
  1402.0 9.2 pad.330
  1426.0 9.3 pad.310
  1441.3 9.2 pad.309
  1453.0 9.2 pad.329
  1478.2 20.8 rev.13
  1499.0 20.9 rev.12
  1520.0 7.1 multiply_reduce_fusion.3
  1544.8 8.9 fusion.44
  1568.6 12.6 fusion.145
  1581.3 12.5 fusion.146
  1593.8 12.2 fusion.30
  1606.2 12.1 fusion.141
  1632.3 29.5 reduce-scatter.9.cloned.1.call-done
  1661.8 214.6 %reduce-scatter.13.cloned.1.call-done = f32[512,1536]{1,0:T(8,128)} async-done(((f32[2048,1536]{1,0:T(8,128)}), f32[512,1536]{1,0:T(8,128)}) %reduce-scatter.13.cloned.1.call-update) | async-done | bytes 3145744 | tf_op jit(solution)/shard_map/reduce_scatter | solution.py:270
  1876.4 215.3 %reduce-scatter.15.cloned.1.call-done = f32[512,1536]{1,0:T(8,128)} async-done(((f32[2048,1536]{1,0:T(8,128)}), f32[512,1536]{1,0:T(8,128)}) %reduce-scatter.15.cloned.1.call-update) | async-done | bytes 3145744 | tf_op jit(solution)/shard_map/reduce_scatter | solution.py:271
  2091.7 215.2 %reduce-scatter.17.cloned.1.call-done = f32[1536,512]{1,0:T(8,128)} async-done(((f32[1536,2048]{1,0:T(8,128)}), f32[1536,512]{1,0:T(8,128)}) %reduce-scatter.17.cloned.1.call-update) | async-done | bytes 3145744 | tf_op jit(solution)/shard_map/reduce_scatter | solution.py:273
  2307.6 291.2 %all-reduce.99.cloned.1.call-done = (f32[1024,2048]{1,0:T(8,128)}, f32[1024,2048]{1,0:T(8,128)}) async-done(((f32[1024,2048]{1,0:T(8,128)}, f32[1024,2048]{1,0:T(8,128)}), (f32[1024,2048]{1,0:T(8,128)}, f32[1024,2048]{1,0:T(8,128)})) %all-reduce.99.cloned.1.call-update) | async-done | bytes 16777232 | tf_op jit(solution)/shard_map/psum | solution.py:182
  2604.6 39.3 %all-reduce.83 = (f32[2048]{0:T(1024)}, f32[4,640]{1,0:T(4,128)}, f32[640]{0:T(1024)}, f32[640]{0:T(1024)}, f32[640]{0:T(1024)}, /*index=5*/f32[640]{0:T(1024)}, f32[2048]{0:T(1024)}) all-reduce(f32[2048]{0:T(1024)S(1)} %get-tuple-element.283, ...), channel_id=1, replica_groups=mesh['fsdp'=4,'ctx'=2,'tp'=4] {'fsdp','ctx'}, use_global_device_ids=true, to_apply=%region_13.14 | all-reduce | flops 9216 | bytes 73728 | tf_op jit(solution)/shard_map/psum | solution.py:280
  2643.9 9.4 fusion.25
  2653.3 8.7 fusion.29
  2662.0 25.7 all-reduce.97.cloned.1.call-done
  2687.7 307.0 %all-reduce.101.cloned.1.call-done = (f32[512,640]{1,0:T(8,128)}, f32[512,640]{1,0:T(8,128)}, f32[640,512]{1,0:T(8,128)}, f32[512,1536]{1,0:T(8,128)}, f32[512,1536]{1,0:T(8,128)}, /*index=5*/f32[1536,512]{1,0:T(8,128)}) async-done(((f32[512,640]{1,0:T(8,128)}, f32[512,640]{1,0:T(8,128)}, f32[640,512]{1,0:T(8,128)}, f32[512,1536]{1,0:T(8,128)}, f32[512,1536]{1,0:T(8,128)}, ...) | async-done | bytes 13369360 | tf_op jit(solution)/shard_map/psum | solution.py:276
  (704 shorter events, 616.1 us)
Async XLA Ops:
  7.2 78.9 %copy-start = (bf16[4,160,160]{2,1,0:T(8,128)(2,1)S(1)}, bf16[4,160,160]{2,1,0:T(8,128)(2,1)}, u32[]{:S(2)}) copy-start(bf16[4,160,160]{2,1,0:T(8,128)(2,1)} %param.30) | copy-start | bytes 614404
  7.2 59.9 %all-gather.7.cloned.1.call-start = ((), (), s32[]{:S(2)}) async-start(), calls=%async_computation.6 | async-start | bytes 3276800 | tf_op jit(solution)/shard_map/all_gather | solution.py:90
  7.9 368.9 %all-gather.9.cloned.1.call-start = ((), (), s32[]{:S(2)}) async-start(), calls=%async_computation.7 | async-start | bytes 3276800 | tf_op jit(solution)/shard_map/all_gather | solution.py:89
  8.7 58.4 %copy-start.85 = (f32[2048]{0:T(1024)S(1)}, f32[2048]{0:T(1024)}, u32[]{:S(2)}) copy-start(f32[2048]{0:T(1024)} %param.25) | copy-start | bytes 24580
  8.7 380.9 %all-gather.11.cloned.1.call-start = ((), (), s32[]{:S(2)}) async-start(), calls=%async_computation.8 | async-start | bytes 3276800 | tf_op jit(solution)/shard_map/all_gather | solution.py:93
  9.5 541.4 %all-reduce.93.cloned.1.call-start = ((), (), s32[]{:S(2)}) async-start(), calls=%async_computation.9 | async-start | bytes 16777216 | tf_op jit(solution)/shard_map/psum | solution.py:173
  12.7 65.6 %copy-start.76 = (f32[640]{0:T(1024)}, f32[640]{0:T(1024)S(1)}, u32[]{:S(2)}) copy-start(f32[640]{0:T(1024)S(1)} %get-tuple-element.290) | copy-start | bytes 7684
  12.7 65.6 %copy-start.78 = (f32[640]{0:T(1024)}, f32[640]{0:T(1024)S(1)}, u32[]{:S(2)}) copy-start(f32[640]{0:T(1024)S(1)} %get-tuple-element.291) | copy-start | bytes 7684
  12.7 65.6 %copy-start.80 = (f32[640]{0:T(1024)}, f32[640]{0:T(1024)S(1)}, u32[]{:S(2)}) copy-start(f32[640]{0:T(1024)S(1)} %get-tuple-element.292) | copy-start | bytes 7684
  12.7 65.6 %copy-start.82 = (f32[640]{0:T(1024)}, f32[640]{0:T(1024)S(1)}, u32[]{:S(2)}) copy-start(f32[640]{0:T(1024)S(1)} %get-tuple-element.293) | copy-start | bytes 7684
  12.7 80.9 %copy-start.60 = (f32[640]{0:T(1024)}, f32[640]{0:T(1024)S(1)}, u32[]{:S(2)}) copy-start(f32[640]{0:T(1024)S(1)} %fusion.106) | copy-start | bytes 7684
  13.5 64.8 %copy-start.129 = (pred[1024]{0:T(1024)(128)(4,1)}, pred[1024]{0:T(1024)(128)(4,1)S(1)}, u32[]{:S(2)}) copy-start(pred[1024]{0:T(1024)(128)(4,1)S(1)} %get-tuple-element.295) | copy-start | bytes 3076
  13.5 64.8 %copy-start.131 = (pred[1024]{0:T(1024)(128)(4,1)}, pred[1024]{0:T(1024)(128)(4,1)S(1)}, u32[]{:S(2)}) copy-start(pred[1024]{0:T(1024)(128)(4,1)S(1)} %get-tuple-element.296) | copy-start | bytes 3076
  13.5 64.8 %copy-start.134 = (f32[640]{0:T(1024)S(1)}, f32[640]{0:T(1024)}, u32[]{:S(2)}) copy-start(f32[640]{0:T(1024)} %param.29) | copy-start | bytes 7684
  73.6 4.7 collective-permute-start
  357.2 19.6 copy-start.86
  398.6 269.3 %all-gather.13.cloned.1.call-start = ((), (), s32[]{:S(2)}) async-start(), calls=%async_computation.10 | async-start | bytes 7864320 | tf_op jit(solution)/shard_map/all_gather | solution.py:91
  399.2 383.6 %all-gather.15.cloned.1.call-start = ((), (), s32[]{:S(2)}) async-start(), calls=%async_computation.11 | async-start | bytes 7864320 | tf_op jit(solution)/shard_map/all_gather | solution.py:92
  399.7 498.2 %all-gather.17.cloned.1.call-start = ((), (), s32[]{:S(2)}) async-start(), calls=%async_computation.12 | async-start | bytes 7864320 | tf_op jit(solution)/shard_map/all_gather | solution.py:94
  400.5 159.6 %copy-start.65 = (f32[2048]{0:T(1024)S(1)}, f32[2048]{0:T(1024)}, u32[]{:S(2)}) copy-start(f32[2048]{0:T(1024)} %param.36) | copy-start | bytes 24580
  400.5 687.6 %all-reduce.95.cloned.1.call-start = ((), (), s32[]{:S(2)}) async-start(), calls=%async_computation.13 | async-start | bytes 16777216 | tf_op jit(solution)/shard_map/psum | solution.py:192
  936.9 695.4 %reduce-scatter.11.cloned.1.call-start = ((), (), s32[]{:S(2)}) async-start(), calls=%async_computation.16 | async-start | bytes 6553600 | tf_op jit(solution)/shard_map/reduce_scatter | solution.py:272
  1110.1 522.2 %reduce-scatter.7.cloned.1.call-start = ((), (), s32[]{:S(2)}) async-start(), calls=%async_computation.14 | async-start | bytes 6553600 | tf_op jit(solution)/shard_map/reduce_scatter | solution.py:268
  1313.6 19.1 copy-start.95
  1313.6 19.1 copy-start.96
  1313.6 19.1 copy-start.97
  1313.6 19.1 copy-start.98
  1313.6 19.1 copy-start.70
  1313.6 19.1 copy-start.71
  1313.6 19.3 copy-start.72
  1313.6 19.3 copy-start.73
  1313.6 19.4 copy-start.119
  1313.6 19.4 copy-start.117
  1341.9 319.9 %reduce-scatter.9.cloned.1.call-start = ((), (), s32[]{:S(2)}) async-start(), calls=%async_computation.15 | async-start | bytes 6553600 | tf_op jit(solution)/shard_map/reduce_scatter | solution.py:269
  1498.9 21.0 copy-start.6
  1498.9 21.0 copy-start.59
  1498.9 21.0 copy-start.61
  1498.9 21.0 copy-start.67
  1498.9 21.0 copy-start.69
  1499.0 21.0 copy-start.90
  1544.8 18.1 copy-start.3
  1553.8 5.6 collective-permute-start.1
  1568.5 307.9 %reduce-scatter.13.cloned.1.call-start = ((), (), s32[]{:S(2)}) async-start(), calls=%async_computation.17 | async-start | bytes 15728640 | tf_op jit(solution)/shard_map/reduce_scatter | solution.py:270
  1581.2 510.5 %reduce-scatter.15.cloned.1.call-start = ((), (), s32[]{:S(2)}) async-start(), calls=%async_computation.18 | async-start | bytes 15728640 | tf_op jit(solution)/shard_map/reduce_scatter | solution.py:271
  1593.8 713.1 %reduce-scatter.17.cloned.1.call-start = ((), (), s32[]{:S(2)}) async-start(), calls=%async_computation.19 | async-start | bytes 15728640 | tf_op jit(solution)/shard_map/reduce_scatter | solution.py:273
  1606.1 992.6 %all-reduce.99.cloned.1.call-start = ((), (), s32[]{:S(2)}) async-start(), calls=%async_computation.21 | async-start | bytes 33554432 | tf_op jit(solution)/shard_map/psum | solution.py:182
  1627.6 1060.1 %all-reduce.97.cloned.1.call-start = ((), (), s32[]{:S(2)}) async-start(), calls=%async_computation.20 | async-start | bytes 2621440 | tf_op jit(solution)/shard_map/psum | solution.py:280
  1632.2 1362.5 %all-reduce.101.cloned.1.call-start = ((), (), s32[]{:S(2)}) async-start(), calls=%async_computation.22 | async-start | bytes 26738688 | tf_op jit(solution)/shard_map/psum | solution.py:276
  (114 other events, 819.6 us)
Sparse Core Ops, SparseCore 0:
  9.6 57.4 all-gather.6
  68.6 53.5 all-gather.8
  123.8 53.4 all-gather.10
  398.7 152.1 all-reduce.92
  552.3 115.4 all-gather.12
  669.3 113.5 all-gather.14
  784.4 113.4 all-gather.16
  937.0 151.0 all-reduce.94
  1110.2 93.9 reduce-scatter.10
  1342.0 93.8 reduce-scatter.6
  1568.6 93.1 reduce-scatter.8
  1664.0 212.3 reduce-scatter.12
  1878.8 212.8 reduce-scatter.14
  2093.9 212.8 reduce-scatter.16
  2309.4 289.3 all-reduce.98
  2603.3 84.3 all-reduce.96
  2690.5 304.0 all-reduce.100
where the time goes:
time: 3040 us; the launch traced here: 3020 us
  waiting for transfers between devices  1970 us (65%)
  local copies, waits for them, and re-layouts  565 us (19%)
  other arithmetic  203 us (7%)
  matrix products  194 us (6%)
  blocking collectives  56.9 us (2%)
    psum x1, waiting for transfers between devices, shards(): lax.psum((owned_branch, owned_input, owned_gate, owned_up, owned_out, own...  307 us
    psum x1, waiting for transfers between devices, shards(): output = (resid_rows + lax.psum(down_term, 'tp')).astype(jnp.bfloat16)  291 us
    reduce_scatter x1, waiting for transfers between devices, shards(): lax.psum_scatter(grad_w_up, 'fsdp', scatter_dimension=0, tiled=True)  215 us
    reduce_scatter x1, waiting for transfers between devices, shards(): lax.psum_scatter(grad_w_down, 'fsdp', scatter_dimension=1, tiled=True)  215 us
    reduce_scatter x1, waiting for transfers between devices, shards(): lax.psum_scatter(grad_w_gate, 'fsdp', scatter_dimension=0, tiled=True)  215 us
    slice x70, local copies, waits for them, and re-layouts, shards(): lax.associative_scan(linear_combine, (jnp.flip(next_factor, 1), jnp.flip(...  170 us
    psum x1, waiting for transfers between devices, shards(): grad_norm_mlp = lax.psum(mlp_back_term, 'tp')  151 us
    psum x1, waiting for transfers between devices, shards(): resid_rows = inputs + lax.psum(mixer_term, 'tp')  150 us
  transfers between devices with their start and end apart: 19, of which 15 were waited for; matrix products, arithmetic and copies ran while one was open for 29% of the time, Pallas kernels for 0%

commit v1 on v0

v1 whole, which is shorter than its diff:
```python
import functools

import jax
import jax.numpy as jnp
import numpy as np
from jax import lax
from jax.experimental import pallas as pl
from jax.experimental.pallas import tpu as pltpu
from jax.sharding import PartitionSpec as P

EPSILON = 1e-06
RATE_SCALE = 8.0
GELU_C = 0.7978845608028654
GELU_K = 0.044715
GROUP = ("ctx", "tp")
F32, BF16 = jnp.float32, jnp.bfloat16


def matmul(left, right):
    return jnp.dot(left, right, preferred_element_type=F32)


def left_inner(left, right):
    return lax.dot_general(left, right, (((0,), (0,)), ((), ())), preferred_element_type=F32)


def right_inner(left, right):
    return lax.dot_general(left, right, (((1,), (1,)), ((), ())), preferred_element_type=F32)


def gelu_parts(v):
    t = jnp.tanh(GELU_C * (v + GELU_K * (v * v * v)))
    half = 0.5 * (1.0 + t)
    slope = half + 0.5 * v * (1.0 - t * t) * (GELU_C * (1.0 + 3.0 * GELU_K * v * v))
    return v * half, slope


def gelu(v):
    return 0.5 * v * (1.0 + jnp.tanh(GELU_C * (v + GELU_K * (v * v * v))))


def one_minus_exp(u):
    series = 1.0 - u * (1.0 / 8.0)
    for n in (7.0, 6.0, 5.0, 4.0, 3.0, 2.0):
        series = 1.0 - u * (1.0 / n) * series
    return jnp.where(u < 0.5, u * series, 1.0 - jnp.exp(-u))


def rms_rows(values):
    return lax.rsqrt(jnp.mean(values * values, axis=-1, keepdims=True) + EPSILON)


def norm_back(grad_norm, scaled, scale_row, gain):
    grad_scaled = grad_norm * gain
    return scale_row * (
        grad_scaled - scaled * jnp.mean(grad_scaled * scaled, axis=-1, keepdims=True)
    )


def step_mask(kind, g):
    core = g % 2
    if kind == "core":
        return 1
    return 2 if (kind == "near") == (core == 0) else 4


def exchange(block, kind):
    pairs = [(g, g ^ step_mask(kind, g)) for g in range(8)]
    return lax.ppermute(block, GROUP, pairs)


def flip(block, mask):
    return lax.ppermute(block, GROUP, [(g, g ^ mask) for g in range(8)])


def place_table():
    table = np.zeros((8, 8), np.int32)
    for g in range(8):
        for spot in range(8):
            at = g ^ (spot >> 2)
            block = at
            if spot & 1:
                block ^= step_mask("near", at)
            if spot & 2:
                block ^= step_mask("far", at)
            table[g, block] = spot
    return table


def gather_rows(rows):
    for kind in ("near", "far", "core"):
        rows = jnp.concatenate([rows, exchange(rows, kind)], axis=0)
    return rows


def reduce_rows(left, right, product):
    half = left.shape[0] // 2
    sent = product(left[half:], right).astype(BF16)
    kept = product(left[:half], right)
    got = exchange(sent, "core")
    kept, got = lax.optimization_barrier((kept, got))
    total = kept + got.astype(F32)
    for kind in ("far", "near"):
        half = half // 2
        got = exchange(total[half:].astype(BF16), kind)
        total = total[:half] + got.astype(F32)
    return total


def whole_rows(rows):
    count = rows.shape[0]
    rows = jnp.concatenate([rows, flip(rows, 2)], axis=0)
    rows = jnp.concatenate([rows, flip(rows, 1)], axis=0)
    place = lax.axis_index("tp")
    blocks = []
    for b in range(4):
        away = jnp.bitwise_xor(place, b)
        spot = (away % 2) * 2 + away // 2
        blocks.append(lax.dynamic_slice_in_dim(rows, spot * count, count, 0))
    return jnp.concatenate(blocks, axis=0)


def sum_fsdp(x):
    size = lax.axis_size("fsdp")
    bit = 1
    while bit < size:
        x = x + lax.ppermute(x, "fsdp", [(i, i ^ bit) for i in range(size)])
        bit *= 2
    return x


def scan_rows(a_ref, b_ref, carry, reverse):
    rows, width = b_ref.shape
    groups = rows // 8
    a = a_ref[...].reshape(groups, 8, width)
    b = b_ref[...].reshape(groups, 8, width)
    at = lax.broadcasted_iota(jnp.int32, (groups, 8, width), 1)
    for shift in (1, 2, 4):
        ok = (at < 8 - shift) if reverse else (at >= shift)
        turn = 8 - shift if reverse else shift
        b_before = jnp.where(ok, pltpu.roll(b, turn, 1), 0.0)
        a_before = jnp.where(ok, pltpu.roll(a, turn, 1), 1.0)
        b = a * b_before + b
        a = a * a_before
    a_ref[...] = a.reshape(rows, width)
    b_ref[...] = b.reshape(rows, width)
    for k in range(groups):
        k = groups - 1 - k if reverse else k
        part = pl.ds(8 * k, 8)
        now = b_ref[part, :] + a_ref[part, :] * carry
        b_ref[part, :] = now
        carry = now[0:1, :] if reverse else now[7:8, :]
    return carry


def mixer_kernel(
    place, pre, masks, params, gate_a, gate_x, mixed, states, recur_out, input_out, conv_out, ext, a_buf, b_buf, carry
):
    rows, width = states.shape

    @pl.when(pl.program_id(0) == 0)
    def _():
        ext[...] = jnp.zeros_like(ext)
        carry[...] = jnp.zeros_like(carry)

    ext[0:8, :] = ext[rows : rows + 8, :]
    ext[8:, :] = pre[:, width:].astype(BF16).astype(F32)
    conv = params[4:5, :] + params[0:1, :] * ext[8:, :]
    for k in range(1, 4):
        conv = conv + params[k : k + 1, :] * (masks[:, k - 1 : k] * ext[pl.ds(8 - k, rows), :])
    conv_low = conv.astype(BF16)
    conv_out[...] = conv_low
    conv = conv_low.astype(F32)
    recur = jax.nn.sigmoid(matmul(conv_low, gate_a[...]) + params[5:6, :])
    opened = jax.nn.sigmoid(matmul(conv_low, gate_x[...]) + params[6:7, :])
    recur_out[...] = recur
    input_out[...] = opened
    log_decay = params[7:8, :] * recur
    same = masks[:, 0:1]
    root = jnp.sqrt(one_minus_exp(-2.0 * log_decay))
    a_buf[...] = same * jnp.exp(log_decay)
    b_buf[...] = opened * conv * jnp.where(same > 0.5, root, 1.0)
    carry[0:1, :] = scan_rows(a_buf, b_buf, carry[0:1, :], False)
    state = b_buf[...]
    states[...] = state
    mixed[...] = (state * gelu(pre[:, :width])).astype(BF16)


def mixer_back_kernel(
    place, grad_mixed, pre, pre_tail, states, states_tail, recur_in, input_in, conv_in, masks, params, gate_a, gate_x,
    grads, sums, sum_a, sum_x, ext, grad_ext, a_buf, b_buf, carry,
):
    rows, width = states.shape
    step = pl.program_id(0)
    first = step == pl.num_programs(0) - 1

    @pl.when(step == 0)
    def _():
        grad_ext[...] = jnp.zeros_like(grad_ext)
        carry[...] = jnp.zeros_like(carry)
        sums[...] = jnp.zeros_like(sums)
        sum_a[...] = jnp.zeros_like(sum_a)
        sum_x[...] = jnp.zeros_like(sum_x)

    inside = jnp.where(first, 0.0, 1.0)
    branch, slope = gelu_parts(pre[:, :width])
    above = grad_mixed[...]
    state = states[...]
    grads[:, :width] = (above * state * slope).astype(BF16)
    recur, opened = recur_in[...], input_in[...]
    conv_low = conv_in[...]
    conv = conv_low.astype(F32)
    same = masks[:, 0:1]
    rate = params[7:8, :]
    log_decay = rate * recur
    decay = jnp.exp(log_decay)
    root = jnp.sqrt(one_minus_exp(-2.0 * log_decay))
    mult = jnp.where(same > 0.5, root, 1.0)
    a_buf[0:rows, :] = same * decay
    head = a_buf[0:1, :]
    a_buf[rows : rows + 8, :] = jnp.broadcast_to(carry[1:2, :], (8, width))
    factor = a_buf[pl.ds(1, rows), :]
    a_buf[0:rows, :] = factor
    b_buf[...] = above * branch
    new_carry = scan_rows(a_buf.at[pl.ds(0, rows), :], b_buf, carry[0:1, :], True)
    carry[0:1, :] = new_carry
    carry[1:2, :] = head
    total = b_buf[...]
    ext[0:8, :] = inside * states_tail[...]
    ext[8:, :] = state
    before = ext[pl.ds(7, rows), :]
    grad_open = total * opened
    grad_log = jnp.where(
        same > 0.5, total * before * decay - grad_open * conv * decay * decay / root, 0.0
    )

    def fold(x):
        return jnp.sum(x.reshape(rows // 8, 8, width), axis=0)

    sums[0:8, :] += fold(grad_log * recur)
    low_a = (grad_log * rate * recur * (1.0 - recur)).astype(BF16)
    low_x = (total * conv * mult * opened * (1.0 - opened)).astype(BF16)
    sums[8:16, :] += fold(low_a.astype(F32))
    sums[16:24, :] += fold(low_x.astype(F32))
    sum_a[...] += left_inner(conv_low, low_a)
    sum_x[...] += left_inner(conv_low, low_x)
    grad_conv = grad_open * mult + (
        right_inner(low_a, gate_a[...]) + right_inner(low_x, gate_x[...])
    )
    sums[24:32, :] += fold(grad_conv)
    ext[0:8, :] = inside * pre_tail[:, width:].astype(BF16).astype(F32)
    ext[8:, :] = pre[:, width:].astype(BF16).astype(F32)
    grad_ext[rows : rows + 8, :] = grad_ext[0:8, :]
    grad_ext[0:rows, :] = grad_conv
    grad_in = params[0:1, :] * grad_conv
    sums[32:40, :] += fold(grad_conv * ext[8:, :])
    for k in range(1, 4):
        earlier = masks[:, k - 1 : k] * ext[pl.ds(8 - k, rows), :]
        sums[32 + 8 * k : 40 + 8 * k, :] += fold(grad_conv * earlier)
        grad_in = grad_in + params[k : k + 1, :] * (
            masks[:, k + 2 : k + 3] * grad_ext[pl.ds(k, rows), :]
        )
    grads[:, width:] = grad_in.astype(BF16)


def mixer(pre, masks, params, gate_a, gate_x, place, rows):
    count, width = pre.shape[0], pre.shape[1] // 2
    steps = count // rows
    spot = lambda i, place: (place[i], 0)
    inorder = lambda i, place: (i, 0)
    fixed = lambda i, place: (0, 0)
    wide = pl.BlockSpec((rows, 2 * width), spot)
    one = pl.BlockSpec((rows, width), spot)
    gate = pl.BlockSpec((width, width), fixed)
    return pl.pallas_call(
        mixer_kernel,
        grid_spec=pltpu.PrefetchScalarGridSpec(
            num_scalar_prefetch=1,
            grid=(steps,),
            in_specs=[wide, pl.BlockSpec((rows, 8), inorder), pl.BlockSpec((8, width), fixed), gate, gate],
            out_specs=[one] * 5,
            scratch_shapes=[
                pltpu.VMEM((rows + 8, width), F32),
                pltpu.VMEM((rows, width), F32),
                pltpu.VMEM((rows, width), F32),
                pltpu.VMEM((8, width), F32),
            ],
        ),
        out_shape=[
            jax.ShapeDtypeStruct((count, width), kind) for kind in (BF16, F32, F32, F32, BF16)
        ],
        cost_estimate=pl.CostEstimate(
            flops=count * width * (4 * width + 120), bytes_accessed=count * width * 24, transcendentals=count * width * 6
        ),
        name="mixer",
    )(place, pre, masks, params, gate_a, gate_x)


def mixer_back(grad_mixed, pre, states, recur, opened, conv, masks, params, gate_a, gate_x, place, rows):
    count, width = states.shape
    steps = count // rows
    last = steps - 1
    spot = lambda i, place: (place[last - i], 0)
    inorder = lambda i, place: (last - i, 0)
    fixed = lambda i, place: (0, 0)

    def tail(i, place):
        return (place[jnp.maximum(last - i - 1, 0)] * (rows // 8) + rows // 8 - 1, 0)

    wide = pl.BlockSpec((rows, 2 * width), spot)
    one = pl.BlockSpec((rows, width), spot)
    gate = pl.BlockSpec((width, width), fixed)
    return pl.pallas_call(
        mixer_back_kernel,
        grid_spec=pltpu.PrefetchScalarGridSpec(
            num_scalar_prefetch=1,
            grid=(steps,),
            in_specs=[
                one, wide, pl.BlockSpec((8, 2 * width), tail), one, pl.BlockSpec((8, width), tail), one, one, one,
                pl.BlockSpec((rows, 8), inorder), pl.BlockSpec((8, width), fixed), gate, gate,
            ],
            out_specs=[wide, pl.BlockSpec((64, width), fixed), gate, gate],
            scratch_shapes=[
                pltpu.VMEM((rows + 8, width), F32),
                pltpu.VMEM((rows + 8, width), F32),
                pltpu.VMEM((rows + 8, width), F32),
                pltpu.VMEM((rows, width), F32),
                pltpu.VMEM((8, width), F32),
            ],
        ),
        out_shape=[
            jax.ShapeDtypeStruct((count, 2 * width), BF16),
            jax.ShapeDtypeStruct((64, width), F32),
            jax.ShapeDtypeStruct((width, width), F32),
            jax.ShapeDtypeStruct((width, width), F32),
        ],
        cost_estimate=pl.CostEstimate(
            flops=count * width * (8 * width + 200), bytes_accessed=count * width * 34, transcendentals=count * width * 4
        ),
        name="mixer_back",
    )(place, grad_mixed, pre, pre, states, states, recur, opened, conv, masks, params, gate_a, gate_x)


def on_diagonal(blocks):
    heads, size = blocks.shape[0], blocks.shape[1]
    out = jnp.zeros((heads * size, heads * size), blocks.dtype)
    for h in range(heads):
        out = lax.dynamic_update_slice(out, blocks[h], (h * size, h * size))
    return out


def shards(
    tokens, segments, cotangent, gain_mix, w_branch, w_input, conv_weight, conv_bias, gate_a, bias_a, gate_x, bias_x,
    decay_param, w_out, gain_mlp, w_gate, w_up, w_down,
):
    half_at = lax.axis_index("ctx")
    place_tp = lax.axis_index("tp")

    def mine(x, axis):
        size = x.shape[axis] // 2
        return lax.dynamic_slice_in_dim(x, half_at * size, size, axis)

    _, tok_count, model_width = tokens.shape
    rows = tok_count // 4
    length = 2 * tok_count
    own_in = jnp.concatenate([mine(w_branch, 1), mine(w_input, 1)], axis=1)
    full_in = lax.all_gather(own_in, "fsdp", axis=0, tiled=True)
    full_out = lax.all_gather(mine(w_out, 0), "fsdp", axis=1, tiled=True)
    own_gu = jnp.concatenate([mine(w_gate, 1), mine(w_up, 1)], axis=1)
    full_gu = lax.all_gather(own_gu, "fsdp", axis=0, tiled=True)
    full_down = lax.all_gather(mine(w_down, 0), "fsdp", axis=1, tiled=True)

    width = own_in.shape[1] // 2
    units = own_gu.shape[1] // 2
    place = jnp.asarray(place_table())[half_at * 4 + place_tp]

    rate = -RATE_SCALE * jax.nn.softplus(-decay_param)
    params = jnp.concatenate(
        [
            mine(conv_weight, 1),
            jnp.stack([mine(v, 0) for v in (conv_bias, bias_a, bias_x, rate)]),
        ],
        axis=0,
    )
    heads_a, heads_x = mine(gate_a, 0), mine(gate_x, 0)
    head_count, head_width = heads_a.shape[0], heads_a.shape[1]
    diag_a, diag_x = on_diagonal(heads_a), on_diagonal(heads_x)
    seg = segments[0]
    around = jnp.pad(seg, (3, 3), constant_values=-1)
    marks = [around[3 - k : 3 - k + length] == seg for k in (1, 2, 3)]
    marks += [around[3 + k : 3 + k + length] == seg for k in (1, 2, 3)]
    marks += [jnp.zeros_like(marks[0])] * 2
    masks = jnp.stack(marks, axis=1).astype(F32)

    own = lax.dynamic_slice_in_dim(tokens[0], place_tp * rows, rows, 0)
    inputs = own.astype(F32)
    scale_mix = rms_rows(inputs)
    scaled_mix = inputs * scale_mix
    normed = gather_rows((scaled_mix * gain_mix).astype(BF16))
    own_cot = lax.dynamic_slice_in_dim(cotangent[0], place_tp * rows, rows, 0)
    cot = gather_rows(own_cot)

    pre = matmul(normed, full_in)
    mixed, states, recur, opened, conv = mixer(pre, masks, params, diag_a, diag_x, place, rows)
    resid = inputs + reduce_rows(mixed, full_out, matmul)
    scale_mlp = rms_rows(resid)
    scaled_mlp = resid * scale_mlp
    normed_mlp = gather_rows((scaled_mlp * gain_mlp).astype(BF16))

    both = matmul(normed_mlp, full_gu)
    gate_pre, up_pre = both[:, :units], both[:, units:]
    gate_act, gate_slope = gelu_parts(gate_pre)
    hidden = (gate_act * up_pre).astype(BF16)
    grad_w_down = left_inner(hidden, cot).astype(BF16)
    output = (resid + reduce_rows(hidden, full_down, matmul)).astype(BF16)

    grad_hidden = right_inner(cot, full_down)
    grad_both = jnp.concatenate(
        [
            (grad_hidden * up_pre * gate_slope).astype(BF16),
            (grad_hidden * gate_act).astype(BF16),
        ],
        axis=1,
    )
    grad_norm_mlp = reduce_rows(grad_both, full_gu, right_inner)
    grad_w_gu = left_inner(normed_mlp, grad_both).astype(BF16)
    grad_resid = own_cot.astype(F32) + norm_back(grad_norm_mlp, scaled_mlp, scale_mlp, gain_mlp)
    gain_mlp_part = jnp.sum(grad_norm_mlp * scaled_mlp, axis=0)
    grad_proj = gather_rows(grad_resid.astype(BF16))

    grad_w_out = left_inner(mixed, grad_proj).astype(BF16)
    grad_mixed = right_inner(grad_proj, full_out)
    grads_in, sums, sum_a, sum_x = mixer_back(
        grad_mixed, pre, states, recur, opened, conv, masks, params, diag_a, diag_x, place, rows
    )
    grad_w_in = left_inner(normed, grads_in).astype(BF16)
    grad_norm_mix = reduce_rows(grads_in, full_in, right_inner)
    gain_mix_part = jnp.sum(grad_norm_mix * scaled_mix, axis=0)
    grad_tokens = (grad_resid + norm_back(grad_norm_mix, scaled_mix, scale_mix, gain_mix)).astype(BF16)

    def owned(x, axis):
        return lax.psum_scatter(x, "fsdp", scatter_dimension=axis, tiled=True)

    def both_halves(x, axis):
        other = flip(x, 4)
        low = jnp.where(half_at == 0, x, other)
        high = jnp.where(half_at == 0, other, x)
        return jnp.concatenate([low, high], axis=axis).astype(F32)

    own_down = both_halves(owned(grad_w_down, 1), 0)
    sum_gu = owned(grad_w_gu, 0)
    own_gate = both_halves(sum_gu[:, :units], 1)
    own_up = both_halves(sum_gu[:, units:], 1)
    own_out = both_halves(owned(grad_w_out, 1), 0)
    sum_in = owned(grad_w_in, 0)
    own_branch = both_halves(sum_in[:, :width], 1)
    own_input = both_halves(sum_in[:, width:], 1)

    lines = jnp.sum(sums.reshape(8, 8, width), axis=1)
    squares = [
        part[h * head_width : (h + 1) * head_width, h * head_width : (h + 1) * head_width]
        for part in (sum_a, sum_x)
        for h in range(head_count)
    ]
    lines = both_halves(sum_fsdp(lines), 1)
    squares = sum_fsdp(jnp.stack(squares).reshape(2, head_count, head_width, head_width))
    squares = both_halves(squares, 1)
    gains = jnp.stack([gain_mix_part, gain_mlp_part])
    for mask in (1, 2, 4):
        gains = gains + flip(gains, mask)
    gains = sum_fsdp(gains)
    return (
        whole_rows(output)[None],
        whole_rows(grad_tokens)[None],
        gains[0],
        own_branch,
        own_input,
        lines[4:8],
        lines[3],
        squares[0],
        lines[1],
        squares[1],
        lines[2],
        RATE_SCALE * jax.nn.sigmoid(-decay_param) * lines[0],
        own_out,
        gains[1],
        own_gate,
        own_up,
        own_down,
    )


def solution(mesh):
    in_specs = (
        P("fsdp", "ctx", None),
        P("fsdp", None),
        P("fsdp", "ctx", None),
        P(),
        P("fsdp", "tp"),
        P("fsdp", "tp"),
        P(None, "tp"),
        P("tp"),
        P("tp", None, None),
        P("tp"),
        P("tp", None, None),
        P("tp"),
        P("tp"),
        P("tp", "fsdp"),
        P(),
        P("fsdp", "tp"),
        P("fsdp", "tp"),
        P("tp", "fsdp"),
    )
    out_specs = (
        P("fsdp", "ctx", None),
        P("fsdp", "ctx", None),
        P(),
        P("fsdp", "tp"),
        P("fsdp", "tp"),
        P(None, "tp"),
        P("tp"),
        P("tp", None, None),
        P("tp"),
        P("tp", None, None),
        P("tp"),
        P("tp"),
        P("tp", "fsdp"),
        P(),
        P("fsdp", "tp"),
        P("fsdp", "tp"),
        P("tp", "fsdp"),
    )
    return jax.shard_map(shards, mesh=mesh, in_specs=in_specs, out_specs=out_specs, check_vma=False)
```

time: 3040 us -> 825 us (0.27)
  waiting for transfers between devices: 1970 us -> 386 us
  local copies, waits for them, and re-layouts: 565 us -> 46.5 us
  other arithmetic: 203 us -> 106 us
  blocking collectives: 56.9 us -> 0 us
  Pallas kernels: 0 us -> 46.6 us
  starting transfers between devices: 5.36 us -> 46.6 us
    psum x5 -> x0, waiting for transfers between devices: 925 us -> none  [the longest x1 307 us: shards(): lax.psum((owned_branch, owned_input, owned_gate, owned_up, owned_out, own...]
    reduce_scatter x6 -> x4, waiting for transfers between devices: 675 us -> 0.01 us  [owned(): return lax.psum_scatter(x, 'fsdp', scatter_dimension=axis, tiled=True)]
    ppermute x2 -> x45, waiting for transfers between devices: 5.52 us -> 343 us  [the longest x24 236 us: exchange(): return lax.ppermute(block, GROUP, pairs)]
    all_gather x6 -> x4, waiting for transfers between devices: 365 us -> 42.7 us  [the longest x1 24.7 us: shards(): full_down = lax.all_gather(mine(w_down, 0), 'fsdp', axis=1, tiled=True)]
    slice x142 -> x11, local copies, waits for them, and re-layouts: 301 us -> 17.8 us  [the longest x8 13.9 us: reduce_rows(): got = exchange(total[half:].astype(BF16), kind)]
    pad x72 -> x0, local copies, waits for them, and re-layouts: 156 us -> none  [the longest x36 78.8 us: shards(): lax.associative_scan(linear_combine, (jnp.flip(next_factor, 1), jnp.flip(...]
    pallas_call x0 -> x2, Pallas kernels: none -> 46.6 us  [the longest x1 27.4 us: mixer_back(): pl.pallas_call(mixer_back_kernel, grid_spec=pltpu.PrefetchScalarGridSpec(...]
    rev x2 -> x0, local copies, waits for them, and re-layouts: 41.7 us -> none  [the longest x1 20.9 us: shards(): local_back = jnp.flip(local_back, 1)]
  transfers between devices with their start and end apart: 19 -> 53, of which waited for: 15 -> 28; matrix products, arithmetic and copies ran while one was open for 29% -> 32% of each run, Pallas kernels for 0% -> 6%
where the time goes in v1:
time: 825 us; the launch traced here: 815 us
  waiting for transfers between devices  386 us (47%)
  matrix products  168 us (20%)
  other arithmetic  106 us (13%)
  starting transfers between devices  46.6 us (6%)
  Pallas kernels  46.6 us (6%)
  local copies, waits for them, and re-layouts  46.5 us (6%)
  between operations  15.5 us (2%)
    ppermute x24, waiting for transfers between devices, exchange(): return lax.ppermute(block, GROUP, pairs)  236 us
    dot_general x6, matrix products, right_inner(): lax.dot_general(left, right, (((1,), (1,)), ((), ())), preferred_element_...  64.3 us
    dot_general x6, matrix products, matmul(): return jnp.dot(left, right, preferred_element_type=F32)  57.3 us
    ppermute x15, waiting for transfers between devices, flip(): return lax.ppermute(block, GROUP, [(g, g ^ mask) for g in range(8)])  57.2 us
    ppermute x6, waiting for transfers between devices, sum_fsdp(): x = x + lax.ppermute(x, 'fsdp', [(i, i ^ bit) for i in range(size)])  49.5 us
    dot_general x4, matrix products, left_inner(): lax.dot_general(left, right, (((0,), (0,)), ((), ())), preferred_element_...  46.5 us
    add x4, other arithmetic, reduce_rows(): total = kept + got.astype(F32)  28.7 us
    pallas_call x1, Pallas kernels, mixer_back(): pl.pallas_call(mixer_back_kernel, grid_spec=pltpu.PrefetchScalarGridSpec(...  27.4 us
  transfers between devices with their start and end apart: 53, of which 28 were waited for; matrix products, arithmetic and copies ran while one was open for 32% of the time, Pallas kernels for 6%

profile of v1, /device:TPU:0, one launch (start us, length us, event | category | flops | bytes accessed | tf_op | source)
XLA Modules:
  0.0 815.3 jit_solution(9742174008801710376)
XLA Ops:
  13.6 12.8 %collective-permute-done = bf16[256,2048]{1,0:T(8,128)(2,1)S(1)} collective-permute-done((bf16[256,2048]{1,0:T(8,128)(2,1)S(1)}, bf16[256,2048]{1,0:T(8,128)(2,1)S(1)}, u32[]{:S(2)}, u32[]{:S(2)}) %collective-permute-start) | collective-permute-done | bytes 1048608 | tf_op jit(solution)/shard_map/ppermute | solution.py:69
  33.4 21.8 %collective-permute-done.1 = bf16[512,2048]{1,0:T(8,128)(2,1)} collective-permute-done((bf16[512,2048]{1,0:T(8,128)(2,1)}, bf16[512,2048]{1,0:T(8,128)(2,1)}, u32[]{:S(2)}, u32[]{:S(2)}) %collective-permute-start.1) | collective-permute-done | bytes 2097184 | tf_op jit(solution)/shard_map/ppermute | solution.py:69
  55.2 3.6 pad_maximum_fusion.6
  71.8 16.8 %all-gather.5.cloned.1.call-done = bf16[2048,640]{1,0:T(8,128)(2,1)} async-done(((bf16[512,640]{1,0:T(8,128)(2,1)}), bf16[2048,640]{1,0:T(8,128)(2,1)}) %all-gather.5.cloned.1.call-update) | async-done | bytes 2621456 | tf_op jit(solution)/shard_map/all_gather | solution.py:367
  88.5 13.0 %fusion.35.pre.pre_tail = f32[2048,640]{1,0:T(8,128)} fusion(bf16[2048,640]{1,0:T(8,128)(2,1)} %all-gather.5.cloned.1.call-done, bf16[1024,2048]{1,0:T(8,128)(2,1)} %collective-permute-done.2, bf16[512,2048]{1,0:T(8,128)(2,1)} %collective-permute-done.1, bf16[256,2048]{1,0:T(8,128)(2,1)} %copy-done.17, bf16[256,2048]{1,0:T(8,128)(2,1)S(1)} %fusion.20), kind=kOutput, calls=%fused_computation.101 | convolution fusion | flops 5402263552 | bytes 16252928 | tf_op jit(solution)/shard_map/dot_general | solution.py:20
  101.6 19.2 %mixer.1 = (bf16[2048,320]{1,0:T(8,128)(2,1)}, f32[2048,320]{1,0:T(8,128)}, f32[2048,320]{1,0:T(8,128)}, f32[2048,320]{1,0:T(8,128)}, bf16[2048,320]{1,0:T(8,128)(2,1)}) custom-call(s32[8]{0:T(128)} %fusion.61.place, f32[2048,640]{1,0:T(8,128)} %fusion.35.pre.pre_tail, f32[2048,8]{1,0:T(8,128)} %convert_element_type.125.masks, ...), custom_call_target="tpu_custom_call" | custom-call | flops 917504000 | bytes 15728640 | tf_op jit(solution)/shard_map/mixer/pallas_call | solution.py:275
  122.0 4.0 convolution_convert_fusion.3
  128.5 4.9 collective-permute-done.3
  133.4 6.8 convert_add_fusion.3
  140.2 3.9 slice.412
  148.3 22.2 %collective-permute-done.4 = bf16[512,2048]{1,0:T(8,128)(2,1)} collective-permute-done((bf16[512,2048]{1,0:T(8,128)(2,1)}, bf16[512,2048]{1,0:T(8,128)(2,1)}, u32[]{:S(2)}, u32[]{:S(2)}) %collective-permute-start.4) | collective-permute-done | bytes 2097184 | tf_op jit(solution)/shard_map/ppermute | solution.py:69
  175.7 13.3 %collective-permute-done.5 = bf16[256,2048]{1,0:T(8,128)(2,1)S(1)} collective-permute-done((bf16[256,2048]{1,0:T(8,128)(2,1)S(1)}, bf16[256,2048]{1,0:T(8,128)(2,1)S(1)}, u32[]{:S(2)}, u32[]{:S(2)}) %collective-permute-start.5) | collective-permute-done | bytes 1048608 | tf_op jit(solution)/shard_map/ppermute | solution.py:69
  194.0 13.3 %collective-permute-done.6 = bf16[256,2048]{1,0:T(8,128)(2,1)S(1)} collective-permute-done((bf16[256,2048]{1,0:T(8,128)(2,1)S(1)}, bf16[256,2048]{1,0:T(8,128)(2,1)S(1)}, u32[]{:S(2)}, u32[]{:S(2)}) %collective-permute-start.6) | collective-permute-done | bytes 1048608 | tf_op jit(solution)/shard_map/ppermute | solution.py:69
  211.9 32.4 %collective-permute-done.7 = bf16[512,2048]{1,0:T(8,128)(2,1)S(1)} collective-permute-done((bf16[512,2048]{1,0:T(8,128)(2,1)S(1)}, bf16[512,2048]{1,0:T(8,128)(2,1)S(1)}, u32[]{:S(2)}, u32[]{:S(2)}) %collective-permute-start.7) | collective-permute-done | bytes 2097184 | tf_op jit(solution)/shard_map/ppermute | solution.py:69
  251.9 23.8 %collective-permute-done.15 = bf16[512,2048]{1,0:T(8,128)(2,1)} collective-permute-done((bf16[512,2048]{1,0:T(8,128)(2,1)}, bf16[512,2048]{1,0:T(8,128)(2,1)}, u32[]{:S(2)}, u32[]{:S(2)}) %collective-permute-start.15) | collective-permute-done | bytes 2097184 | tf_op jit(solution)/shard_map/ppermute | solution.py:69
  275.8 4.0 pad_maximum_fusion.9
  279.8 20.6 %fusion.33 = f32[2048,1536]{0,1:T(8,128)} fusion(bf16[2048,1536]{1,0:T(8,128)(2,1)} %all-gather.9.cloned.1.call-done, bf16[1024,2048]{1,0:T(8,128)(2,1)} %collective-permute-done.8, bf16[512,2048]{1,0:T(8,128)(2,1)} %copy-done.26, bf16[256,2048]{1,0:T(8,128)(2,1)} %copy-done.19, bf16[256,2048]{1,0:T(8,128)(2,1)S(1)} %copy-done.13), kind=kOutput, calls=%fused_computation.99 | convolution fusion | flops 12918456320 | bytes 27262976 | tf_op jit(solution)/shard_map/dot_general | solution.py:20
  300.3 24.7 %all-gather.11.cloned.1.call-done = bf16[768,2048]{1,0:T(8,128)(2,1)} async-done(((bf16[768,512]{1,0:T(8,128)(2,1)}), bf16[768,2048]{1,0:T(8,128)(2,1)}) %all-gather.11.cloned.1.call-update) | async-done | bytes 3145744 | tf_op jit(solution)/shard_map/all_gather | solution.py:371
  325.0 19.1 %multiply_convert_fusion = (bf16[2048,768]{0,1:T(8,128)(2,1)}, bf16[2048,768]{0,1:T(8,128)(2,1)}, bf16[2048,768]{0,1:T(8,128)(2,1)}) fusion(f32[2048,1536]{0,1:T(8,128)} %fusion.33, bf16[768,2048]{1,0:T(8,128)(2,1)} %all-gather.11.cloned.1.call-done, bf16[1024,2048]{1,0:T(8,128)(2,1)} %collective-permute-done.16, ...), kind=kOutput, calls=%fused_computation.26 | convolution fusion | flops 6515326976 | bytes 33554432 | tf_op jit(solution)/shard_map/dot_general | solution.py:28
  344.2 8.0 convolution_convert_fusion.4
  352.2 8.5 %convolution_convert_fusion.1 = bf16[1024,2048]{1,0:T(8,128)(2,1)} fusion(bf16[2048,1536]{1,0:T(8,128)(2,1)S(1)} %copy-done.52, bf16[2048,768]{0,1:T(8,128)(2,1)S(1)} %copy-done.56, bf16[2048,768]{0,1:T(8,128)(2,1)S(1)} %copy-done.54), kind=kOutput, calls=%fused_computation.46 | convolution fusion | flops 6450839552 | bytes 16777216 | tf_op jit(solution)/shard_map/dot_general | solution.py:28
  361.2 9.9 %convolution_convert_fusion.5 = bf16[768,2048]{1,0:T(8,128)(2,1)} fusion(bf16[2048,768]{0,1:T(8,128)(2,1)S(1)} %copy-done.53, bf16[1024,2048]{1,0:T(8,128)(2,1)} %collective-permute-done.16, bf16[512,2048]{1,0:T(8,128)(2,1)} %collective-permute-done.15, bf16[256,2048]{1,0:T(8,128)(2,1)S(1)} %copy-done.22, bf16[256,2048]{1,0:T(8,128)(2,1)S(1)} %dynamic-slice_bitcast_fusion), kind=kOutput, calls=%fused_computation.50 | convolution fusion | flops 6477578240 | bytes 14680064 | tf_op jit(solution)/shard_map/dot_general | solution.py:24
  371.2 9.3 %fusion.31 = f32[1024,2048]{1,0:T(8,128)} fusion(bf16[768,2048]{1,0:T(8,128)(2,1)} %all-gather.11.cloned.1.call-done, bf16[2048,768]{0,1:T(8,128)(2,1)} %get-tuple-element.65), kind=kOutput, calls=%fused_computation.93 | convolution fusion | flops 3221225472 | bytes 13107200 | tf_op jit(solution)/shard_map/dot_general | solution.py:20
  380.6 11.2 %fusion.12 = f32[1024,2048]{1,0:T(8,128)} fusion(bf16[2048,1536]{1,0:T(8,128)(2,1)} %all-gather.9.cloned.1.call-done, bf16[2048,768]{0,1:T(8,128)(2,1)S(1)} %copy-done.57, bf16[2048,768]{0,1:T(8,128)(2,1)S(1)} %copy-done.55), kind=kOutput, calls=%fused_computation.53 | convolution fusion | flops 6448742400 | bytes 20971520 | tf_op jit(solution)/shard_map/dot_general | solution.py:28
  391.7 5.9 convert_add_fusion.2
  399.5 10.1 %convert_add_fusion.1 = f32[1024,2048]{1,0:T(8,128)} fusion(f32[1024,2048]{1,0:T(8,128)} %fusion.12, bf16[1024,2048]{1,0:T(8,128)(2,1)} %collective-permute-done.17), kind=kLoop, calls=%fused_computation.7 | loop fusion | flops 4194304 | bytes 20971520 | tf_op jit(solution)/shard_map/add | solution.py:102
  412.8 11.2 %collective-permute-done.10 = bf16[512,2048]{1,0:T(8,128)(2,1)S(1)} collective-permute-done((bf16[512,2048]{1,0:T(8,128)(2,1)S(1)}, bf16[512,2048]{1,0:T(8,128)(2,1)S(1)}, u32[]{:S(2)}, u32[]{:S(2)}) %collective-permute-start.10) | collective-permute-done | bytes 2097184 | tf_op jit(solution)/shard_map/ppermute | solution.py:69
  427.4 30.4 %collective-permute-done.18 = bf16[512,2048]{1,0:T(8,128)(2,1)S(1)} collective-permute-done((bf16[512,2048]{1,0:T(8,128)(2,1)S(1)}, bf16[512,2048]{1,0:T(8,128)(2,1)S(1)}, u32[]{:S(2)}, u32[]{:S(2)}) %collective-permute-start.18) | collective-permute-done | bytes 2097184 | tf_op jit(solution)/shard_map/ppermute | solution.py:69
  464.6 19.3 %convolution_convert_fusion = bf16[2048,1536]{1,0:T(8,128)(2,1)} fusion(bf16[2048,768]{0,1:T(8,128)(2,1)} %get-tuple-element.63, bf16[2048,768]{0,1:T(8,128)(2,1)} %get-tuple-element.64, bf16[1024,2048]{1,0:T(8,128)(2,1)} %collective-permute-done.8, bf16[512,2048]{1,0:T(8,128)(2,1)} %copy-done.26, bf16[256,2048]{1,0:T(8,128)(2,1)S(1)} %copy-done.20, ...), kind=kOutput, calls=%fused_computation.15 | convolution fusion | flops 12934184960 | bytes 20971520 | tf_op jit(solution)/shard_map/dot_general | solution.py:24
  488.5 5.7 fusion.73
  495.4 13.6 %collective-permute-done.20 = bf16[256,2048]{1,0:T(8,128)(2,1)S(1)} collective-permute-done((bf16[256,2048]{1,0:T(8,128)(2,1)S(1)}, bf16[256,2048]{1,0:T(8,128)(2,1)S(1)}, u32[]{:S(2)}, u32[]{:S(2)}) %collective-permute-start.20) | collective-permute-done | bytes 1048608 | tf_op jit(solution)/shard_map/ppermute | solution.py:69
  510.9 24.4 %collective-permute-done.21 = bf16[512,2048]{1,0:T(8,128)(2,1)S(1)} collective-permute-done((bf16[512,2048]{1,0:T(8,128)(2,1)S(1)}, bf16[512,2048]{1,0:T(8,128)(2,1)S(1)}, u32[]{:S(2)}, u32[]{:S(2)}) %collective-permute-start.21) | collective-permute-done | bytes 2097184 | tf_op jit(solution)/shard_map/ppermute | solution.py:69
  540.7 23.1 %collective-permute-done.12 = bf16[256,2048]{1,0:T(8,128)(2,1)S(1)} collective-permute-done((bf16[256,2048]{1,0:T(8,128)(2,1)}, bf16[256,2048]{1,0:T(8,128)(2,1)S(1)}, u32[]{:S(2)}, u32[]{:S(2)}) %collective-permute-start.12) | collective-permute-done | bytes 1048608 | tf_op jit(solution)/shard_map/ppermute | solution.py:73
  566.5 9.0 %fusion.36.grad_mixed = f32[2048,320]{1,0:T(8,128)} fusion(bf16[320,2048]{1,0:T(8,128)(2,1)S(1)} %copy-done.28, bf16[1024,2048]{1,0:T(8,128)(2,1)} %collective-permute-done.22, bf16[512,2048]{1,0:T(8,128)(2,1)S(1)} %copy-done.25, bf16[256,2048]{1,0:T(8,128)(2,1)S(1)} %collective-permute-done.20, bf16[256,2048]{1,0:T(8,128)(2,1)S(1)} %get-tuple-element.59), kind=kOutput, calls=%fused_computation.102 | convolution fusion | flops 2717908992 | bytes 12320768 | tf_op jit(solution)/shard_map/dot_general | solution.py:28
  575.5 27.4 %mixer_back.1 = (bf16[2048,640]{1,0:T(8,128)(2,1)}, f32[64,320]{1,0:T(8,128)}, f32[320,320]{1,0:T(8,128)}, f32[320,320]{1,0:T(8,128)}) custom-call(s32[8]{0:T(128)} %fusion.61.place, f32[2048,320]{1,0:T(8,128)} %fusion.36.grad_mixed, f32[2048,640]{1,0:T(8,128)} %fusion.35.pre.pre_tail, f32[2048,640]{1,0:T(8,128)} %fusion.35.pre.pre_tail, ...), custom_call_target="tpu_custom_call" | custom-call | flops 1808793600 | bytes 22282240 | tf_op jit(solution)/shard_map/mixer_back/pallas_call | solution.py:313
  602.8 7.6 convolution_convert_fusion.2
  623.2 6.5 convolution_convert_fusion.7
  629.8 8.9 %fusion.38 = f32[1024,2048]{1,0:T(8,128)} fusion(bf16[2048,640]{1,0:T(8,128)(2,1)} %all-gather.5.cloned.1.call-done, bf16[2048,640]{1,0:T(8,128)(2,1)} %get-tuple-element.45), kind=kOutput, calls=%fused_computation.106 | convolution fusion | flops 2684354560 | bytes 12320768 | tf_op jit(solution)/shard_map/dot_general | solution.py:28
  638.7 5.9 convert_add_fusion
  650.2 10.8 %convolution_convert_fusion.6 = bf16[2048,640]{1,0:T(8,128)(2,1)} fusion(bf16[2048,640]{1,0:T(8,128)(2,1)} %get-tuple-element.45, bf16[1024,2048]{1,0:T(8,128)(2,1)} %collective-permute-done.2, bf16[512,2048]{1,0:T(8,128)(2,1)} %collective-permute-done.1, bf16[256,2048]{1,0:T(8,128)(2,1)S(1)} %copy-done.18, bf16[256,2048]{1,0:T(8,128)(2,1)S(1)} %copy-done.11), kind=kOutput, calls=%fused_computation.51 | convolution fusion | flops 5403574272 | bytes 13631488 | tf_op jit(solution)/shard_map/dot_general | solution.py:24
  673.1 12.2 %collective-permute-done.24 = bf16[512,2048]{1,0:T(8,128)(2,1)} collective-permute-done((bf16[512,2048]{1,0:T(8,128)(2,1)}, bf16[512,2048]{1,0:T(8,128)(2,1)}, u32[]{:S(2)}, u32[]{:S(2)}) %collective-permute-start.24) | collective-permute-done | bytes 2097184 | tf_op jit(solution)/shard_map/ppermute | solution.py:69
  692.0 10.1 %collective-permute-done.42 = bf16[512,768]{1,0:T(8,128)(2,1)S(1)} collective-permute-done((bf16[512,768]{1,0:T(8,128)(2,1)S(1)}, bf16[512,768]{1,0:T(8,128)(2,1)S(1)}, u32[]{:S(2)}, u32[]{:S(2)}) %collective-permute-start.42) | collective-permute-done | bytes 786464 | tf_op jit(solution)/shard_map/ppermute | solution.py:73
  704.8 7.3 collective-permute-done.38
  715.8 33.5 %collective-permute-done.39 = f32[2,2,160,160]{3,2,1,0:T(8,128)S(1)} collective-permute-done((f32[2,2,160,160]{3,2,1,0:T(8,128)S(1)}, f32[2,2,160,160]{3,2,1,0:T(8,128)S(1)}, u32[]{:S(2)}, u32[]{:S(2)}) %collective-permute-start.39) | collective-permute-done | bytes 409632 | tf_op jit(solution)/shard_map/ppermute | solution.py:127
  758.9 9.3 %collective-permute-done.40 = f32[2,2,160,160]{3,2,1,0:T(8,128)} collective-permute-done((f32[2,2,160,160]{3,2,1,0:T(8,128)}, f32[2,2,160,160]{3,2,1,0:T(8,128)}, u32[]{:S(2)}, u32[]{:S(2)}) %collective-permute-start.40) | collective-permute-done | bytes 409632 | tf_op jit(solution)/shard_map/ppermute | solution.py:73
  777.8 3.9 collective-permute-done.26
  789.1 6.1 collective-permute-done.30
  795.4 3.8 collective-permute-done.31
  (319 shorter events, 166.7 us)
Async XLA Ops:
  7.2 81.3 %all-gather.5.cloned.1.call-start = ((), (), s32[]{:S(2)}) async-start(), calls=%async_computation.4 | async-start | bytes 3276800 | tf_op jit(solution)/shard_map/all_gather | solution.py:367
  10.5 15.8 %collective-permute-start = (bf16[256,2048]{1,0:T(8,128)(2,1)S(1)}, bf16[256,2048]{1,0:T(8,128)(2,1)S(1)}, u32[]{:S(2)}, u32[]{:S(2)}) collective-permute-start(bf16[256,2048]{1,0:T(8,128)(2,1)S(1)} %fusion.20), channel_id=1, source_target_pairs={{0,2},{1,5},{2,0},{3,7},{4,6},{5,1},{6,4},{7,3},{8,10},{9,13},{10,... | collective-permute-start | bytes 3145736 | tf_op jit(solution)/shard_map/ppermute | solution.py:69
  28.9 26.4 %collective-permute-start.1 = (bf16[512,2048]{1,0:T(8,128)(2,1)}, bf16[512,2048]{1,0:T(8,128)(2,1)}, u32[]{:S(2)}, u32[]{:S(2)}) collective-permute-start(bf16[512,2048]{1,0:T(8,128)(2,1)} %pad_maximum_fusion.12), channel_id=1, source_target_pairs={{0,4},{1,3},{2,6},{3,1},{4,0},{5,7},{6,2},{7,5},{8,12},{9,11},{10,... | collective-permute-start | bytes 6291464 | tf_op jit(solution)/shard_map/ppermute | solution.py:69
  33.4 88.6 %all-gather.7.cloned.1.call-start = ((), (), s32[]{:S(2)}) async-start(), calls=%async_computation.5 | async-start | bytes 1638400 | tf_op jit(solution)/shard_map/all_gather | solution.py:368
  58.8 29.8 %collective-permute-start.2 = (bf16[1024,2048]{1,0:T(8,128)(2,1)}, bf16[1024,2048]{1,0:T(8,128)(2,1)}, u32[]{:S(2)}, u32[]{:S(2)}) collective-permute-start(bf16[1024,2048]{1,0:T(8,128)(2,1)} %pad_maximum_fusion.6), channel_id=1, source_target_pairs={{0,1},{1,0},{2,3},{3,2},{4,5},{5,4},{6,7},{7,6},{8,9},{9,8},{10,11... | collective-permute-start | bytes 12582920 | tf_op jit(solution)/shard_map/ppermute | solution.py:69
  59.6 220.2 %all-gather.9.cloned.1.call-start = ((), (), s32[]{:S(2)}) async-start(), calls=%async_computation.6 | async-start | bytes 7864320 | tf_op jit(solution)/shard_map/all_gather | solution.py:370
  126.0 7.4 collective-permute-start.3
  144.1 26.4 %collective-permute-start.4 = (bf16[512,2048]{1,0:T(8,128)(2,1)}, bf16[512,2048]{1,0:T(8,128)(2,1)}, u32[]{:S(2)}, u32[]{:S(2)}) collective-permute-start(bf16[512,2048]{1,0:T(8,128)(2,1)} %slice.412), channel_id=1, source_target_pairs={{0,4},{1,3},{2,6},{3,1},{4,0},{5,7},{6,2},{7,5},{8,12},{9,11},{10,... | collective-permute-start | bytes 6291464 | tf_op jit(solution)/shard_map/ppermute | solution.py:69
  148.2 176.8 %all-gather.11.cloned.1.call-start = ((), (), s32[]{:S(2)}) async-start(), calls=%async_computation.7 | async-start | bytes 3932160 | tf_op jit(solution)/shard_map/all_gather | solution.py:371
  174.2 14.9 %collective-permute-start.5 = (bf16[256,2048]{1,0:T(8,128)(2,1)S(1)}, bf16[256,2048]{1,0:T(8,128)(2,1)S(1)}, u32[]{:S(2)}, u32[]{:S(2)}) collective-permute-start(bf16[256,2048]{1,0:T(8,128)(2,1)S(1)} %slice.416), channel_id=1, source_target_pairs={{0,2},{1,5},{2,0},{3,7},{4,6},{5,1},{6,4},{7,3},{8,10},{9,13},{10,... | collective-permute-start | bytes 3145736 | tf_op jit(solution)/shard_map/ppermute | solution.py:69
  192.4 14.9 %collective-permute-start.6 = (bf16[256,2048]{1,0:T(8,128)(2,1)S(1)}, bf16[256,2048]{1,0:T(8,128)(2,1)S(1)}, u32[]{:S(2)}, u32[]{:S(2)}) collective-permute-start(bf16[256,2048]{1,0:T(8,128)(2,1)S(1)} %multiply_convert_fusion.2), channel_id=1, source_target_pairs={{0,2},{1,5},{2,0},{3,7},{4,6},{5,1},{6,4},{7,3},{8,10},{9,13},{10,... | collective-permute-start | bytes 3145736 | tf_op jit(solution)/shard_map/ppermute | solution.py:69
  207.5 36.7 %collective-permute-start.7 = (bf16[512,2048]{1,0:T(8,128)(2,1)S(1)}, bf16[512,2048]{1,0:T(8,128)(2,1)S(1)}, u32[]{:S(2)}, u32[]{:S(2)}) collective-permute-start(bf16[512,2048]{1,0:T(8,128)(2,1)S(1)} %pad_maximum_fusion.13), channel_id=1, source_target_pairs={{0,4},{1,3},{2,6},{3,1},{4,0},{5,7},{6,2},{7,5},{8,12},{9,11},{10,... | collective-permute-start | bytes 6291464 | tf_op jit(solution)/shard_map/ppermute | solution.py:69
  210.4 36.6 %collective-permute-start.14 = (bf16[256,2048]{1,0:T(8,128)(2,1)S(1)}, bf16[256,2048]{1,0:T(8,128)(2,1)S(1)}, u32[]{:S(2)}, u32[]{:S(2)}) collective-permute-start(bf16[256,2048]{1,0:T(8,128)(2,1)S(1)} %dynamic-slice_bitcast_fusion), channel_id=1, source_target_pairs={{0,2},{1,5},{2,0},{3,7},{4,6},{5,1},{6,4},{7,3},{8,10},{9,13},{10,... | collective-permute-start | bytes 3145736 | tf_op jit(solution)/shard_map/ppermute | solution.py:69
  246.9 32.8 %collective-permute-start.8 = (bf16[1024,2048]{1,0:T(8,128)(2,1)}, bf16[1024,2048]{1,0:T(8,128)(2,1)}, u32[]{:S(2)}, u32[]{:S(2)}) collective-permute-start(bf16[1024,2048]{1,0:T(8,128)(2,1)} %pad_maximum_fusion.7), channel_id=1, source_target_pairs={{0,1},{1,0},{2,3},{3,2},{4,5},{5,4},{6,7},{7,6},{8,9},{9,8},{10,11... | collective-permute-start | bytes 12582920 | tf_op jit(solution)/shard_map/ppermute | solution.py:69
  249.4 26.4 %collective-permute-start.15 = (bf16[512,2048]{1,0:T(8,128)(2,1)}, bf16[512,2048]{1,0:T(8,128)(2,1)}, u32[]{:S(2)}, u32[]{:S(2)}) collective-permute-start(bf16[512,2048]{1,0:T(8,128)(2,1)} %pad_maximum_fusion.15), channel_id=1, source_target_pairs={{0,4},{1,3},{2,6},{3,1},{4,0},{5,7},{6,2},{7,5},{8,12},{9,11},{10,... | collective-permute-start | bytes 6291464 | tf_op jit(solution)/shard_map/ppermute | solution.py:69
  251.9 287.3 %reduce-scatter.11.cloned.1.call-start = ((), (), s32[]{:S(2)}) async-start(), calls=%async_computation.11 | async-start | bytes 3932160 | tf_op jit(solution)/shard_map/reduce_scatter | solution.py:442
  279.7 45.3 %collective-permute-start.16 = (bf16[1024,2048]{1,0:T(8,128)(2,1)}, bf16[1024,2048]{1,0:T(8,128)(2,1)}, u32[]{:S(2)}, u32[]{:S(2)}) collective-permute-start(bf16[1024,2048]{1,0:T(8,128)(2,1)} %pad_maximum_fusion.9), channel_id=1, source_target_pairs={{0,1},{1,0},{2,3},{3,2},{4,5},{5,4},{6,7},{7,6},{8,9},{9,8},{10,11... | collective-permute-start | bytes 12582920 | tf_op jit(solution)/shard_map/ppermute | solution.py:69
  352.2 39.5 %collective-permute-start.9 = (bf16[1024,2048]{1,0:T(8,128)(2,1)}, bf16[1024,2048]{1,0:T(8,128)(2,1)}, u32[]{:S(2)}, u32[]{:S(2)}) collective-permute-start(bf16[1024,2048]{1,0:T(8,128)(2,1)} %convolution_convert_fusion.4), channel_id=1, source_target_pairs={{0,1},{1,0},{2,3},{3,2},{4,5},{5,4},{6,7},{7,6},{8,9},{9,8},{10,11... | collective-permute-start | bytes 12582920 | tf_op jit(solution)/shard_map/ppermute | solution.py:69
  360.7 38.7 %collective-permute-start.17 = (bf16[1024,2048]{1,0:T(8,128)(2,1)}, bf16[1024,2048]{1,0:T(8,128)(2,1)}, u32[]{:S(2)}, u32[]{:S(2)}) collective-permute-start(bf16[1024,2048]{1,0:T(8,128)(2,1)} %convolution_convert_fusion.1), channel_id=1, source_target_pairs={{0,1},{1,0},{2,3},{3,2},{4,5},{5,4},{6,7},{7,6},{8,9},{9,8},{10,11... | collective-permute-start | bytes 12582920 | tf_op jit(solution)/shard_map/ppermute | solution.py:69
  371.1 248.4 %reduce-scatter.9.cloned.1.call-start = ((), (), s32[]{:S(2)}) async-start(), calls=%async_computation.10 | async-start | bytes 7864320 | tf_op jit(solution)/shard_map/reduce_scatter | solution.py:442
  397.9 26.1 %collective-permute-start.10 = (bf16[512,2048]{1,0:T(8,128)(2,1)S(1)}, bf16[512,2048]{1,0:T(8,128)(2,1)S(1)}, u32[]{:S(2)}, u32[]{:S(2)}) collective-permute-start(bf16[512,2048]{1,0:T(8,128)(2,1)S(1)} %slice.411), channel_id=1, source_target_pairs={{0,4},{1,3},{2,6},{3,1},{4,0},{5,7},{6,2},{7,5},{8,12},{9,11},{10,... | collective-permute-start | bytes 6291464 | tf_op jit(solution)/shard_map/ppermute | solution.py:69
  412.3 45.5 %collective-permute-start.18 = (bf16[512,2048]{1,0:T(8,128)(2,1)S(1)}, bf16[512,2048]{1,0:T(8,128)(2,1)S(1)}, u32[]{:S(2)}, u32[]{:S(2)}) collective-permute-start(bf16[512,2048]{1,0:T(8,128)(2,1)S(1)} %slice.410), channel_id=1, source_target_pairs={{0,4},{1,3},{2,6},{3,1},{4,0},{5,7},{6,2},{7,5},{8,12},{9,11},{10,... | collective-permute-start | bytes 6291464 | tf_op jit(solution)/shard_map/ppermute | solution.py:69
  425.9 62.6 %collective-permute-start.11 = (bf16[256,2048]{1,0:T(8,128)(2,1)}, bf16[256,2048]{1,0:T(8,128)(2,1)}, u32[]{:S(2)}, u32[]{:S(2)}) collective-permute-start(bf16[256,2048]{1,0:T(8,128)(2,1)} %slice.415), channel_id=1, source_target_pairs={{0,2},{1,5},{2,0},{3,7},{4,6},{5,1},{6,4},{7,3},{8,10},{9,13},{10,... | collective-permute-start | bytes 3145736 | tf_op jit(solution)/shard_map/ppermute | solution.py:69
  463.2 20.8 %collective-permute-start.19 = (bf16[256,2048]{1,0:T(8,128)(2,1)}, bf16[256,2048]{1,0:T(8,128)(2,1)S(1)}, u32[]{:S(2)}, u32[]{:S(2)}) collective-permute-start(bf16[256,2048]{1,0:T(8,128)(2,1)} %slice.414), channel_id=1, source_target_pairs={{0,2},{1,5},{2,0},{3,7},{4,6},{5,1},{6,4},{7,3},{8,10},{9,13},{10,... | collective-permute-start | bytes 3145736 | tf_op jit(solution)/shard_map/ppermute | solution.py:69
  483.9 268.0 %reduce-scatter.7.cloned.1.call-start = ((), (), s32[]{:S(2)}) async-start(), calls=%async_computation.9 | async-start | bytes 1638400 | tf_op jit(solution)/shard_map/reduce_scatter | solution.py:442
  494.2 14.8 %collective-permute-start.20 = (bf16[256,2048]{1,0:T(8,128)(2,1)S(1)}, bf16[256,2048]{1,0:T(8,128)(2,1)S(1)}, u32[]{:S(2)}, u32[]{:S(2)}) collective-permute-start(bf16[256,2048]{1,0:T(8,128)(2,1)S(1)} %get-tuple-element.59), channel_id=1, source_target_pairs={{0,2},{1,5},{2,0},{3,7},{4,6},{5,1},{6,4},{7,3},{8,10},{9,13},{10,... | collective-permute-start | bytes 3145736 | tf_op jit(solution)/shard_map/ppermute | solution.py:69
  509.2 26.1 %collective-permute-start.21 = (bf16[512,2048]{1,0:T(8,128)(2,1)S(1)}, bf16[512,2048]{1,0:T(8,128)(2,1)S(1)}, u32[]{:S(2)}, u32[]{:S(2)}) collective-permute-start(bf16[512,2048]{1,0:T(8,128)(2,1)S(1)} %pad_maximum_fusion.16), channel_id=1, source_target_pairs={{0,4},{1,3},{2,6},{3,1},{4,0},{5,7},{6,2},{7,5},{8,12},{9,11},{10,... | collective-permute-start | bytes 6291464 | tf_op jit(solution)/shard_map/ppermute | solution.py:69
  538.0 28.5 %collective-permute-start.22 = (bf16[1024,2048]{1,0:T(8,128)(2,1)}, bf16[1024,2048]{1,0:T(8,128)(2,1)}, u32[]{:S(2)}, u32[]{:S(2)}) collective-permute-start(bf16[1024,2048]{1,0:T(8,128)(2,1)} %pad_maximum_fusion.10), channel_id=1, source_target_pairs={{0,1},{1,0},{2,3},{3,2},{4,5},{5,4},{6,7},{7,6},{8,9},{9,8},{10,11... | collective-permute-start | bytes 12582920 | tf_op jit(solution)/shard_map/ppermute | solution.py:69
  538.0 25.8 %collective-permute-start.12 = (bf16[256,2048]{1,0:T(8,128)(2,1)}, bf16[256,2048]{1,0:T(8,128)(2,1)S(1)}, u32[]{:S(2)}, u32[]{:S(2)}) collective-permute-start(bf16[256,2048]{1,0:T(8,128)(2,1)} %get-tuple-element.78), channel_id=1, source_target_pairs={{0,2},{1,3},{2,0},{3,1},{4,6},{5,7},{6,4},{7,5},{8,10},{9,11},{10,... | collective-permute-start | bytes 3145736 | tf_op jit(solution)/shard_map/ppermute | solution.py:73
  539.2 71.7 %collective-permute-start.44 = (bf16[768,512]{1,0:T(8,128)(2,1)}, bf16[768,512]{1,0:T(8,128)(2,1)}, u32[]{:S(2)}, u32[]{:S(2)}) collective-permute-start(bf16[768,512]{1,0:T(8,128)(2,1)} %reduce-scatter.11.cloned.1.call-done), channel_id=1, source_target_pairs={{0,4},{1,5},{2,6},{3,7},{4,0},{5,1},{6,2},{7,3},{8,12},{9,13},{10,... | collective-permute-start | bytes 2359304 | tf_op jit(solution)/shard_map/ppermute | solution.py:73
  566.5 48.0 %collective-permute-start.13 = (bf16[512,2048]{1,0:T(8,128)(2,1)}, bf16[512,2048]{1,0:T(8,128)(2,1)}, u32[]{:S(2)}, u32[]{:S(2)}) collective-permute-start(bf16[512,2048]{1,0:T(8,128)(2,1)} %pad_maximum_fusion.14), channel_id=1, source_target_pairs={{0,1},{1,0},{2,3},{3,2},{4,5},{5,4},{6,7},{7,6},{8,9},{9,8},{10,11... | collective-permute-start | bytes 6291464 | tf_op jit(solution)/shard_map/ppermute | solution.py:73
  610.4 28.3 %collective-permute-start.23 = (bf16[1024,2048]{1,0:T(8,128)(2,1)}, bf16[1024,2048]{1,0:T(8,128)(2,1)}, u32[]{:S(2)}, u32[]{:S(2)}) collective-permute-start(bf16[1024,2048]{1,0:T(8,128)(2,1)} %convolution_convert_fusion.2), channel_id=1, source_target_pairs={{0,1},{1,0},{2,3},{3,2},{4,5},{5,4},{6,7},{7,6},{8,9},{9,8},{10,11... | collective-permute-start | bytes 12582920 | tf_op jit(solution)/shard_map/ppermute | solution.py:69
  621.6 39.5 %collective-permute-start.43 = (bf16[512,768]{1,0:T(8,128)(2,1)}, bf16[512,768]{1,0:T(8,128)(2,1)}, u32[]{:S(2)}, u32[]{:S(2)}) collective-permute-start(bf16[512,768]{1,0:T(8,128)(2,1)} %slice.259), channel_id=1, source_target_pairs={{0,4},{1,5},{2,6},{3,7},{4,0},{5,1},{6,2},{7,3},{8,12},{9,13},{10,... | collective-permute-start | bytes 2359304 | tf_op jit(solution)/shard_map/ppermute | solution.py:73
  629.7 144.9 %reduce-scatter.5.cloned.1.call-start = ((), (), s32[]{:S(2)}) async-start(), calls=%async_computation.8 | async-start | bytes 3276800 | tf_op jit(solution)/shard_map/reduce_scatter | solution.py:442
  649.6 35.8 %collective-permute-start.24 = (bf16[512,2048]{1,0:T(8,128)(2,1)}, bf16[512,2048]{1,0:T(8,128)(2,1)}, u32[]{:S(2)}, u32[]{:S(2)}) collective-permute-start(bf16[512,2048]{1,0:T(8,128)(2,1)} %slice.409), channel_id=1, source_target_pairs={{0,4},{1,3},{2,6},{3,1},{4,0},{5,7},{6,2},{7,5},{8,12},{9,11},{10,... | collective-permute-start | bytes 6291464 | tf_op jit(solution)/shard_map/ppermute | solution.py:69
  662.6 39.5 %collective-permute-start.42 = (bf16[512,768]{1,0:T(8,128)(2,1)S(1)}, bf16[512,768]{1,0:T(8,128)(2,1)S(1)}, u32[]{:S(2)}, u32[]{:S(2)}) collective-permute-start(bf16[512,768]{1,0:T(8,128)(2,1)S(1)} %get-tuple-element.81), channel_id=1, source_target_pairs={{0,4},{1,5},{2,6},{3,7},{4,0},{5,1},{6,2},{7,3},{8,12},{9,13},{10,... | collective-permute-start | bytes 2359304 | tf_op jit(solution)/shard_map/ppermute | solution.py:73
  667.0 45.1 %collective-permute-start.38 = (f32[2,2,160,160]{3,2,1,0:T(8,128)S(1)}, f32[2,2,160,160]{3,2,1,0:T(8,128)S(1)}, u32[]{:S(2)}, u32[]{:S(2)}) collective-permute-start(f32[2,2,160,160]{3,2,1,0:T(8,128)S(1)} %bitcast.64), channel_id=1, source_target_pairs={{0,8},{8,0},{16,24},{24,16},{1,9},{9,1},{17,25},{25,17},{2,10},{10... | collective-permute-start | bytes 1228808 | tf_op jit(solution)/shard_map/ppermute | solution.py:127
  670.1 32.2 %collective-permute-start.36 = (f32[8,320]{1,0:T(8,128)S(1)}, f32[8,320]{1,0:T(8,128)S(1)}, u32[]{:S(2)}, u32[]{:S(2)}) collective-permute-start(f32[8,320]{1,0:T(8,128)S(1)} %add.252), channel_id=1, source_target_pairs={{0,16},{8,24},{16,0},{24,8},{1,17},{9,25},{17,1},{25,9},{2,18},{10... | collective-permute-start | bytes 30728 | tf_op jit(solution)/shard_map/ppermute | solution.py:127
  691.0 61.2 %collective-permute-start.25 = (bf16[256,2048]{1,0:T(8,128)(2,1)}, bf16[256,2048]{1,0:T(8,128)(2,1)}, u32[]{:S(2)}, u32[]{:S(2)}) collective-permute-start(bf16[256,2048]{1,0:T(8,128)(2,1)} %slice.413), channel_id=1, source_target_pairs={{0,2},{1,5},{2,0},{3,7},{4,6},{5,1},{6,4},{7,3},{8,10},{9,13},{10,... | collective-permute-start | bytes 3145736 | tf_op jit(solution)/shard_map/ppermute | solution.py:69
  702.3 11.5 %collective-permute-start.37 = (f32[8,320]{1,0:T(8,128)S(1)}, f32[8,320]{1,0:T(8,128)S(1)}, u32[]{:S(2)}, u32[]{:S(2)}) collective-permute-start(f32[8,320]{1,0:T(8,128)S(1)} %add.253), channel_id=1, source_target_pairs={{0,4},{1,5},{2,6},{3,7},{4,0},{5,1},{6,2},{7,3},{8,12},{9,13},{10,... | collective-permute-start | bytes 30728 | tf_op jit(solution)/shard_map/ppermute | solution.py:73
  712.2 37.1 %collective-permute-start.39 = (f32[2,2,160,160]{3,2,1,0:T(8,128)S(1)}, f32[2,2,160,160]{3,2,1,0:T(8,128)S(1)}, u32[]{:S(2)}, u32[]{:S(2)}) collective-permute-start(f32[2,2,160,160]{3,2,1,0:T(8,128)S(1)} %add.254), channel_id=1, source_target_pairs={{0,16},{8,24},{16,0},{24,8},{1,17},{9,25},{17,1},{25,9},{2,18},{10... | collective-permute-start | bytes 1228808 | tf_op jit(solution)/shard_map/ppermute | solution.py:127
  750.2 17.9 %collective-permute-start.40 = (f32[2,2,160,160]{3,2,1,0:T(8,128)}, f32[2,2,160,160]{3,2,1,0:T(8,128)}, u32[]{:S(2)}, u32[]{:S(2)}) collective-permute-start(f32[2,2,160,160]{3,2,1,0:T(8,128)} %add.255), channel_id=1, source_target_pairs={{0,4},{1,5},{2,6},{3,7},{4,0},{5,1},{6,2},{7,3},{8,12},{9,13},{10,... | collective-permute-start | bytes 1228808 | tf_op jit(solution)/shard_map/ppermute | solution.py:73
  751.9 21.4 %collective-permute-start.41 = (bf16[320,512]{1,0:T(8,128)(2,1)}, bf16[320,512]{1,0:T(8,128)(2,1)S(1)}, u32[]{:S(2)}, u32[]{:S(2)}) collective-permute-start(bf16[320,512]{1,0:T(8,128)(2,1)} %reduce-scatter.7.cloned.1.call-done), channel_id=1, source_target_pairs={{0,4},{1,5},{2,6},{3,7},{4,0},{5,1},{6,2},{7,3},{8,12},{9,13},{10,... | collective-permute-start | bytes 983048 | tf_op jit(solution)/shard_map/ppermute | solution.py:73
  757.7 24.0 %collective-permute-start.26 = (bf16[256,2048]{1,0:T(8,128)(2,1)S(1)}, bf16[256,2048]{1,0:T(8,128)(2,1)S(1)}, u32[]{:S(2)}, u32[]{:S(2)}) collective-permute-start(bf16[256,2048]{1,0:T(8,128)(2,1)S(1)} %fusion.25), channel_id=1, source_target_pairs={{0,2},{1,3},{2,0},{3,1},{4,6},{5,7},{6,4},{7,5},{8,10},{9,11},{10,... | collective-permute-start | bytes 3145736 | tf_op jit(solution)/shard_map/ppermute | solution.py:73
  775.9 9.5 %collective-permute-start.34 = (bf16[512,320]{1,0:T(8,128)(2,1)S(1)}, bf16[512,320]{1,0:T(8,128)(2,1)S(1)}, u32[]{:S(2)}, u32[]{:S(2)}) collective-permute-start(bf16[512,320]{1,0:T(8,128)(2,1)S(1)} %slice.246), channel_id=1, source_target_pairs={{0,4},{1,5},{2,6},{3,7},{4,0},{5,1},{6,2},{7,3},{8,12},{9,13},{10,... | collective-permute-start | bytes 983048 | tf_op jit(solution)/shard_map/ppermute | solution.py:73
  781.9 22.7 %collective-permute-start.27 = (bf16[512,2048]{1,0:T(8,128)(2,1)S(1)}, bf16[512,2048]{1,0:T(8,128)(2,1)S(1)}, u32[]{:S(2)}, u32[]{:S(2)}) collective-permute-start(bf16[512,2048]{1,0:T(8,128)(2,1)S(1)} %pad_maximum_fusion.17), channel_id=1, source_target_pairs={{0,1},{1,0},{2,3},{3,2},{4,5},{5,4},{6,7},{7,6},{8,9},{9,8},{10,11... | collective-permute-start | bytes 6291464 | tf_op jit(solution)/shard_map/ppermute | solution.py:73
  785.6 9.7 %collective-permute-start.33 = (bf16[512,320]{1,0:T(8,128)(2,1)S(1)}, bf16[512,320]{1,0:T(8,128)(2,1)S(1)}, u32[]{:S(2)}, u32[]{:S(2)}) collective-permute-start(bf16[512,320]{1,0:T(8,128)(2,1)S(1)} %get-tuple-element.92), channel_id=1, source_target_pairs={{0,4},{1,5},{2,6},{3,7},{4,0},{5,1},{6,2},{7,3},{8,12},{9,13},{10,... | collective-permute-start | bytes 983048 | tf_op jit(solution)/shard_map/ppermute | solution.py:73
  787.5 7.7 collective-permute-start.30
  (65 other events, 1319.6 us)
Sparse Core Ops, SparseCore 0:
  33.4 55.0 all-gather.4
  90.7 31.2 all-gather.6
  148.4 113.5 all-gather.8
  263.4 61.6 all-gather.10
  371.3 59.0 reduce-scatter.10
  484.1 108.5 reduce-scatter.8
  629.8 29.9 reduce-scatter.6
  662.2 74.3 reduce-scatter.4

commit v2 on v1

--- a/solution.py
+++ b/solution.py
@@ -87,12 +87,6 @@
     return table
 
 
-def gather_rows(rows):
-    for kind in ("near", "far", "core"):
-        rows = jnp.concatenate([rows, exchange(rows, kind)], axis=0)
-    return rows
-
-
 def reduce_rows(left, right, product):
     half = left.shape[0] // 2
     sent = product(left[half:], right).astype(BF16)
@@ -107,17 +101,338 @@
     return total
 
 
-def whole_rows(rows):
-    count = rows.shape[0]
-    rows = jnp.concatenate([rows, flip(rows, 2)], axis=0)
-    rows = jnp.concatenate([rows, flip(rows, 1)], axis=0)
-    place = lax.axis_index("tp")
-    blocks = []
-    for b in range(4):
-        away = jnp.bitwise_xor(place, b)
-        spot = (away % 2) * 2 + away // 2
-        blocks.append(lax.dynamic_slice_in_dim(rows, spot * count, count, 0))
-    return jnp.concatenate(blocks, axis=0)
+def partners():
+    fsdp, ctx, tp = lax.axis_index("fsdp"), lax.axis_index("ctx"), lax.axis_index("tp")
+    core, line = tp % 2, tp // 2
+    across = (fsdp, 1 - ctx, tp)
+    along = (fsdp, ctx, (1 - line) * 2 + core)
+    same = (fsdp, ctx, line * 2 + 1 - core)
+    near = (fsdp, ctx + core * (1 - 2 * ctx), (line + (1 - core) * (1 - 2 * line)) * 2 + core)
+    far = (fsdp, ctx + (1 - core) * (1 - 2 * ctx), (line + core * (1 - 2 * line)) * 2 + core)
+    return core, line, tp, across, along, same, near, far
+
+
+def meet(*devices):
+    barrier = pltpu.get_barrier_semaphore()
+    for device in devices:
+        pl.semaphore_signal(barrier, inc=1, device_id=device, device_id_type=pl.DeviceIdType.MESH)
+    pl.semaphore_wait(barrier, len(devices))
+
+
+def remote(src, dst, send_sem, recv_sem, device):
+    return pltpu.make_async_remote_copy(
+        src_ref=src, dst_ref=dst, send_sem=send_sem, recv_sem=recv_sem, device_id=device,
+        device_id_type=pl.DeviceIdType.MESH,
+    )
+
+
+def by_rows(count, step, body):
+    def turn(i, _):
+        body(pl.multiple_of(i * step, step))
+        return 0
+
+    lax.fori_loop(0, count // step, turn, 0)
+
+
+def head_kernel(tokens, cot, gain, normed_out, cot_out, x_buf, n_buf, c_buf, load, store, send, recv):
+    rows = x_buf.shape[0] // 4
+    core, line, tp, across, along, same, _, _ = partners()
+    load_x = pltpu.make_async_copy(tokens, x_buf, load.at[0])
+    load_c = pltpu.make_async_copy(cot, c_buf, load.at[1])
+    load_x.start()
+    load_c.start()
+    meet(across, along, same)
+
+    def block(j):
+        return pl.ds(pl.multiple_of(j * rows, rows), rows)
+
+    def normalize(j):
+        def body(r):
+            at = pl.ds(pl.multiple_of(j * rows + r, 32), 32)
+            x = x_buf[at, :].astype(F32)
+            n_buf[at, :] = (x * rms_rows(x) * gain[...]).astype(BF16)
+
+        by_rows(rows, 32, body)
+
+    load_x.wait()
+    normalize(tp)
+    outs = (normed_out, cot_out)
+    bufs = (n_buf, c_buf)
+    first = [
+        remote(bufs[i].at[block(tp)], outs[i].at[2 - core], send.at[i], recv.at[i], across) for i in range(2)
+    ]
+    first[0].start()
+    load_c.wait()
+    first[1].start()
+    for j in range(1, 4):
+        normalize((tp + j) % 4)
+    kept = []
+    for k, (dy, dc) in enumerate(((0, 0), (1, 0), (0, 1), (1, 1))):
+        there = line + dy * (1 - 2 * line)
+        which = core + dc * (1 - 2 * core)
+        effect = which
+        spot = 4 * dc + dy * (1 + effect)
+        for i in range(2):
+            copy = pltpu.make_async_copy(bufs[i].at[block(there * 2 + which)], outs[i].at[spot], store.at[2 * k + i])
+            copy.start()
+            kept.append(copy)
+    later = []
+    for i in range(2):
+        first[i].wait_recv()
+        second = remote(outs[i].at[2 - core], outs[i].at[3], send.at[2 + i], recv.at[2 + i], along)
+        second.start()
+        third = remote(outs[i].at[2 - core], outs[i].at[6 - core], send.at[4 + i], recv.at[4 + i], same)
+        third.start()
+        later.append((second, third))
+    last = []
+    for i in range(2):
+        later[i][0].wait_recv()
+        fourth = remote(outs[i].at[3], outs[i].at[7], send.at[6 + i], recv.at[6 + i], same)
+        fourth.start()
+        last.append(fourth)
+    for i in range(2):
+        later[i][1].wait_recv()
+        last[i].wait_recv()
+        first[i].wait_send()
+        later[i][0].wait_send()
+        later[i][1].wait_send()
+        last[i].wait_send()
+    for copy in kept:
+        copy.wait()
+
+
+def head(tokens, cot, gain, collective_id):
+    count, width = tokens.shape
+    rows = count // 4
+    out = jax.ShapeDtypeStruct((8, rows, width), BF16)
+    anywhere = pl.BlockSpec(memory_space=pl.ANY)
+    return pl.pallas_call(
+        head_kernel,
+        in_specs=[anywhere, anywhere, pl.BlockSpec(memory_space=pltpu.VMEM)],
+        out_specs=[anywhere, anywhere],
+        out_shape=[out, out],
+        scratch_shapes=[pltpu.VMEM((count, width), BF16)] * 3
+        + [
+            pltpu.SemaphoreType.DMA((2,)),
+            pltpu.SemaphoreType.DMA((8,)),
+            pltpu.SemaphoreType.DMA((8,)),
+            pltpu.SemaphoreType.DMA((8,)),
+        ],
+        compiler_params=pltpu.CompilerParams(
+            collective_id=collective_id, has_side_effects=True, vmem_limit_bytes=60 << 20
+        ),
+        cost_estimate=pl.CostEstimate(flops=5 << 33, bytes_accessed=64 << 20, transcendentals=0),
+        name="head",
+    )(tokens, cot, gain)
+
+
+def plane_sum_kernel(
+    epilogue, wide, left, right, base, source, gain, *refs
+):
+    if epilogue == "norm":
+        out, kept_out, refs = refs[0], refs[1], refs[2:]
+    elif wide:
+        out, kept_out, gain_out, refs = refs[0], refs[1], refs[2], refs[3:]
+    else:
+        rows_in, pair, single, out, gain_out, rows_out, pair_a, pair_b, single_out = refs[:9]
+        refs = refs[9:]
+    to_core, from_core, acc, to_far, from_far, to_near, from_near, own, store, send, recv, gsend, grecv = refs
+    rows, width = own.shape
+    core, line, tp, across, along, same, near, far = partners()
+    meet(same, near, far)
+    tile = width // 4
+
+    def products(row, ref, at):
+        def turn(i, _):
+            cols = pl.ds(pl.multiple_of(i * tile, tile), tile)
+            part = right_inner(left[pl.ds(row, 2 * rows), :], right[cols, :])
+            ref[pl.ds(at, 2 * rows), cols] = part.astype(ref.dtype)
+            return 0
+
+        lax.fori_loop(0, 4, turn, 0)
+
+    def both(a):
+        return pl.ds(a * rows, 2 * rows)
+
+    core_copy = [
+        remote(to_core.at[both(2 * h)], from_core.at[both(2 * h)], send.at[h], recv.at[h], same) for h in range(2)
+    ]
+    far_copy = [remote(to_far.at[h], from_far.at[h], send.at[2 + h], recv.at[2 + h], far) for h in range(2)]
+    near_copy = remote(to_near, from_near, send.at[4], recv.at[4], near)
+
+    local = []
+    if not wide:
+        came = (1 - line) * 2 + core
+        local.append(pltpu.make_async_copy(rows_in, rows_out.at[tp], store.at[1]))
+        rows_copy = [
+            remote(rows_in, rows_out.at[tp], gsend.at[3], grecv.at[3], along),
+            remote(rows_in, rows_out.at[tp], gsend.at[4], grecv.at[4], same),
+            remote(rows_out.at[came], rows_out.at[came], gsend.at[5], grecv.at[5], same),
+        ]
+        half_at = lax.axis_index("ctx")
+        units, deep = pair.shape[1] // 2, single.shape[0]
+        cols = pl.ds(pl.multiple_of(half_at * units, 128), units)
+        lines = pl.ds(pl.multiple_of(half_at * deep, 16), deep)
+        swap = (
+            (pair.at[:, pl.ds(0, units)], pair_a.at[:, cols]),
+            (pair.at[:, pl.ds(units, units)], pair_b.at[:, cols]),
+            (single, single_out.at[lines, :]),
+        )
+        half_copy = [
+            remote(src, dst, gsend.at[6 + i], grecv.at[6 + i], across) for i, (src, dst) in enumerate(swap)
+        ]
+        local += [pltpu.make_async_copy(src, dst, store.at[2 + i]) for i, (src, dst) in enumerate(swap)]
+        rows_copy[0].start()
+        rows_copy[1].start()
+        for copy in local:
+            copy.start()
+
+    products(6 * rows, to_core, 2 * rows)
+    core_copy[1].start()
+    products(2 * rows, acc, 2 * rows)
+    core_copy[1].wait_recv()
+    for h in (1, 0):
+        def body(r, h=h):
+            at = pl.ds(pl.multiple_of((2 + h) * rows + r, 32), 32)
+            to_far[h, pl.ds(r, 32), :] = (acc[at, :] + from_core[at, :].astype(F32)).astype(BF16)
+
+        by_rows(rows, 32, body)
+        far_copy[h].start()
+    products(4 * rows, to_core, 0)
+    core_copy[0].start()
+    products(0, acc, 0)
+    core_copy[0].wait_recv()
+    far_copy[1].wait_recv()
+
+    def send_near(r):
+        at = pl.ds(pl.multiple_of(rows + r, 32), 32)
+        total = acc[at, :] + from_core[at, :].astype(F32) + from_far[1, pl.ds(r, 32), :].astype(F32)
+        to_near[pl.ds(r, 32), :] = total.astype(BF16)
+
+    by_rows(rows, 32, send_near)
+    near_copy.start()
+    far_copy[0].wait_recv()
+    if not wide:
+        for copy in half_copy:
+            copy.start()
+        rows_copy[0].wait_recv()
+        rows_copy[2].start()
+
+    def settle(r):
+        at = pl.ds(r, 32)
+        acc[at, :] = acc[at, :] + from_core[at, :].astype(F32) + from_far[0, at, :].astype(F32)
+
+    by_rows(rows, 32, settle)
+    if epilogue != "norm":
+        gain_out[...] = jnp.zeros_like(gain_out)
+    near_copy.wait_recv()
+
+    def finish(r):
+        at = pl.ds(r, 32)
+        total = acc[at, :] + from_near[at, :].astype(F32)
+        if epilogue == "norm":
+            resid = base[at, :].astype(F32) + total
+            kept_out[at, :] = resid
+            own[at, :] = (resid * rms_rows(resid) * gain[...]).astype(BF16)
+        else:
+            x = source[at, :].astype(F32)
+            scale = rms_rows(x)
+            scaled = x * scale
+            grad = base[at, :].astype(F32) + norm_back(total, scaled, scale, gain[...])
+            gain_out[...] += jnp.sum((total * scaled).reshape(4, 8, width), axis=0)
+            if wide:
+                kept_out[at, :] = grad
+            own[at, :] = grad.astype(BF16)
+
+    by_rows(rows, 32, finish)
+    if wide:
+        mine = pltpu.make_async_copy(own, out.at[0], store.at[0])
+        mine.start()
+        copies = [
+            remote(own, out.at[1], gsend.at[1], grecv.at[1], near),
+            remote(own, out.at[2], gsend.at[2], grecv.at[2], far),
+            remote(own, out.at[4], gsend.at[4], grecv.at[4], same),
+            remote(out.at[1], out.at[3], gsend.at[3], grecv.at[3], far),
+            remote(out.at[1], out.at[5], gsend.at[5], grecv.at[5], same),
+            remote(out.at[2], out.at[6], gsend.at[6], grecv.at[6], same),
+            remote(out.at[3], out.at[7], gsend.at[7], grecv.at[7], same),
+        ]
+        for k in range(3):
+            copies[k].start()
+        copies[0].wait_recv()
+        copies[3].start()
+        copies[4].start()
+        copies[1].wait_recv()
+        copies[5].start()
+        copies[3].wait_recv()
+        copies[6].start()
+        for k in (2, 4, 5, 6):
+            copies[k].wait_recv()
+    else:
+        mine = pltpu.make_async_copy(own, out.at[tp], store.at[0])
+        mine.start()
+        copies = [
+            remote(own, out.at[tp], gsend.at[0], grecv.at[0], along),
+            remote(own, out.at[tp], gsend.at[1], grecv.at[1], same),
+        ]
+        copies[0].start()
+        copies[1].start()
+        copies[0].wait_recv()
+        copies.append(remote(out.at[came], out.at[came], gsend.at[2], grecv.at[2], same))
+        copies[2].start()
+        copies[1].wait_recv()
+        copies[2].wait_recv()
+        for copy in rows_copy[1:] + half_copy:
+            copy.wait_recv()
+        copies += rows_copy + half_copy
+    for copy in copies + core_copy + far_copy + [near_copy]:
+        copy.wait_send()
+    for copy in local + [mine]:
+        copy.wait()
+
+
+def plane_sum(epilogue, wide, left, right, base, source, gain, collective_id, cost, extra_in=()):
+    count, width = left.shape[0], right.shape[0]
+    rows = count // 8
+    vmem = pl.BlockSpec(memory_space=pltpu.VMEM)
+    anywhere = pl.BlockSpec(memory_space=pl.ANY)
+    whole = jax.ShapeDtypeStruct((rows, width), F32)
+    gains = jax.ShapeDtypeStruct((8, width), F32)
+    extra = [whole] if epilogue == "norm" else [whole, gains] if wide else [gains]
+    carried = []
+    if not wide:
+        _, pair, single = extra_in
+        carried = [(4, rows, width), pair.shape, pair.shape, (2 * single.shape[0], single.shape[1])]
+        carried = [jax.ShapeDtypeStruct(shape, BF16) for shape in carried]
+    return pl.pallas_call(
+        functools.partial(plane_sum_kernel, epilogue, wide),
+        in_specs=[vmem] * (5 + len(extra_in)),
+        out_specs=[anywhere] + [vmem] * len(extra) + [anywhere] * len(carried),
+        out_shape=[jax.ShapeDtypeStruct((8 if wide else 4, rows, width), BF16)] + extra + carried,
+        scratch_shapes=[
+            pltpu.VMEM((4 * rows, width), BF16),
+            pltpu.VMEM((4 * rows, width), BF16),
+            pltpu.VMEM((4 * rows, width), F32),
+            pltpu.VMEM((2, rows, width), BF16),
+            pltpu.VMEM((2, rows, width), BF16),
+            pltpu.VMEM((rows, width), BF16),
+            pltpu.VMEM((rows, width), BF16),
+            pltpu.VMEM((rows, width), BF16),
+            pltpu.SemaphoreType.DMA((5,)),
+            pltpu.SemaphoreType.DMA((5,)),
+            pltpu.SemaphoreType.DMA((5,)),
+            pltpu.SemaphoreType.DMA((9,)),
+            pltpu.SemaphoreType.DMA((9,)),
+        ],
+        compiler_params=pltpu.CompilerParams(
+            collective_id=collective_id, has_side_effects=True, vmem_limit_bytes=62 << 20
+        ),
+        cost_estimate=pl.CostEstimate(flops=cost, bytes_accessed=count * width, transcendentals=0),
+        name="plane_sum",
+    )(left, right, base, source, gain, *extra_in)
+
+
+tied = lax.optimization_barrier
 
 
 def sum_fsdp(x):
@@ -125,6 +440,17 @@
     bit = 1
     while bit < size:
         x = x + lax.ppermute(x, "fsdp", [(i, i ^ bit) for i in range(size)])
+        bit *= 2
+    return x
+
+
+def gather_fsdp(x):
+    size, at = lax.axis_size("fsdp"), lax.axis_index("fsdp")
+    bit = 1
+    while bit < size:
+        other = lax.ppermute(x, "fsdp", [(i, i ^ bit) for i in range(size)])
+        later = (at // bit) % 2 == 1
+        x = jnp.concatenate([jnp.where(later, other, x), jnp.where(later, x, other)], axis=0)
         bit *= 2
     return x
 
@@ -360,17 +686,20 @@
         size = x.shape[axis] // 2
         return lax.dynamic_slice_in_dim(x, half_at * size, size, axis)
 
+    def owned(x, axis):
+        return lax.psum_scatter(x, "fsdp", scatter_dimension=axis, tiled=True)
+
     _, tok_count, model_width = tokens.shape
     rows = tok_count // 4
     length = 2 * tok_count
-    own_in = jnp.concatenate([mine(w_branch, 1), mine(w_input, 1)], axis=1)
-    full_in = lax.all_gather(own_in, "fsdp", axis=0, tiled=True)
-    full_out = lax.all_gather(mine(w_out, 0), "fsdp", axis=1, tiled=True)
+    own_in = jnp.concatenate([mine(w_branch, 1), mine(w_input, 1), mine(w_out, 0).T], axis=1)
+    full_mix = lax.all_gather(own_in, "fsdp", axis=0, tiled=True)
     own_gu = jnp.concatenate([mine(w_gate, 1), mine(w_up, 1)], axis=1)
     full_gu = lax.all_gather(own_gu, "fsdp", axis=0, tiled=True)
     full_down = lax.all_gather(mine(w_down, 0), "fsdp", axis=1, tiled=True)
 
-    width = own_in.shape[1] // 2
+    width = own_in.shape[1] // 3
+    full_in, full_out = full_mix[:, : 2 * width], full_mix[:, 2 * width :]
     units = own_gu.shape[1] // 2
     place = jnp.asarray(place_table())[half_at * 4 + place_tp]
 
@@ -393,26 +722,23 @@
     masks = jnp.stack(marks, axis=1).astype(F32)
 
     own = lax.dynamic_slice_in_dim(tokens[0], place_tp * rows, rows, 0)
-    inputs = own.astype(F32)
-    scale_mix = rms_rows(inputs)
-    scaled_mix = inputs * scale_mix
-    normed = gather_rows((scaled_mix * gain_mix).astype(BF16))
     own_cot = lax.dynamic_slice_in_dim(cotangent[0], place_tp * rows, rows, 0)
-    cot = gather_rows(own_cot)
+    gain_mix, gain_mlp = gain_mix[None], gain_mlp[None]
+    normed, cot = head(tokens[0], cotangent[0], gain_mix, 1)
+    normed, cot = normed.reshape(length, model_width), cot.reshape(length, model_width)
 
     pre = matmul(normed, full_in)
     mixed, states, recur, opened, conv = mixer(pre, masks, params, diag_a, diag_x, place, rows)
-    resid = inputs + reduce_rows(mixed, full_out, matmul)
-    scale_mlp = rms_rows(resid)
-    scaled_mlp = resid * scale_mlp
-    normed_mlp = gather_rows((scaled_mlp * gain_mlp).astype(BF16))
+    normed_mlp, resid = plane_sum("norm", True, mixed, full_out, own, own, gain_mlp, 2, 9 << 33)
+    normed_mlp = normed_mlp.reshape(length, model_width)
 
     both = matmul(normed_mlp, full_gu)
     gate_pre, up_pre = both[:, :units], both[:, units:]
     gate_act, gate_slope = gelu_parts(gate_pre)
     hidden = (gate_act * up_pre).astype(BF16)
     grad_w_down = left_inner(hidden, cot).astype(BF16)
-    output = (resid + reduce_rows(hidden, full_down, matmul)).astype(BF16)
+    full_down, grad_w_down, hidden = tied((full_down, grad_w_down, hidden))
+    own_down = owned(grad_w_down, 1)
 
     grad_hidden = right_inner(cot, full_down)
     grad_both = jnp.concatenate(
@@ -422,56 +748,87 @@
         ],
         axis=1,
     )
-    grad_norm_mlp = reduce_rows(grad_both, full_gu, right_inner)
     grad_w_gu = left_inner(normed_mlp, grad_both).astype(BF16)
-    grad_resid = own_cot.astype(F32) + norm_back(grad_norm_mlp, scaled_mlp, scale_mlp, gain_mlp)
-    gain_mlp_part = jnp.sum(grad_norm_mlp * scaled_mlp, axis=0)
-    grad_proj = gather_rows(grad_resid.astype(BF16))
+    half = length // 2
+    sent = matmul(hidden[half:], full_down).astype(BF16)
+    grad_w_gu, sent = tied((grad_w_gu, sent))
+    own_gu = owned(grad_w_gu, 0)
+    got = exchange(sent, "core")
+    kept = matmul(hidden[:half], full_down)
+    grad_both, kept, got, grad_w_gu = tied((grad_both, kept, got, grad_w_gu))
+    total = kept + got.astype(F32)
+    got_far = exchange(total[half // 2 :].astype(BF16), "far")
+    total = total[: half // 2]
+    grad_both, total = tied((grad_both, total))
+    grad_proj, grad_resid, gain_mlp_part = plane_sum(
+        "back", True, grad_both, full_gu, own_cot, resid, gain_mlp, 3, 9 << 33
+    )
+    grad_proj = grad_proj.reshape(length, model_width)
+    grad_proj, got_far, total = tied((grad_proj, got_far, total))
+    total = total + got_far.astype(F32)
+    got_near = exchange(total[half // 4 :].astype(BF16), "near")
+    total = total[: half // 4]
 
     grad_w_out = left_inner(mixed, grad_proj).astype(BF16)
-    grad_mixed = right_inner(grad_proj, full_out)
+    grad_proj, own_down, grad_w_out = tied((grad_proj, own_down, grad_w_out))
+    own_out = owned(grad_w_out, 1)
+    grad_mixed = matmul(grad_proj, full_out)
+    other_down = flip(own_down, 4)
     grads_in, sums, sum_a, sum_x = mixer_back(
         grad_mixed, pre, states, recur, opened, conv, masks, params, diag_a, diag_x, place, rows
     )
-    grad_w_in = left_inner(normed, grads_in).astype(BF16)
-    grad_norm_mix = reduce_rows(grads_in, full_in, right_inner)
-    gain_mix_part = jnp.sum(grad_norm_mix * scaled_mix, axis=0)
-    grad_tokens = (grad_resid + norm_back(grad_norm_mix, scaled_mix, scale_mix, gain_mix)).astype(BF16)
-
-    def owned(x, axis):
-        return lax.psum_scatter(x, "fsdp", scatter_dimension=axis, tiled=True)
-
-    def both_halves(x, axis):
-        other = flip(x, 4)
+    grads_in, got_near, total, other_down, own_gu = tied((grads_in, got_near, total, other_down, own_gu))
+    output = (resid + total + got_near.astype(F32)).astype(BF16)
+    lines = jnp.sum(sums.reshape(8, 8, width), axis=1)
+    head_at = lax.broadcasted_iota(jnp.int32, (head_width, width), 1) // head_width
+    squares = [
+        sum(
+            jnp.where(head_at == h, part[h * head_width : (h + 1) * head_width], 0.0) for h in range(head_count)
+        )
+        for part in (sum_a, sum_x)
+    ]
+    fsdp_size = lax.axis_size("fsdp")
+    part_rows = 16 * -(-(8 + 2 * head_width) // (16 * fsdp_size))
+    spare = fsdp_size * part_rows - 8 - 2 * head_width
+    small = jnp.concatenate([lines] + squares + [jnp.zeros((spare, width), F32)], axis=0).astype(BF16)
+    small = small.reshape(fsdp_size, 2, part_rows // 2, width)
+    small = jnp.concatenate([small[:, 0], small[:, 1]], axis=2)
+    grad_w_in = left_inner(normed, grads_in).astype(BF16).reshape(fsdp_size, -1, 2 * width)
+    grad_w_in = jnp.concatenate([grad_w_in, small], axis=1).reshape(-1, 2 * width)
+    grads_in, grad_w_in, own_out = tied((grads_in, grad_w_in, own_out))
+    own_in = owned(grad_w_in, 0)
+    grad_tokens, gain_mix_part, output, own_gate, own_up, own_out = plane_sum(
+        "back", False, grads_in, full_in, grad_resid, own, gain_mix, 4, 5 << 33, (output, own_gu, own_out)
+    )
+    gain_mix_part, gain_mlp_part = jnp.sum(gain_mix_part, axis=0), jnp.sum(gain_mlp_part, axis=0)
+
+    def both_halves(x, other, axis):
         low = jnp.where(half_at == 0, x, other)
         high = jnp.where(half_at == 0, other, x)
         return jnp.concatenate([low, high], axis=axis).astype(F32)
 
-    own_down = both_halves(owned(grad_w_down, 1), 0)
-    sum_gu = owned(grad_w_gu, 0)
-    own_gate = both_halves(sum_gu[:, :units], 1)
-    own_up = both_halves(sum_gu[:, units:], 1)
-    own_out = both_halves(owned(grad_w_out, 1), 0)
-    sum_in = owned(grad_w_in, 0)
-    own_branch = both_halves(sum_in[:, :width], 1)
-    own_input = both_halves(sum_in[:, width:], 1)
-
-    lines = jnp.sum(sums.reshape(8, 8, width), axis=1)
-    squares = [
-        part[h * head_width : (h + 1) * head_width, h * head_width : (h + 1) * head_width]
-        for part in (sum_a, sum_x)
-        for h in range(head_count)
-    ]
-    lines = both_halves(sum_fsdp(lines), 1)
-    squares = sum_fsdp(jnp.stack(squares).reshape(2, head_count, head_width, head_width))
-    squares = both_halves(squares, 1)
+    other_in = flip(own_in, 4)
+    small_part = own_in[model_width // fsdp_size :]
+    own_in, other_in = [x[: model_width // fsdp_size] for x in (own_in, other_in)]
+    small = gather_fsdp(jnp.concatenate([small_part[:, :width], small_part[:, width:]], axis=0))
+    other_small = flip(small, 4)
+    own_down = both_halves(own_down, other_down, 0)
+    lines = both_halves(small[:8], other_small[:8], 1)
+    squares = []
+    for i in range(2):
+        part = both_halves(small[8 + i * head_width :][:head_width], other_small[8 + i * head_width :][:head_width], 1)
+        squares.append(
+            jnp.stack([part[:, h * head_width : (h + 1) * head_width] for h in range(2 * head_count)])
+        )
     gains = jnp.stack([gain_mix_part, gain_mlp_part])
     for mask in (1, 2, 4):
         gains = gains + flip(gains, mask)
     gains = sum_fsdp(gains)
+    own_branch = both_halves(own_in[:, :width], other_in[:, :width], 1)
+    own_input = both_halves(own_in[:, width:], other_in[:, width:], 1)
     return (
-        whole_rows(output)[None],
-        whole_rows(grad_tokens)[None],
+        output.reshape(1, tok_count, model_width),
+        grad_tokens.reshape(1, tok_count, model_width),
         gains[0],
         own_branch,
         own_input,
@@ -482,10 +839,10 @@
         squares[1],
         lines[2],
         RATE_SCALE * jax.nn.sigmoid(-decay_param) * lines[0],
-        own_out,
+        own_out.astype(F32),
         gains[1],
-        own_gate,
-        own_up,
+        own_gate.astype(F32),
+        own_up.astype(F32),
         own_down,
     )
 

time: 825 us -> 678 us (0.82)
  Pallas kernels: 46.6 us -> 411 us
  waiting for transfers between devices: 386 us -> 33.6 us
  other arithmetic: 106 us -> 44.2 us
  matrix products: 168 us -> 113 us
  starting transfers between devices: 46.6 us -> 14 us
    pallas_call x0 -> x4, Pallas kernels: none -> 364 us  [the longest x3 284 us: plane_sum(): pl.pallas_call(functools.partial(plane_sum_kernel, epilogue, wide), in_sp...]
    ppermute x24 -> x3, waiting for transfers between devices: 236 us -> 0.01 us  [exchange(): return lax.ppermute(block, GROUP, pairs)]
    ppermute x6 -> x2, waiting for transfers between devices: 49.5 us -> 0.01 us  [sum_fsdp(): x = x + lax.ppermute(x, 'fsdp', [(i, i ^ bit) for i in range(size)])]
    dot_general x6 -> x1, matrix products: 64.3 us -> 15.9 us  [right_inner(): lax.dot_general(left, right, (((1,), (1,)), ((), ())), preferred_element_...]
    ppermute x15 -> x6, waiting for transfers between devices: 57.2 us -> 22 us  [flip(): return lax.ppermute(block, GROUP, [(g, g ^ mask) for g in range(8)])]
    add x8 -> x2, other arithmetic: 37.9 us -> 9.46 us  [the longest x1 5.84 us: shards(): total = kept + got.astype(F32)]
    ppermute x24 -> x3, starting transfers between devices: 24.5 us -> 2.05 us  [exchange(): return lax.ppermute(block, GROUP, pairs)]
    all_gather x2 -> x1, waiting for transfers between devices: 18 us -> 0.01 us  [shards(): full_mix = lax.all_gather(own_in, 'fsdp', axis=0, tiled=True)]
  transfers between devices with their start and end apart: 53 -> 20, of which waited for: 28 -> 6; matrix products, arithmetic and copies ran while one was open for 32% -> 27% of each run, Pallas kernels for 6% -> 61%
where the time goes in v2:
time: 678 us; the launch traced here: 675 us
  Pallas kernels  411 us (61%)
  matrix products  113 us (17%)
  other arithmetic  44.2 us (7%)
  local copies, waits for them, and re-layouts  43.8 us (6%)
  waiting for transfers between devices  33.6 us (5%)
  between operations  15.1 us (2%)
  starting transfers between devices  14 us (2%)
    pallas_call x3, Pallas kernels, plane_sum(): pl.pallas_call(functools.partial(plane_sum_kernel, epilogue, wide), in_sp...  284 us
    pallas_call x1, Pallas kernels, head(): pl.pallas_call(head_kernel, in_specs=[anywhere, anywhere, pl.BlockSpec(me...  79.9 us
    dot_general x5, matrix products, matmul(): return jnp.dot(left, right, preferred_element_type=F32)  54.8 us
    dot_general x4, matrix products, left_inner(): lax.dot_general(left, right, (((0,), (0,)), ((), ())), preferred_element_...  42.5 us
    pallas_call x1, Pallas kernels, mixer_back(): pl.pallas_call(mixer_back_kernel, grid_spec=pltpu.PrefetchScalarGridSpec(...  27.4 us
    ppermute x6, waiting for transfers between devices, flip(): return lax.ppermute(block, GROUP, [(g, g ^ mask) for g in range(8)])  22 us
    pallas_call x1, Pallas kernels, mixer(): pl.pallas_call(mixer_kernel, grid_spec=pltpu.PrefetchScalarGridSpec(num_s...  19 us
    dot_general x1, matrix products, right_inner(): lax.dot_general(left, right, (((1,), (1,)), ((), ())), preferred_element_...  15.9 us
  transfers between devices with their start and end apart: 20, of which 6 were waited for; matrix products, arithmetic and copies ran while one was open for 27% of the time, Pallas kernels for 61%

profile of v2, /device:TPU:0, one launch (start us, length us, event | category | flops | bytes accessed | tf_op | source)
XLA Modules:
  0.0 674.7 jit_solution(17202073740540667223)
XLA Ops:
  8.6 1.7 constant_dynamic-slice_fusion.4
  19.0 1.8 dynamic_update_slice.13.gate_a
  20.7 1.6 dynamic_update_slice.15.gate_x
  22.4 2.5 dynamic-slice_bitcast_fusion.1.base.source
  24.8 79.9 %head.1 = (bf16[8,256,2048]{2,1,0:T(8,128)(2,1)}, bf16[8,256,2048]{2,1,0:T(8,128)(2,1)}) custom-call(bf16[1024,2048]{1,0:T(8,128)(2,1)} %bitcast.78, bf16[1024,2048]{1,0:T(8,128)(2,1)} %bitcast.79, f32[1,2048]{1,0:T(1,128)} %bitcast.91), custom_call_target="tpu_custom_call" | custom-call | flops 42949672960 | bytes 67108864 | tf_op jit(solution)/shard_map/head/pallas_call | solution.py:209
  105.4 11.8 %fusion.37.pre.pre_tail = f32[2048,640]{1,0:T(8,128)} fusion(bf16[2048,2048]{1,0:T(8,128)(2,1)} %bitcast.93, bf16[2048,960]{1,0:T(8,128)(2,1)} %all-gather.6.cloned.1.call-done), kind=kOutput, calls=%fused_computation.130 | convolution fusion | flops 5368709120 | bytes 16252928 | tf_op jit(solution)/shard_map/dot_general | solution.py:20
  117.2 19.0 %mixer.1 = (bf16[2048,320]{1,0:T(8,128)(2,1)}, f32[2048,320]{1,0:T(8,128)}, f32[2048,320]{1,0:T(8,128)}, f32[2048,320]{1,0:T(8,128)}, bf16[2048,320]{1,0:T(8,128)(2,1)}) custom-call(s32[8]{0:T(128)} %fusion.33.place, f32[2048,640]{1,0:T(8,128)} %fusion.37.pre.pre_tail, f32[2048,8]{1,0:T(8,128)} %convert_element_type.73.masks, f32[8,320]{1,0:T(8,128)} %concatenate.50.params, ...), custom_call_target="tpu_custom_call" | custom-call | flops 917504000 | bytes 15728640 | tf_op jit(solution)/shard_map/mixer/pallas_call | solution.py:601
  136.2 2.7 slice.233.right
  138.9 89.9 %plane_sum.3 = (bf16[8,256,2048]{2,1,0:T(8,128)(2,1)}, f32[256,2048]{1,0:T(8,128)}) custom-call(bf16[2048,320]{1,0:T(8,128)(2,1)} %get-tuple-element.65.left, bf16[2048,320]{1,0:T(8,128)(2,1)} %slice.233.right, bf16[256,2048]{1,0:T(8,128)(2,1)} %dynamic-slice_bitcast_fusion.1.base.source, bf16[256,2048]{1,0:T(8,128)(2,1)} %dynamic-slice_bitcast_fusion.1.base.source, ...), custom_call_target="tpu_custom_call" | custom-call | flops 77309411328 | bytes 4194304 | tf_op jit(solution)/shard_map/plane_sum/pallas_call | solution.py:407
  228.8 17.4 %fusion.41 = f32[2048,1536]{1,0:T(8,128)S(1)} fusion(bf16[2048,2048]{1,0:T(8,128)(2,1)} %bitcast.99, bf16[2048,1536]{1,0:T(8,128)(2,1)} %all-gather.8.cloned.1.call-done.right), kind=kOutput, calls=%fused_computation.134 | convolution fusion | flops 12884901888 | bytes 27262976 | tf_op jit(solution)/shard_map/dot_general | solution.py:20
  246.3 2.6 multiply_convert_fusion.1
  248.9 1.9 copy-done.2
  250.9 1.7 copy-done.9
  252.6 10.5 %convolution_convert_fusion.2 = bf16[768,2048]{1,0:T(8,128)(2,1)} fusion(bf16[2048,768]{1,0:T(8,128)(2,1)S(1)} %multiply_convert_fusion.1, bf16[2048,2048]{1,0:T(8,128)(2,1)} %bitcast.95), kind=kOutput, calls=%fused_computation.22 | convolution fusion | flops 6444023808 | bytes 14680064 | tf_op jit(solution)/shard_map/dot_general | solution.py:24
  263.0 11.3 %all-gather.4.cloned.1.call-done = bf16[768,2048]{1,0:T(8,128)(2,1)} async-done(((bf16[768,512]{1,0:T(8,128)(2,1)}), bf16[768,2048]{1,0:T(8,128)(2,1)}) %all-gather.4.cloned.1.call-update) | async-done | bytes 3145744 | tf_op jit(solution)/shard_map/all_gather | solution.py:699
  274.4 7.9 %convolution_convert_fusion.1 = bf16[1024,2048]{1,0:T(8,128)(2,1)} fusion(bf16[768,2048]{1,0:T(8,128)(2,1)} %all-gather.4.cloned.1.call-done, bf16[2048,768]{1,0:T(8,128)(2,1)} %copy-done.9), kind=kOutput, calls=%fused_computation.21 | convolution fusion | flops 3223322624 | bytes 8912896 | tf_op jit(solution)/shard_map/dot_general | solution.py:20
  282.4 15.9 %fusion.9 = (bf16[2048,768]{1,0:T(8,128)(2,1)S(1)}, bf16[2048,768]{1,0:T(8,128)(2,1)S(1)}) fusion(f32[2048,1536]{1,0:T(8,128)} %copy-done.2, bf16[2048,2048]{1,0:T(8,128)(2,1)} %bitcast.96, bf16[768,2048]{1,0:T(8,128)(2,1)S(1)} %copy-done.28), kind=kOutput, calls=%fused_computation.13 | convolution fusion | flops 6478626816 | bytes 30408704 | tf_op jit(solution)/shard_map/dot_general | solution.py:28
  298.3 1.6 copy-done.5
  300.9 17.7 %convolution_convert_fusion = bf16[2048,1536]{1,0:T(8,128)(2,1)} fusion(bf16[2048,2048]{1,0:T(8,128)(2,1)} %bitcast.100, bf16[2048,768]{1,0:T(8,128)(2,1)S(1)} %get-tuple-element.114, bf16[2048,768]{1,0:T(8,128)(2,1)S(1)} %get-tuple-element.113), kind=kOutput, calls=%fused_computation.3 | convolution fusion | flops 12900630528 | bytes 20971520 | tf_op jit(solution)/shard_map/dot_general | solution.py:24
  318.9 2.5 dynamic-slice_bitcast_fusion.base
  321.3 3.5 slice.232.right
  324.8 3.1 pad_maximum_fusion.left
  327.9 7.7 %fusion.12 = f32[1024,2048]{1,0:T(8,128)} fusion(bf16[768,2048]{1,0:T(8,128)(2,1)} %all-gather.4.cloned.1.call-done, bf16[2048,768]{1,0:T(8,128)(2,1)S(1)} %copy-done.10), kind=kOutput, calls=%fused_computation.31 | convolution fusion | flops 3221225472 | bytes 13107200 | tf_op jit(solution)/shard_map/dot_general | solution.py:20
  335.6 5.8 convert_add_fusion
  341.4 2.3 slice.236
  343.7 1.6 slice.353
  346.9 104.6 %plane_sum.4 = (bf16[8,256,2048]{2,1,0:T(8,128)(2,1)}, f32[256,2048]{1,0:T(8,128)}, f32[8,2048]{1,0:T(8,128)}) custom-call(bf16[2048,1536]{1,0:T(8,128)(2,1)} %pad_maximum_fusion.left, bf16[2048,1536]{1,0:T(8,128)(2,1)} %all-gather.8.cloned.1.call-done.right, bf16[256,2048]{1,0:T(8,128)(2,1)} %dynamic-slice_bitcast_fusion.base, ...), custom_call_target="tpu_custom_call" | custom-call | flops 77309411328 | bytes 4194304 | tf_op jit(solution)/shard_map/plane_sum/pallas_call | solution.py:407
  452.3 3.6 convert_add_fusion.1
  458.9 4.1 convolution_convert_fusion.4
  463.9 10.0 %fusion.35.grad_mixed = f32[2048,320]{1,0:T(8,128)} fusion(bf16[2048,2048]{1,0:T(8,128)(2,1)} %bitcast.97, bf16[2048,960]{1,0:T(8,128)(2,1)} %all-gather.6.cloned.1.call-done), kind=kOutput, calls=%fused_computation.128 | convolution fusion | flops 2684354560 | bytes 12582912 | tf_op jit(solution)/shard_map/dot_general | solution.py:20
  473.9 27.4 %mixer_back.1 = (bf16[2048,640]{1,0:T(8,128)(2,1)}, f32[64,320]{1,0:T(8,128)}, f32[320,320]{1,0:T(8,128)}, f32[320,320]{1,0:T(8,128)}) custom-call(s32[8]{0:T(128)} %fusion.33.place, f32[2048,320]{1,0:T(8,128)} %fusion.35.grad_mixed, f32[2048,640]{1,0:T(8,128)} %fusion.37.pre.pre_tail, f32[2048,640]{1,0:T(8,128)} %fusion.37.pre.pre_tail, ...), custom_call_target="tpu_custom_call" | custom-call | flops 1808793600 | bytes 22282240 | tf_op jit(solution)/shard_map/mixer_back/pallas_call | solution.py:639
  503.8 10.2 %convolution_convert_fusion.3 = bf16[2048,640]{1,0:T(8,128)(2,1)S(1)} fusion(bf16[2048,2048]{1,0:T(8,128)(2,1)} %bitcast.94, bf16[2048,640]{1,0:T(8,128)(2,1)} %get-tuple-element.94.left), kind=kOutput, calls=%fused_computation.23 | convolution fusion | flops 5370019840 | bytes 13631488 | tf_op jit(solution)/shard_map/dot_general | solution.py:24
  514.1 1.9 maximum_maximum_fusion
  516.0 3.7 add_convert_fusion.refs_0_
  519.7 90.1 %plane_sum.5 = (bf16[4,256,2048]{2,1,0:T(8,128)(2,1)}, f32[8,2048]{1,0:T(8,128)}, bf16[4,256,2048]{2,1,0:T(8,128)(2,1)}, bf16[512,1536]{1,0:T(8,128)(2,1)}, bf16...) custom-call(bf16[2048,640]{1,0:T(8,128)(2,1)} %get-tuple-element.94.left, bf16[2048,640]{1,0:T(8,128)(2,1)} %slice.232.right, ...), custom_call_target="tpu_custom_call" | custom-call | flops 42949672960 | bytes 4194304 | tf_op jit(solution)/shard_map/plane_sum/pallas_call | solution.py:407
  610.6 3.2 collective-permute-start.4
  614.8 3.6 collective-permute-done.5
  618.8 3.5 collective-permute-done.6
  623.4 2.0 collective-permute-start.10
  628.5 1.6 collective-permute-start.11
  630.1 2.1 maximum_convert_fusion
  633.4 2.1 convert_element_type.93
  635.5 2.1 convert_element_type.94
  638.6 1.8 collective-permute-start.9
  640.4 7.2 %collective-permute-done.12 = bf16[384,320]{1,0:T(8,128)(2,1)S(1)} collective-permute-done((bf16[384,320]{1,0:T(8,128)(2,1)S(1)}, bf16[384,320]{1,0:T(8,128)(2,1)S(1)}, u32[]{:S(2)}, u32[]{:S(2)}) %collective-permute-start.12) | collective-permute-done | bytes 245792 | tf_op jit(solution)/shard_map/ppermute | solution.py:73
  652.1 6.8 %collective-permute-done.9 = bf16[560,640]{1,0:T(8,128)(2,1)S(1)} collective-permute-done((bf16[560,640]{1,0:T(8,128)(2,1)S(1)}, bf16[560,640]{1,0:T(8,128)(2,1)S(1)}, u32[]{:S(2)}, u32[]{:S(2)}) %collective-permute-start.9) | collective-permute-done | bytes 716832 | tf_op jit(solution)/shard_map/ppermute | solution.py:73
  661.9 2.1 copy.73
  665.6 2.0 copy.74
  (171 shorter events, 38.0 us)
Async XLA Ops:
  7.2 7.1 %copy-start = (bf16[1536,512]{1,0:T(8,128)(2,1)S(1)}, bf16[1536,512]{1,0:T(8,128)(2,1)}, u32[]{:S(2)}) copy-start(bf16[1536,512]{1,0:T(8,128)(2,1)} %param.36) | copy-start | bytes 4718596
  7.2 98.2 %all-gather.6.cloned.1.call-start = ((), (), s32[]{:S(2)}) async-start(), calls=%async_computation.5 | async-start | bytes 5242880 | tf_op jit(solution)/shard_map/all_gather | solution.py:696
  8.6 3.0 copy-start.18
  11.6 217.3 %all-gather.8.cloned.1.call-start = ((), (), s32[]{:S(2)}) async-start(), calls=%async_computation.6 | async-start | bytes 7864320 | tf_op jit(solution)/shard_map/all_gather | solution.py:698
  12.9 4.3 copy-start.24
  12.9 4.4 copy-start.25
  12.9 4.4 copy-start.26
  12.9 4.5 copy-start.27
  12.9 4.6 copy-start.21
  12.9 4.7 copy-start.19
  13.0 4.7 copy-start.20
  14.3 260.1 %all-gather.4.cloned.1.call-start = ((), (), s32[]{:S(2)}) async-start(), calls=%async_computation.4 | async-start | bytes 3932160 | tf_op jit(solution)/shard_map/all_gather | solution.py:699
  15.3 447.8 %reduce-scatter.5.cloned.1.call-start = ((), (), s32[]{:S(2)}) async-start(), calls=%async_computation.7 | async-start | bytes 3932160 | tf_op jit(solution)/shard_map/reduce_scatter | solution.py:690
  20.7 84.0 %copy-start.15 = (bf16[320,320]{1,0:T(8,128)(2,1)}, bf16[320,320]{1,0:T(8,128)(2,1)S(1)}, u32[]{:S(2)}) copy-start(bf16[320,320]{1,0:T(8,128)(2,1)S(1)} %dynamic_update_slice.13.gate_a) | copy-start | bytes 614404
  22.4 82.4 %copy-start.14 = (bf16[320,320]{1,0:T(8,128)(2,1)}, bf16[320,320]{1,0:T(8,128)(2,1)S(1)}, u32[]{:S(2)}) copy-start(bf16[320,320]{1,0:T(8,128)(2,1)S(1)} %dynamic_update_slice.15.gate_x) | copy-start | bytes 614404
  246.3 4.6 copy-start.2
  274.4 229.4 %reduce-scatter.7.cloned.1.call-start = ((), (), s32[]{:S(2)}) async-start(), calls=%async_computation.8 | async-start | bytes 7864320 | tf_op jit(solution)/shard_map/reduce_scatter | solution.py:690
  274.4 8.0 %copy-start.28 = (bf16[768,2048]{1,0:T(8,128)(2,1)S(1)}, bf16[768,2048]{1,0:T(8,128)(2,1)}, u32[]{:S(2)}) copy-start(bf16[768,2048]{1,0:T(8,128)(2,1)} %all-gather.4.cloned.1.call-done) | copy-start | bytes 9437188
  298.2 2.7 copy-start.7
  318.7 16.9 %collective-permute-start = (bf16[1024,2048]{1,0:T(8,128)(2,1)}, bf16[1024,2048]{1,0:T(8,128)(2,1)}, u32[]{:S(2)}, u32[]{:S(2)}) collective-permute-start(bf16[1024,2048]{1,0:T(8,128)(2,1)} %convolution_convert_fusion.1), channel_id=1, source_target_pairs={{0,1},{1,0},{2,3},{3,2},{4,5},{5,4},{6,7},{7,6},{8,9},{9,8},{10,11... | collective-permute-start | bytes 12582920 | tf_op jit(solution)/shard_map/ppermute | solution.py:69
  318.7 197.2 %reduce-scatter.9.cloned.1.call-start = ((), (), s32[]{:S(2)}) async-start(), calls=%async_computation.9 | async-start | bytes 1638400 | tf_op jit(solution)/shard_map/reduce_scatter | solution.py:690
  318.7 6.1 copy-start.6
  318.8 6.1 copy-start.8
  324.8 3.1 copy-start.10
  345.4 106.9 %collective-permute-start.1 = (bf16[512,2048]{1,0:T(8,128)(2,1)}, bf16[512,2048]{1,0:T(8,128)(2,1)}, u32[]{:S(2)}, u32[]{:S(2)}) collective-permute-start(bf16[512,2048]{1,0:T(8,128)(2,1)} %slice.353), channel_id=1, source_target_pairs={{0,4},{1,3},{2,6},{3,1},{4,0},{5,7},{6,2},{7,5},{8,12},{9,11},{10,... | collective-permute-start | bytes 6291464 | tf_op jit(solution)/shard_map/ppermute | solution.py:69
  452.3 5.9 copy-start.29
  455.9 3.0 copy-start.30
  457.6 46.1 %collective-permute-start.2 = (bf16[256,2048]{1,0:T(8,128)(2,1)S(1)}, bf16[256,2048]{1,0:T(8,128)(2,1)S(1)}, u32[]{:S(2)}, u32[]{:S(2)}) collective-permute-start(bf16[256,2048]{1,0:T(8,128)(2,1)S(1)} %slice.354), channel_id=1, source_target_pairs={{0,2},{1,5},{2,0},{3,7},{4,6},{5,1},{6,4},{7,3},{8,10},{9,13},{10,... | collective-permute-start | bytes 3145736 | tf_op jit(solution)/shard_map/ppermute | solution.py:69
  463.1 40.7 %collective-permute-start.3 = (bf16[768,512]{1,0:T(8,128)(2,1)}, bf16[768,512]{1,0:T(8,128)(2,1)S(1)}, u32[]{:S(2)}, u32[]{:S(2)}) collective-permute-start(bf16[768,512]{1,0:T(8,128)(2,1)} %reduce-scatter.5.cloned.1.call-done), channel_id=1, source_target_pairs={{0,4},{1,5},{2,6},{3,7},{4,0},{5,1},{6,2},{7,3},{8,12},{9,13},{10,... | collective-permute-start | bytes 2359304 | tf_op jit(solution)/shard_map/ppermute | solution.py:73
  463.6 158.8 %reduce-scatter.11.cloned.1.call-start = ((), (), s32[]{:S(2)}) async-start(), calls=%async_computation.10 | async-start | bytes 3584000 | tf_op jit(solution)/shard_map/reduce_scatter | solution.py:690
  503.7 10.3 %copy-start.16 = (bf16[768,512]{1,0:T(8,128)(2,1)}, bf16[768,512]{1,0:T(8,128)(2,1)S(1)}, u32[]{:S(2)}) copy-start(bf16[768,512]{1,0:T(8,128)(2,1)S(1)} %collective-permute-done.3) | copy-start | bytes 2359300
  610.6 4.0 collective-permute-start.4
  614.7 3.8 collective-permute-start.5
  618.5 3.8 collective-permute-start.6
  622.3 4.6 collective-permute-start.7
  623.4 8.8 %copy-start.17 = (bf16[640,512]{1,0:T(8,128)(2,1)S(1)}, bf16[640,512]{1,0:T(8,128)(2,1)}, u32[]{:S(2)}) copy-start(bf16[640,512]{1,0:T(8,128)(2,1)} %get-tuple-element.105) | copy-start | bytes 1966084
  623.4 5.1 collective-permute-start.10
  626.9 6.5 copy-start.12
  626.9 10.6 %collective-permute-start.8 = (f32[2,2048]{1,0:T(2,128)S(1)}, f32[2,2048]{1,0:T(2,128)S(1)}, u32[]{:S(2)}, u32[]{:S(2)}) collective-permute-start(f32[2,2048]{1,0:T(2,128)S(1)} %add.126), channel_id=1, source_target_pairs={{0,16},{8,24},{16,0},{24,8},{1,17},{9,25},{17,1},{25,9},{2,18},{10... | collective-permute-start | bytes 49160 | tf_op jit(solution)/shard_map/ppermute | solution.py:442
  628.5 9.1 %collective-permute-start.11 = (bf16[192,320]{1,0:T(8,128)(2,1)S(1)}, bf16[192,320]{1,0:T(8,128)(2,1)S(1)}, u32[]{:S(2)}, u32[]{:S(2)}) collective-permute-start(bf16[192,320]{1,0:T(8,128)(2,1)S(1)} %pad_maximum_fusion.6), channel_id=1, source_target_pairs={{0,16},{8,24},{16,0},{24,8},{1,17},{9,25},{17,1},{25,9},{2,18},{10... | collective-permute-start | bytes 368648 | tf_op jit(solution)/shard_map/ppermute | solution.py:451
  632.2 3.3 copy-start.11
  633.4 5.2 copy-start.13
  637.6 13.9 %copy-start.22 = (f32[640]{0:T(1024)S(1)}, f32[640]{0:T(1024)}, u32[]{:S(2)}) copy-start(f32[640]{0:T(1024)} %param.31) | copy-start | bytes 7684
  637.7 9.9 %collective-permute-start.12 = (bf16[384,320]{1,0:T(8,128)(2,1)S(1)}, bf16[384,320]{1,0:T(8,128)(2,1)S(1)}, u32[]{:S(2)}, u32[]{:S(2)}) collective-permute-start(bf16[384,320]{1,0:T(8,128)(2,1)S(1)} %pad_maximum_fusion.5), channel_id=1, source_target_pairs={{0,4},{1,5},{2,6},{3,7},{4,0},{5,1},{6,2},{7,3},{8,12},{9,13},{10,... | collective-permute-start | bytes 737288 | tf_op jit(solution)/shard_map/ppermute | solution.py:73
  638.6 20.3 %collective-permute-start.9 = (bf16[560,640]{1,0:T(8,128)(2,1)S(1)}, bf16[560,640]{1,0:T(8,128)(2,1)S(1)}, u32[]{:S(2)}, u32[]{:S(2)}) collective-permute-start(bf16[560,640]{1,0:T(8,128)(2,1)S(1)} %copy-done.13), channel_id=1, source_target_pairs={{0,4},{1,5},{2,6},{3,7},{4,0},{5,1},{6,2},{7,3},{8,12},{9,13},{10,... | collective-permute-start | bytes 2150408 | tf_op jit(solution)/shard_map/ppermute | solution.py:73
  650.6 11.3 %copy-start.4 = (bf16[4,256,2048]{2,1,0:T(8,128)(2,1)S(1)}, bf16[4,256,2048]{2,1,0:T(8,128)(2,1)}, u32[]{:S(2)}) copy-start(bf16[4,256,2048]{2,1,0:T(8,128)(2,1)} %get-tuple-element.100) | copy-start | bytes 12582916
  661.9 3.7 copy-start.3
  661.9 5.7 copy-start.1
  (3 other events, 5.8 us)
Sparse Core Ops, SparseCore 0:
  11.7 83.3 all-gather.5
  97.2 113.8 all-gather.7
  212.7 61.6 all-gather.3
  276.5 59.0 reduce-scatter.4
  337.7 110.6 reduce-scatter.6
  463.8 29.6 reduce-scatter.8
  516.1 54.5 reduce-scatter.10

commit v3 on v2

--- a/solution.py
+++ b/solution.py
@@ -14,6 +14,7 @@
 GELU_K = 0.044715
 GROUP = ("ctx", "tp")
 F32, BF16 = jnp.float32, jnp.bfloat16
+tied = lax.optimization_barrier
 
 
 def matmul(left, right):
@@ -432,27 +433,88 @@
     )(left, right, base, source, gain, *extra_in)
 
 
-tied = lax.optimization_barrier
-
-
-def sum_fsdp(x):
-    size = lax.axis_size("fsdp")
-    bit = 1
-    while bit < size:
-        x = x + lax.ppermute(x, "fsdp", [(i, i ^ bit) for i in range(size)])
-        bit *= 2
-    return x
-
-
-def gather_fsdp(x):
-    size, at = lax.axis_size("fsdp"), lax.axis_index("fsdp")
-    bit = 1
-    while bit < size:
-        other = lax.ppermute(x, "fsdp", [(i, i ^ bit) for i in range(size)])
-        later = (at // bit) % 2 == 1
-        x = jnp.concatenate([jnp.where(later, other, x), jnp.where(later, x, other)], axis=0)
-        bit *= 2
-    return x
+def last_kernel(
+    size, deep, own_in, gain_a, gain_b, smalls, gains, plane, mine, lines, store, small_send, small_recv, plane_send,
+    plane_recv, line_send, line_recv,
+):
+    thin = smalls.shape[2]
+    fsdp, ctx, tp = lax.axis_index("fsdp"), lax.axis_index("ctx"), lax.axis_index("tp")
+
+    def away(dz, dc, dt):
+        return (lax.rem(fsdp + dz, size), lax.rem(ctx + dc, 2), lax.rem(tp + dt, 4))
+
+    in_plane = [(0, dc, dt) for dc in range(2) for dt in range(4)][1:]
+    across_line = [(dz, dc, 0) for dz in range(size) for dc in range(2)][1:]
+    along_line = [(dz, 0, 0) for dz in range(1, size)]
+    meet(*[away(*d) for d in in_plane + [d for d in across_line if d not in in_plane]])
+    copies = []
+    at = lax.broadcasted_iota(jnp.int32, gains.shape, 0)
+    sum_a = jnp.sum(gain_a[...], axis=0, keepdims=True)
+    sum_b = jnp.sum(gain_b[...], axis=0, keepdims=True)
+    place = ctx * 4 + tp
+    plane[place] = jnp.where(at == 0, sum_a, jnp.where(at == 1, sum_b, 0.0))
+    sent = [
+        remote(plane.at[place], plane.at[place], plane_send.at[i], plane_recv.at[i], away(*d))
+        for i, d in enumerate(in_plane)
+    ]
+    for copy in sent:
+        copy.start()
+    thin_rows = own_in.at[pl.ds(deep, thin), :]
+    local = pltpu.make_async_copy(thin_rows, smalls.at[ctx, fsdp], store.at[0])
+    local.start()
+    for i, d in enumerate(across_line):
+        copies.append(remote(thin_rows, smalls.at[ctx, fsdp], small_send.at[i], small_recv.at[i], away(*d)))
+        copies[-1].start()
+    for copy in sent:
+        copy.wait_recv()
+    total = plane[0]
+    for i in range(1, 8):
+        total = total + plane[i]
+    mine[...] = total
+    lines[fsdp] = total
+    further = [
+        remote(mine, lines.at[fsdp], line_send.at[i], line_recv.at[i], away(*d)) for i, d in enumerate(along_line)
+    ]
+    for copy in further:
+        copy.start()
+    for copy in further:
+        copy.wait_recv()
+    total = lines[0]
+    for i in range(1, size):
+        total = total + lines[i]
+    gains[...] = total
+    for copy in copies:
+        copy.wait_recv()
+    for copy in copies + sent + further:
+        copy.wait_send()
+    local.wait()
+
+
+def last(own_in, gain_a, gain_b, deep, size, collective_id):
+    width, thin = own_in.shape[1], own_in.shape[0] - deep
+    vmem = pl.BlockSpec(memory_space=pltpu.VMEM)
+    anywhere = pl.BlockSpec(memory_space=pl.ANY)
+    sems = [pltpu.SemaphoreType.DMA((n,)) for n in (1, 2 * size, 2 * size, 8, 8, size, size)]
+    return pl.pallas_call(
+        functools.partial(last_kernel, size, deep),
+        in_specs=[anywhere, vmem, vmem],
+        out_specs=[anywhere, vmem],
+        out_shape=[
+            jax.ShapeDtypeStruct((2, size, thin, width), BF16),
+            jax.ShapeDtypeStruct(gain_a.shape, F32),
+        ],
+        scratch_shapes=[
+            pltpu.VMEM((8,) + gain_a.shape, F32),
+            pltpu.VMEM(gain_a.shape, F32),
+            pltpu.VMEM((size,) + gain_a.shape, F32),
+        ]
+        + sems,
+        compiler_params=pltpu.CompilerParams(
+            collective_id=collective_id, has_side_effects=True, vmem_limit_bytes=32 << 20
+        ),
+        cost_estimate=pl.CostEstimate(flops=1 << 33, bytes_accessed=4 << 20, transcendentals=0),
+        name="last",
+    )(own_in, gain_a, gain_b)
 
 
 def scan_rows(a_ref, b_ref, carry, reverse):
@@ -737,7 +799,7 @@
     gate_act, gate_slope = gelu_parts(gate_pre)
     hidden = (gate_act * up_pre).astype(BF16)
     grad_w_down = left_inner(hidden, cot).astype(BF16)
-    full_down, grad_w_down, hidden = tied((full_down, grad_w_down, hidden))
+    full_down, grad_w_down, hidden, full_in, own_cot = tied((full_down, grad_w_down, hidden, full_in, own_cot))
     own_down = owned(grad_w_down, 1)
 
     grad_hidden = right_inner(cot, full_down)
@@ -754,20 +816,18 @@
     grad_w_gu, sent = tied((grad_w_gu, sent))
     own_gu = owned(grad_w_gu, 0)
     got = exchange(sent, "core")
-    kept = matmul(hidden[:half], full_down)
-    grad_both, kept, got, grad_w_gu = tied((grad_both, kept, got, grad_w_gu))
-    total = kept + got.astype(F32)
-    got_far = exchange(total[half // 2 :].astype(BF16), "far")
-    total = total[: half // 2]
-    grad_both, total = tied((grad_both, total))
+    grad_both, got, grad_w_gu = tied((grad_both, got, grad_w_gu))
+    far_sent = (matmul(hidden[half // 2 : half], full_down) + got[half // 2 :].astype(F32)).astype(BF16)
+    got_far = exchange(far_sent, "far")
+    low = matmul(hidden[: half // 2], full_down) + got[: half // 2].astype(F32)
+    grad_both, low, far_sent = tied((grad_both, low, far_sent))
     grad_proj, grad_resid, gain_mlp_part = plane_sum(
         "back", True, grad_both, full_gu, own_cot, resid, gain_mlp, 3, 9 << 33
     )
     grad_proj = grad_proj.reshape(length, model_width)
-    grad_proj, got_far, total = tied((grad_proj, got_far, total))
-    total = total + got_far.astype(F32)
-    got_near = exchange(total[half // 4 :].astype(BF16), "near")
-    total = total[: half // 4]
+    grad_proj, got_far, low = tied((grad_proj, got_far, low))
+    near_sent = (low[rows:] + got_far[rows:].astype(F32)).astype(BF16)
+    got_near = exchange(near_sent, "near")
 
     grad_w_out = left_inner(mixed, grad_proj).astype(BF16)
     grad_proj, own_down, grad_w_out = tied((grad_proj, own_down, grad_w_out))
@@ -777,8 +837,8 @@
     grads_in, sums, sum_a, sum_x = mixer_back(
         grad_mixed, pre, states, recur, opened, conv, masks, params, diag_a, diag_x, place, rows
     )
-    grads_in, got_near, total, other_down, own_gu = tied((grads_in, got_near, total, other_down, own_gu))
-    output = (resid + total + got_near.astype(F32)).astype(BF16)
+    grads_in, got_near, other_down, own_gu = tied((grads_in, got_near, other_down, own_gu))
+    output = (resid + low[:rows] + got_far[:rows].astype(F32) + got_near.astype(F32)).astype(BF16)
     lines = jnp.sum(sums.reshape(8, 8, width), axis=1)
     head_at = lax.broadcasted_iota(jnp.int32, (head_width, width), 1) // head_width
     squares = [
@@ -800,30 +860,27 @@
     grad_tokens, gain_mix_part, output, own_gate, own_up, own_out = plane_sum(
         "back", False, grads_in, full_in, grad_resid, own, gain_mix, 4, 5 << 33, (output, own_gu, own_out)
     )
-    gain_mix_part, gain_mlp_part = jnp.sum(gain_mix_part, axis=0), jnp.sum(gain_mlp_part, axis=0)
+    own_in, own_gate, own_up, own_out, own_down = tied((own_in, own_gate, own_up, own_out, own_down))
+    other_in = flip(own_in, 4)
+    own_in, other_in = tied((own_in, other_in))
+    smalls, gains = last(own_in, gain_mix_part, gain_mlp_part, model_width // fsdp_size, fsdp_size, 5)
 
     def both_halves(x, other, axis):
         low = jnp.where(half_at == 0, x, other)
         high = jnp.where(half_at == 0, other, x)
         return jnp.concatenate([low, high], axis=axis).astype(F32)
 
-    other_in = flip(own_in, 4)
-    small_part = own_in[model_width // fsdp_size :]
     own_in, other_in = [x[: model_width // fsdp_size] for x in (own_in, other_in)]
-    small = gather_fsdp(jnp.concatenate([small_part[:, :width], small_part[:, width:]], axis=0))
-    other_small = flip(small, 4)
     own_down = both_halves(own_down, other_down, 0)
-    lines = both_halves(small[:8], other_small[:8], 1)
+    smalls = jnp.stack([smalls[..., :width], smalls[..., width:]], axis=2).reshape(2, fsdp_size * part_rows, width)
+    smalls = jnp.concatenate([smalls[0], smalls[1]], axis=1).astype(F32)
+    lines = smalls[:8]
     squares = []
     for i in range(2):
-        part = both_halves(small[8 + i * head_width :][:head_width], other_small[8 + i * head_width :][:head_width], 1)
+        part = smalls[8 + i * head_width : 8 + (i + 1) * head_width]
         squares.append(
             jnp.stack([part[:, h * head_width : (h + 1) * head_width] for h in range(2 * head_count)])
         )
-    gains = jnp.stack([gain_mix_part, gain_mlp_part])
-    for mask in (1, 2, 4):
-        gains = gains + flip(gains, mask)
-    gains = sum_fsdp(gains)
     own_branch = both_halves(own_in[:, :width], other_in[:, :width], 1)
     own_input = both_halves(own_in[:, width:], other_in[:, width:], 1)
     return (

time: 678 us -> 657 us (0.969)
  waiting for transfers between devices: 33.6 us -> 13.5 us
  Pallas kernels: 411 us -> 426 us
  starting transfers between devices: 14 us -> 4.14 us
  local copies, waits for them, and re-layouts: 43.8 us -> 35.8 us
    pallas_call x0 -> x1, Pallas kernels: none -> 21.2 us  [last(): pl.pallas_call(functools.partial(last_kernel, size, deep), in_specs=[anyw...]
    ppermute x6 -> x2, waiting for transfers between devices: 22 us -> 5.99 us  [flip(): return lax.ppermute(block, GROUP, [(g, g ^ mask) for g in range(8)])]
    add x7 -> x0, other arithmetic: 9.54 us -> none  [the longest x1 5.84 us: shards(): total = kept + got.astype(F32)]
    slice x6 -> x2, local copies, waits for them, and re-layouts: 7.12 us -> 0.06 us  [shards(): smalls = jnp.concatenate([smalls[0], smalls[1]], axis=1).astype(F32)]
    dot_general x5 -> x6, matrix products: 54.8 us -> 57 us  [matmul(): return jnp.dot(left, right, preferred_element_type=F32)]
  transfers between devices with their start and end apart: 20 -> 12, of which waited for: 6 -> 3; matrix products, arithmetic and copies ran while one was open for 27% -> 26% of each run, Pallas kernels for 61% -> 62%
where the time goes in v3:
time: 657 us; the launch traced here: 654 us
  Pallas kernels  426 us (65%)
  matrix products  119 us (18%)
  other arithmetic  40.2 us (6%)
  local copies, waits for them, and re-layouts  35.8 us (5%)
  between operations  15 us (2%)
  waiting for transfers between devices  13.5 us (2%)
    pallas_call x3, Pallas kernels, plane_sum(): pl.pallas_call(functools.partial(plane_sum_kernel, epilogue, wide), in_sp...  279 us
    pallas_call x1, Pallas kernels, head(): pl.pallas_call(head_kernel, in_specs=[anywhere, anywhere, pl.BlockSpec(me...  79.9 us
    dot_general x6, matrix products, matmul(): return jnp.dot(left, right, preferred_element_type=F32)  57 us
    dot_general x4, matrix products, left_inner(): lax.dot_general(left, right, (((0,), (0,)), ((), ())), preferred_element_...  45.9 us
    pallas_call x1, Pallas kernels, mixer_back(): pl.pallas_call(mixer_back_kernel, grid_spec=pltpu.PrefetchScalarGridSpec(...  27.6 us
    pallas_call x1, Pallas kernels, last(): pl.pallas_call(functools.partial(last_kernel, size, deep), in_specs=[anyw...  21.2 us
    pallas_call x1, Pallas kernels, mixer(): pl.pallas_call(mixer_kernel, grid_spec=pltpu.PrefetchScalarGridSpec(num_s...  19 us
    dot_general x1, matrix products, right_inner(): lax.dot_general(left, right, (((1,), (1,)), ((), ())), preferred_element_...  15.9 us
  transfers between devices with their start and end apart: 12, of which 3 were waited for; matrix products, arithmetic and copies ran while one was open for 26% of the time, Pallas kernels for 62%

profile of v3, /device:TPU:0, one launch (start us, length us, event | category | flops | bytes accessed | tf_op | source)
XLA Modules:
  0.0 653.8 jit_solution(5870381666068298000)
XLA Ops:
  8.6 1.7 constant_dynamic-slice_fusion.4
  10.3 1.3 pad_maximum_fusion.2
  13.0 1.3 pad_maximum_fusion.1
  17.7 2.3 dynamic-slice_bitcast_fusion.1.base.source
  20.1 2.4 dynamic-slice_bitcast_fusion.base
  23.7 1.8 dynamic_update_slice.13.gate_a
  25.5 1.6 dynamic_update_slice.15.gate_x
  27.1 79.9 %head.1 = (bf16[8,256,2048]{2,1,0:T(8,128)(2,1)}, bf16[8,256,2048]{2,1,0:T(8,128)(2,1)}) custom-call(bf16[1024,2048]{1,0:T(8,128)(2,1)} %bitcast.91, bf16[1024,2048]{1,0:T(8,128)(2,1)} %bitcast.92, f32[1,2048]{1,0:T(1,128)} %bitcast.98), custom_call_target="tpu_custom_call" | custom-call | flops 42949672960 | bytes 67108864 | tf_op jit(solution)/shard_map/head/pallas_call | solution.py:210
  107.7 11.3 %fusion.42.pre.pre_tail = f32[2048,640]{1,0:T(8,128)} fusion(bf16[2048,2048]{1,0:T(8,128)(2,1)} %bitcast.100, bf16[2048,960]{1,0:T(8,128)(2,1)} %all-gather.6.cloned.1.call-done), kind=kOutput, calls=%fused_computation.118 | convolution fusion | flops 5368709120 | bytes 16252928 | tf_op jit(solution)/shard_map/dot_general | solution.py:21
  119.0 19.0 %mixer.1 = (bf16[2048,320]{1,0:T(8,128)(2,1)}, f32[2048,320]{1,0:T(8,128)}, f32[2048,320]{1,0:T(8,128)}, f32[2048,320]{1,0:T(8,128)}, bf16[2048,320]{1,0:T(8,128)(2,1)}) custom-call(s32[8]{0:T(128)} %fusion.39.place, f32[2048,640]{1,0:T(8,128)} %fusion.42.pre.pre_tail, f32[2048,8]{1,0:T(8,128)} %convert_element_type.77.masks, f32[8,320]{1,0:T(8,128)} %concatenate.35.params, ...), custom_call_target="tpu_custom_call" | custom-call | flops 917504000 | bytes 15728640 | tf_op jit(solution)/shard_map/mixer/pallas_call | solution.py:663
  138.1 2.7 slice.233.right
  140.8 89.8 %plane_sum.3 = (bf16[8,256,2048]{2,1,0:T(8,128)(2,1)}, f32[256,2048]{1,0:T(8,128)}) custom-call(bf16[2048,320]{1,0:T(8,128)(2,1)} %get-tuple-element.74.left, bf16[2048,320]{1,0:T(8,128)(2,1)} %slice.233.right, bf16[256,2048]{1,0:T(8,128)(2,1)} %dynamic-slice_bitcast_fusion.1.base.source, bf16[256,2048]{1,0:T(8,128)(2,1)} %dynamic-slice_bitcast_fusion.1.base.source, ...), custom_call_target="tpu_custom_call" | custom-call | flops 77309411328 | bytes 4194304 | tf_op jit(solution)/shard_map/plane_sum/pallas_call | solution.py:408
  230.6 3.4 slice.232.right
  234.0 17.4 %fusion.45 = f32[2048,1536]{1,0:T(8,128)S(1)} fusion(bf16[2048,2048]{1,0:T(8,128)(2,1)} %bitcast.106, bf16[2048,1536]{1,0:T(8,128)(2,1)} %all-gather.8.cloned.1.call-done.right), kind=kOutput, calls=%fused_computation.121 | convolution fusion | flops 12884901888 | bytes 27262976 | tf_op jit(solution)/shard_map/dot_general | solution.py:21
  251.4 2.6 multiply_convert_fusion.1
  254.1 1.9 copy-done.5
  256.0 1.7 copy-done.10
  257.7 10.4 %convolution_convert_fusion.2 = bf16[768,2048]{1,0:T(8,128)(2,1)} fusion(bf16[2048,768]{1,0:T(8,128)(2,1)S(1)} %multiply_convert_fusion.1, bf16[2048,2048]{1,0:T(8,128)(2,1)} %bitcast.102), kind=kOutput, calls=%fused_computation.21 | convolution fusion | flops 6444023808 | bytes 14680064 | tf_op jit(solution)/shard_map/dot_general | solution.py:25
  268.1 6.2 all-gather.4.cloned.1.call-done
  274.4 7.9 %convolution_convert_fusion.1 = bf16[1024,2048]{1,0:T(8,128)(2,1)} fusion(bf16[768,2048]{1,0:T(8,128)(2,1)} %all-gather.4.cloned.1.call-done, bf16[2048,768]{1,0:T(8,128)(2,1)} %copy-done.10), kind=kOutput, calls=%fused_computation.20 | convolution fusion | flops 3223322624 | bytes 8912896 | tf_op jit(solution)/shard_map/dot_general | solution.py:21
  282.4 15.9 %fusion.9 = (bf16[2048,768]{1,0:T(8,128)(2,1)S(1)}, bf16[2048,768]{1,0:T(8,128)(2,1)S(1)}) fusion(f32[2048,1536]{1,0:T(8,128)} %copy-done.5, bf16[2048,2048]{1,0:T(8,128)(2,1)} %bitcast.103, bf16[768,2048]{1,0:T(8,128)(2,1)S(1)} %copy-done.28), kind=kOutput, calls=%fused_computation.12 | convolution fusion | flops 6478626816 | bytes 30408704 | tf_op jit(solution)/shard_map/dot_general | solution.py:29
  298.3 1.6 copy-done.8
  300.9 17.7 %convolution_convert_fusion = bf16[2048,1536]{1,0:T(8,128)(2,1)} fusion(bf16[2048,2048]{1,0:T(8,128)(2,1)} %bitcast.107, bf16[2048,768]{1,0:T(8,128)(2,1)S(1)} %get-tuple-element.132, bf16[2048,768]{1,0:T(8,128)(2,1)S(1)} %get-tuple-element.131), kind=kOutput, calls=%fused_computation.2 | convolution fusion | flops 12900630528 | bytes 20971520 | tf_op jit(solution)/shard_map/dot_general | solution.py:25
  319.0 6.1 pad_maximum_fusion.left
  326.2 4.8 add_convert_fusion
  330.9 1.5 collective-permute-start.1
  332.4 5.4 convert_add_fusion
  337.8 98.5 %plane_sum.4 = (bf16[8,256,2048]{2,1,0:T(8,128)(2,1)}, f32[256,2048]{1,0:T(8,128)}, f32[8,2048]{1,0:T(8,128)}) custom-call(bf16[2048,1536]{1,0:T(8,128)(2,1)} %pad_maximum_fusion.left, bf16[2048,1536]{1,0:T(8,128)(2,1)} %all-gather.8.cloned.1.call-done.right, bf16[256,2048]{1,0:T(8,128)(2,1)} %dynamic-slice_bitcast_fusion.base, ...), custom_call_target="tpu_custom_call" | custom-call | flops 77309411328 | bytes 4194304 | tf_op jit(solution)/shard_map/plane_sum/pallas_call | solution.py:408
  436.3 2.3 add_convert_fusion.2
  439.2 7.5 %convolution_convert_fusion.4 = bf16[320,2048]{1,0:T(8,128)(2,1)} fusion(bf16[2048,320]{1,0:T(8,128)(2,1)S(1)} %copy-done.30, bf16[2048,2048]{1,0:T(8,128)(2,1)} %bitcast.104), kind=kOutput, calls=%fused_computation.24 | convolution fusion | flops 2685009920 | bytes 11010048 | tf_op jit(solution)/shard_map/dot_general | solution.py:25
  447.1 10.1 %fusion.40.grad_mixed = f32[2048,320]{1,0:T(8,128)} fusion(bf16[2048,2048]{1,0:T(8,128)(2,1)} %bitcast.105, bf16[2048,960]{1,0:T(8,128)(2,1)} %all-gather.6.cloned.1.call-done), kind=kOutput, calls=%fused_computation.116 | convolution fusion | flops 2684354560 | bytes 12582912 | tf_op jit(solution)/shard_map/dot_general | solution.py:21
  457.3 27.6 %mixer_back.1 = (bf16[2048,640]{1,0:T(8,128)(2,1)}, f32[64,320]{1,0:T(8,128)}, f32[320,320]{1,0:T(8,128)}, f32[320,320]{1,0:T(8,128)}) custom-call(s32[8]{0:T(128)} %fusion.39.place, f32[2048,320]{1,0:T(8,128)} %fusion.40.grad_mixed, f32[2048,640]{1,0:T(8,128)} %fusion.42.pre.pre_tail, f32[2048,640]{1,0:T(8,128)} %fusion.42.pre.pre_tail, ...), custom_call_target="tpu_custom_call" | custom-call | flops 1808793600 | bytes 22282240 | tf_op jit(solution)/shard_map/mixer_back/pallas_call | solution.py:701
  484.9 1.4 fusion.26
  487.4 10.2 %convolution_convert_fusion.3 = bf16[2048,640]{1,0:T(8,128)(2,1)S(1)} fusion(bf16[2048,2048]{1,0:T(8,128)(2,1)} %bitcast.101, bf16[2048,640]{1,0:T(8,128)(2,1)} %get-tuple-element.103.left), kind=kOutput, calls=%fused_computation.22 | convolution fusion | flops 5370019840 | bytes 13631488 | tf_op jit(solution)/shard_map/dot_general | solution.py:25
  497.7 1.9 maximum_maximum_fusion
  499.6 4.1 add_convert_fusion.1.refs_0_
  503.6 90.4 %plane_sum.5 = (bf16[4,256,2048]{2,1,0:T(8,128)(2,1)}, f32[8,2048]{1,0:T(8,128)}, bf16[4,256,2048]{2,1,0:T(8,128)(2,1)}, bf16[512,1536]{1,0:T(8,128)(2,1)}, bf16...) custom-call(bf16[2048,640]{1,0:T(8,128)(2,1)} %get-tuple-element.103.left, bf16[2048,640]{1,0:T(8,128)(2,1)} %slice.232.right, ...), custom_call_target="tpu_custom_call" | custom-call | flops 42949672960 | bytes 4194304 | tf_op jit(solution)/shard_map/plane_sum/pallas_call | solution.py:408
  595.4 2.3 convert_element_type.98
  597.7 3.6 convert_element_type.99
  601.3 2.1 convert_element_type.100
  603.5 2.1 maximum_convert_fusion
  605.6 6.0 collective-permute-done.4
  611.6 21.2 %last.1 = (bf16[2,4,48,640]{3,2,1,0:T(8,128)(2,1)S(1)}, f32[8,2048]{1,0:T(8,128)S(1)}) custom-call(bf16[560,640]{1,0:T(8,128)(2,1)S(1)} %copy-done.2, f32[8,2048]{1,0:T(8,128)S(1)} %copy-done.4, f32[8,2048]{1,0:T(8,128)S(1)} %copy-done.3), custom_call_target="tpu_custom_call" | custom-call | flops 8589934592 | bytes 4194304 | tf_op jit(solution)/shard_map/last/pallas_call | solution.py:498
  636.6 1.3 maximum_convert_fusion.1
  637.9 1.3 maximum_convert_fusion.2
  641.0 2.1 copy.81
  643.1 1.6 copy-done.6
  644.7 2.0 copy.82
  (137 shorter events, 19.5 us)
Async XLA Ops:
  7.2 7.1 %copy-start = (bf16[1536,512]{1,0:T(8,128)(2,1)S(1)}, bf16[1536,512]{1,0:T(8,128)(2,1)}, u32[]{:S(2)}) copy-start(bf16[1536,512]{1,0:T(8,128)(2,1)} %param.36) | copy-start | bytes 4718596
  7.2 100.5 %all-gather.6.cloned.1.call-start = ((), (), s32[]{:S(2)}) async-start(), calls=%async_computation.5 | async-start | bytes 5242880 | tf_op jit(solution)/shard_map/all_gather | solution.py:758
  8.6 3.0 copy-start.18
  11.6 222.5 %all-gather.8.cloned.1.call-start = ((), (), s32[]{:S(2)}) async-start(), calls=%async_computation.6 | async-start | bytes 7864320 | tf_op jit(solution)/shard_map/all_gather | solution.py:760
  12.9 2.5 copy-start.23
  12.9 4.3 copy-start.24
  12.9 4.4 copy-start.25
  12.9 4.4 copy-start.26
  12.9 4.5 copy-start.27
  12.9 4.6 copy-start.21
  12.9 4.7 copy-start.19
  13.0 4.7 copy-start.20
  14.3 260.1 %all-gather.4.cloned.1.call-start = ((), (), s32[]{:S(2)}) async-start(), calls=%async_computation.4 | async-start | bytes 3932160 | tf_op jit(solution)/shard_map/all_gather | solution.py:761
  15.3 431.4 %reduce-scatter.5.cloned.1.call-start = ((), (), s32[]{:S(2)}) async-start(), calls=%async_computation.7 | async-start | bytes 3932160 | tf_op jit(solution)/shard_map/reduce_scatter | solution.py:752
  25.5 81.6 %copy-start.14 = (bf16[320,320]{1,0:T(8,128)(2,1)}, bf16[320,320]{1,0:T(8,128)(2,1)S(1)}, u32[]{:S(2)}) copy-start(bf16[320,320]{1,0:T(8,128)(2,1)S(1)} %dynamic_update_slice.13.gate_a) | copy-start | bytes 614404
  27.1 79.9 %copy-start.13 = (bf16[320,320]{1,0:T(8,128)(2,1)}, bf16[320,320]{1,0:T(8,128)(2,1)S(1)}, u32[]{:S(2)}) copy-start(bf16[320,320]{1,0:T(8,128)(2,1)S(1)} %dynamic_update_slice.15.gate_x) | copy-start | bytes 614404
  251.4 4.6 copy-start.5
  256.0 1.7 copy-start.10
  274.4 213.0 %reduce-scatter.7.cloned.1.call-start = ((), (), s32[]{:S(2)}) async-start(), calls=%async_computation.8 | async-start | bytes 7864320 | tf_op jit(solution)/shard_map/reduce_scatter | solution.py:752
  274.4 8.0 %copy-start.28 = (bf16[768,2048]{1,0:T(8,128)(2,1)S(1)}, bf16[768,2048]{1,0:T(8,128)(2,1)}, u32[]{:S(2)}) copy-start(bf16[768,2048]{1,0:T(8,128)(2,1)} %all-gather.4.cloned.1.call-done) | copy-start | bytes 9437188
  298.2 1.6 copy-start.8
  298.3 2.7 copy-start.9
  318.7 7.5 %collective-permute-start = (bf16[1024,2048]{1,0:T(8,128)(2,1)}, bf16[1024,2048]{1,0:T(8,128)(2,1)}, u32[]{:S(2)}, u32[]{:S(2)}) collective-permute-start(bf16[1024,2048]{1,0:T(8,128)(2,1)} %convolution_convert_fusion.1), channel_id=1, source_target_pairs={{0,1},{1,0},{2,3},{3,2},{4,5},{5,4},{6,7},{7,6},{8,9},{9,8},{10,11... | collective-permute-start | bytes 12582920 | tf_op jit(solution)/shard_map/ppermute | solution.py:70
  318.7 180.8 %reduce-scatter.9.cloned.1.call-start = ((), (), s32[]{:S(2)}) async-start(), calls=%async_computation.9 | async-start | bytes 1638400 | tf_op jit(solution)/shard_map/reduce_scatter | solution.py:752
  319.0 7.2 %copy-start.11 = (bf16[2048,768]{1,0:T(8,128)(2,1)S(1)}, bf16[2048,768]{1,0:T(8,128)(2,1)}, u32[]{:S(2)}) copy-start(bf16[2048,768]{1,0:T(8,128)(2,1)} %copy-done.10) | copy-start | bytes 9437188
  319.0 7.1 %copy-start.29 = (bf16[768,2048]{1,0:T(8,128)(2,1)S(1)}, bf16[768,2048]{1,0:T(8,128)(2,1)}, u32[]{:S(2)}) copy-start(bf16[768,2048]{1,0:T(8,128)(2,1)} %all-gather.4.cloned.1.call-done) | copy-start | bytes 9437188
  330.9 105.4 %collective-permute-start.1 = (bf16[512,2048]{1,0:T(8,128)(2,1)}, bf16[512,2048]{1,0:T(8,128)(2,1)}, u32[]{:S(2)}, u32[]{:S(2)}) collective-permute-start(bf16[512,2048]{1,0:T(8,128)(2,1)} %add_convert_fusion), channel_id=1, source_target_pairs={{0,4},{1,3},{2,6},{3,1},{4,0},{5,7},{6,2},{7,5},{8,12},{9,11},{10,... | collective-permute-start | bytes 6291464 | tf_op jit(solution)/shard_map/ppermute | solution.py:70
  436.3 2.9 copy-start.30
  438.6 48.7 %collective-permute-start.2 = (bf16[256,2048]{1,0:T(8,128)(2,1)S(1)}, bf16[256,2048]{1,0:T(8,128)(2,1)S(1)}, u32[]{:S(2)}, u32[]{:S(2)}) collective-permute-start(bf16[256,2048]{1,0:T(8,128)(2,1)S(1)} %add_convert_fusion.2), channel_id=1, source_target_pairs={{0,2},{1,5},{2,0},{3,7},{4,6},{5,1},{6,4},{7,3},{8,10},{9,13},{10,... | collective-permute-start | bytes 3145736 | tf_op jit(solution)/shard_map/ppermute | solution.py:70
  446.7 40.6 %collective-permute-start.3 = (bf16[768,512]{1,0:T(8,128)(2,1)}, bf16[768,512]{1,0:T(8,128)(2,1)S(1)}, u32[]{:S(2)}, u32[]{:S(2)}) collective-permute-start(bf16[768,512]{1,0:T(8,128)(2,1)} %reduce-scatter.5.cloned.1.call-done), channel_id=1, source_target_pairs={{0,4},{1,5},{2,6},{3,7},{4,0},{5,1},{6,2},{7,3},{8,12},{9,13},{10,... | collective-permute-start | bytes 2359304 | tf_op jit(solution)/shard_map/ppermute | solution.py:74
  447.1 147.0 %reduce-scatter.11.cloned.1.call-start = ((), (), s32[]{:S(2)}) async-start(), calls=%async_computation.10 | async-start | bytes 3584000 | tf_op jit(solution)/shard_map/reduce_scatter | solution.py:752
  487.3 10.3 %copy-start.16 = (bf16[768,512]{1,0:T(8,128)(2,1)}, bf16[768,512]{1,0:T(8,128)(2,1)S(1)}, u32[]{:S(2)}) copy-start(bf16[768,512]{1,0:T(8,128)(2,1)S(1)} %collective-permute-done.3) | copy-start | bytes 2359300
  594.1 7.2 %copy-start.12 = (bf16[512,1536]{1,0:T(8,128)(2,1)S(1)}, bf16[512,1536]{1,0:T(8,128)(2,1)}, u32[]{:S(2)}) copy-start(bf16[512,1536]{1,0:T(8,128)(2,1)} %get-tuple-element.124) | copy-start | bytes 4718596
  594.1 17.5 %collective-permute-start.4 = (bf16[560,640]{1,0:T(8,128)(2,1)}, bf16[560,640]{1,0:T(8,128)(2,1)S(1)}, u32[]{:S(2)}, u32[]{:S(2)}) collective-permute-start(bf16[560,640]{1,0:T(8,128)(2,1)} %reduce-scatter.11.cloned.1.call-done.own_in), channel_id=1, source_target_pairs={{0,4},{1,5},{2,6},{3,7},{4,0},{5,1},{6,2},{7,3},{8,12},{9,13},{10,... | collective-permute-start | bytes 2150408 | tf_op jit(solution)/shard_map/ppermute | solution.py:74
  597.7 5.7 copy-start.15
  597.7 5.7 copy-start.17
  603.4 8.2 %copy-start.2 = (bf16[560,640]{1,0:T(8,128)(2,1)S(1)}, bf16[560,640]{1,0:T(8,128)(2,1)}, u32[]{:S(2)}) copy-start(bf16[560,640]{1,0:T(8,128)(2,1)} %reduce-scatter.11.cloned.1.call-done.own_in) | copy-start | bytes 2150404
  603.4 8.2 %copy-start.3 = (f32[8,2048]{1,0:T(8,128)S(1)}, f32[8,2048]{1,0:T(8,128)}, u32[]{:S(2)}) copy-start(f32[8,2048]{1,0:T(8,128)} %get-tuple-element.118.gain_b) | copy-start | bytes 196612
  603.4 8.2 %copy-start.4 = (f32[8,2048]{1,0:T(8,128)S(1)}, f32[8,2048]{1,0:T(8,128)}, u32[]{:S(2)}) copy-start(f32[8,2048]{1,0:T(8,128)} %get-tuple-element.117.gain_a) | copy-start | bytes 196612
  633.2 2.9 copy-start.22
  635.7 5.3 copy-start.7
  641.0 3.7 copy-start.6
  641.0 5.7 copy-start.1
Sparse Core Ops, SparseCore 0:
  11.7 83.3 all-gather.5
  97.2 113.8 all-gather.7
  212.7 61.6 all-gather.3
  276.5 59.0 reduce-scatter.4
  337.7 110.6 reduce-scatter.6
  451.2 31.8 reduce-scatter.8
  499.7 55.6 reduce-scatter.10

commit v4 on v3

--- a/solution.py
+++ b/solution.py
@@ -235,10 +235,12 @@
     elif wide:
         out, kept_out, gain_out, refs = refs[0], refs[1], refs[2], refs[3:]
     else:
-        rows_in, pair, single, out, gain_out, rows_out, pair_a, pair_b, single_out = refs[:9]
-        refs = refs[9:]
+        rows_in, rows_along, pair, out, gain_out, rows_out, pair_a = refs[:7]
+        refs = refs[7:]
     to_core, from_core, acc, to_far, from_far, to_near, from_near, own, store, send, recv, gsend, grecv = refs
     rows, width = own.shape
+    if not wide:
+        own = out
     core, line, tp, across, along, same, near, far = partners()
     meet(same, near, far)
     tile = width // 4
@@ -261,30 +263,23 @@
     far_copy = [remote(to_far.at[h], from_far.at[h], send.at[2 + h], recv.at[2 + h], far) for h in range(2)]
     near_copy = remote(to_near, from_near, send.at[4], recv.at[4], near)
 
-    local = []
+    local, carried = [], []
     if not wide:
         came = (1 - line) * 2 + core
-        local.append(pltpu.make_async_copy(rows_in, rows_out.at[tp], store.at[1]))
-        rows_copy = [
-            remote(rows_in, rows_out.at[tp], gsend.at[3], grecv.at[3], along),
-            remote(rows_in, rows_out.at[tp], gsend.at[4], grecv.at[4], same),
-            remote(rows_out.at[came], rows_out.at[came], gsend.at[5], grecv.at[5], same),
+        units = pair.shape[1] // 2
+        cols = pl.ds(pl.multiple_of(lax.axis_index("ctx") * units, 128), units)
+        mine = pair.at[:, pl.ds(0, units)]
+        carried = [
+            remote(rows_in, rows_out.at[tp], gsend.at[0], grecv.at[0], same),
+            remote(rows_along, rows_out.at[came], gsend.at[1], grecv.at[1], same),
+            remote(mine, pair_a.at[:, cols], gsend.at[2], grecv.at[2], across),
         ]
-        half_at = lax.axis_index("ctx")
-        units, deep = pair.shape[1] // 2, single.shape[0]
-        cols = pl.ds(pl.multiple_of(half_at * units, 128), units)
-        lines = pl.ds(pl.multiple_of(half_at * deep, 16), deep)
-        swap = (
-            (pair.at[:, pl.ds(0, units)], pair_a.at[:, cols]),
-            (pair.at[:, pl.ds(units, units)], pair_b.at[:, cols]),
-            (single, single_out.at[lines, :]),
-        )
-        half_copy = [
-            remote(src, dst, gsend.at[6 + i], grecv.at[6 + i], across) for i, (src, dst) in enumerate(swap)
+        local = [
+            pltpu.make_async_copy(rows_in, rows_out.at[tp], store.at[0]),
+            pltpu.make_async_copy(rows_along, rows_out.at[came], store.at[1]),
+            pltpu.make_async_copy(mine, pair_a.at[:, cols], store.at[2]),
         ]
-        local += [pltpu.make_async_copy(src, dst, store.at[2 + i]) for i, (src, dst) in enumerate(swap)]
-        rows_copy[0].start()
-        rows_copy[1].start()
+        carried[2].start()
         for copy in local:
             copy.start()
 
@@ -312,12 +307,10 @@
 
     by_rows(rows, 32, send_near)
     near_copy.start()
+    if not wide:
+        carried[0].start()
+        carried[1].start()
     far_copy[0].wait_recv()
-    if not wide:
-        for copy in half_copy:
-            copy.start()
-        rows_copy[0].wait_recv()
-        rows_copy[2].start()
 
     def settle(r):
         at = pl.ds(r, 32)
@@ -369,26 +362,14 @@
         copies[6].start()
         for k in (2, 4, 5, 6):
             copies[k].wait_recv()
+        local.append(mine)
     else:
-        mine = pltpu.make_async_copy(own, out.at[tp], store.at[0])
-        mine.start()
-        copies = [
-            remote(own, out.at[tp], gsend.at[0], grecv.at[0], along),
-            remote(own, out.at[tp], gsend.at[1], grecv.at[1], same),
-        ]
-        copies[0].start()
-        copies[1].start()
-        copies[0].wait_recv()
-        copies.append(remote(out.at[came], out.at[came], gsend.at[2], grecv.at[2], same))
-        copies[2].start()
-        copies[1].wait_recv()
-        copies[2].wait_recv()
-        for copy in rows_copy[1:] + half_copy:
+        for copy in carried:
             copy.wait_recv()
-        copies += rows_copy + half_copy
+        copies = carried
     for copy in copies + core_copy + far_copy + [near_copy]:
         copy.wait_send()
-    for copy in local + [mine]:
+    for copy in local:
         copy.wait()
 
 
@@ -401,15 +382,15 @@
     gains = jax.ShapeDtypeStruct((8, width), F32)
     extra = [whole] if epilogue == "norm" else [whole, gains] if wide else [gains]
     carried = []
+    result = jax.ShapeDtypeStruct((8, rows, width), BF16)
     if not wide:
-        _, pair, single = extra_in
-        carried = [(4, rows, width), pair.shape, pair.shape, (2 * single.shape[0], single.shape[1])]
-        carried = [jax.ShapeDtypeStruct(shape, BF16) for shape in carried]
+        carried = [jax.ShapeDtypeStruct((4, rows, width), BF16), jax.ShapeDtypeStruct(extra_in[2].shape, BF16)]
+        result = jax.ShapeDtypeStruct((rows, width), BF16)
     return pl.pallas_call(
         functools.partial(plane_sum_kernel, epilogue, wide),
         in_specs=[vmem] * (5 + len(extra_in)),
-        out_specs=[anywhere] + [vmem] * len(extra) + [anywhere] * len(carried),
-        out_shape=[jax.ShapeDtypeStruct((8 if wide else 4, rows, width), BF16)] + extra + carried,
+        out_specs=[anywhere if wide else vmem] + [vmem] * len(extra) + [anywhere] * len(carried),
+        out_shape=[result] + extra + carried,
         scratch_shapes=[
             pltpu.VMEM((4 * rows, width), BF16),
             pltpu.VMEM((4 * rows, width), BF16),
@@ -434,8 +415,8 @@
 
 
 def last_kernel(
-    size, deep, own_in, gain_a, gain_b, smalls, gains, plane, mine, lines, store, small_send, small_recv, plane_send,
-    plane_recv, line_send, line_recv,
+    size, deep, own_in, gain_a, gain_b, rows_in, pair, single, other_in, smalls, gains, rows_out, pair_b, single_out,
+    plane, mine, lines, store, send, recv, small_send, small_recv, plane_send, plane_recv, line_send, line_recv,
 ):
     thin = smalls.shape[2]
     fsdp, ctx, tp = lax.axis_index("fsdp"), lax.axis_index("ctx"), lax.axis_index("tp")
@@ -447,7 +428,29 @@
     across_line = [(dz, dc, 0) for dz in range(size) for dc in range(2)][1:]
     along_line = [(dz, 0, 0) for dz in range(1, size)]
     meet(*[away(*d) for d in in_plane + [d for d in across_line if d not in in_plane]])
-    copies = []
+    core, row, _, across, along, same, _, _ = partners()
+    came = (1 - row) * 2 + core
+    units, tall = pair.shape[1] // 2, single.shape[0]
+    cols = pl.ds(pl.multiple_of(ctx * units, 128), units)
+    tall_rows = pl.ds(pl.multiple_of(ctx * tall, 16), tall)
+    high = pair.at[:, pl.ds(units, units)]
+    copies = [
+        remote(own_in.at[pl.ds(0, deep), :], other_in, send.at[0], recv.at[0], across),
+        remote(rows_in, rows_out.at[tp], send.at[1], recv.at[1], along),
+        remote(rows_in, rows_out.at[tp], send.at[2], recv.at[2], same),
+        remote(rows_out.at[came], rows_out.at[came], send.at[3], recv.at[3], same),
+        remote(high, pair_b.at[:, cols], send.at[4], recv.at[4], across),
+        remote(single, single_out.at[tall_rows, :], send.at[5], recv.at[5], across),
+    ]
+    local = [
+        pltpu.make_async_copy(rows_in, rows_out.at[tp], store.at[1]),
+        pltpu.make_async_copy(high, pair_b.at[:, cols], store.at[2]),
+        pltpu.make_async_copy(single, single_out.at[tall_rows, :], store.at[3]),
+    ]
+    for i in (1, 0, 2, 4, 5):
+        copies[i].start()
+    for copy in local:
+        copy.start()
     at = lax.broadcasted_iota(jnp.int32, gains.shape, 0)
     sum_a = jnp.sum(gain_a[...], axis=0, keepdims=True)
     sum_b = jnp.sum(gain_b[...], axis=0, keepdims=True)
@@ -460,8 +463,8 @@
     for copy in sent:
         copy.start()
     thin_rows = own_in.at[pl.ds(deep, thin), :]
-    local = pltpu.make_async_copy(thin_rows, smalls.at[ctx, fsdp], store.at[0])
-    local.start()
+    local.append(pltpu.make_async_copy(thin_rows, smalls.at[ctx, fsdp], store.at[0]))
+    local[-1].start()
     for i, d in enumerate(across_line):
         copies.append(remote(thin_rows, smalls.at[ctx, fsdp], small_send.at[i], small_recv.at[i], away(*d)))
         copies[-1].start()
@@ -483,25 +486,32 @@
     for i in range(1, size):
         total = total + lines[i]
     gains[...] = total
-    for copy in copies:
+    copies[1].wait_recv()
+    copies[3].start()
+    for copy in copies[:1] + copies[2:]:
         copy.wait_recv()
     for copy in copies + sent + further:
         copy.wait_send()
-    local.wait()
-
-
-def last(own_in, gain_a, gain_b, deep, size, collective_id):
+    for copy in local:
+        copy.wait()
+
+
+def last(own_in, gain_a, gain_b, rows, pair, single, deep, size, collective_id):
     width, thin = own_in.shape[1], own_in.shape[0] - deep
     vmem = pl.BlockSpec(memory_space=pltpu.VMEM)
     anywhere = pl.BlockSpec(memory_space=pl.ANY)
-    sems = [pltpu.SemaphoreType.DMA((n,)) for n in (1, 2 * size, 2 * size, 8, 8, size, size)]
+    sems = [pltpu.SemaphoreType.DMA((n,)) for n in (4, 6, 6, 2 * size, 2 * size, 8, 8, size, size)]
     return pl.pallas_call(
         functools.partial(last_kernel, size, deep),
-        in_specs=[anywhere, vmem, vmem],
-        out_specs=[anywhere, vmem],
+        in_specs=[anywhere] + [vmem] * 5,
+        out_specs=[anywhere, anywhere, vmem, anywhere, anywhere, anywhere],
         out_shape=[
+            jax.ShapeDtypeStruct((deep, width), BF16),
             jax.ShapeDtypeStruct((2, size, thin, width), BF16),
             jax.ShapeDtypeStruct(gain_a.shape, F32),
+            jax.ShapeDtypeStruct((4,) + rows.shape, BF16),
+            jax.ShapeDtypeStruct(pair.shape, BF16),
+            jax.ShapeDtypeStruct((2 * single.shape[0], single.shape[1]), BF16),
         ],
         scratch_shapes=[
             pltpu.VMEM((8,) + gain_a.shape, F32),
@@ -514,7 +524,7 @@
         ),
         cost_estimate=pl.CostEstimate(flops=1 << 33, bytes_accessed=4 << 20, transcendentals=0),
         name="last",
-    )(own_in, gain_a, gain_b)
+    )(own_in, gain_a, gain_b, rows, pair, single)
 
 
 def scan_rows(a_ref, b_ref, carry, reverse):
@@ -834,11 +844,13 @@
     own_out = owned(grad_w_out, 1)
     grad_mixed = matmul(grad_proj, full_out)
     other_down = flip(own_down, 4)
+    output = (resid + low[:rows] + got_far[:rows].astype(F32) + got_near.astype(F32)).astype(BF16)
+    states, output = tied((states, output))
+    output_along = flip(output, 2)
     grads_in, sums, sum_a, sum_x = mixer_back(
         grad_mixed, pre, states, recur, opened, conv, masks, params, diag_a, diag_x, place, rows
     )
-    grads_in, got_near, other_down, own_gu = tied((grads_in, got_near, other_down, own_gu))
-    output = (resid + low[:rows] + got_far[:rows].astype(F32) + got_near.astype(F32)).astype(BF16)
+    grads_in, output_along, other_down, own_gu = tied((grads_in, output_along, other_down, own_gu))
     lines = jnp.sum(sums.reshape(8, 8, width), axis=1)
     head_at = lax.broadcasted_iota(jnp.int32, (head_width, width), 1) // head_width
     squares = [
@@ -857,20 +869,19 @@
     grad_w_in = jnp.concatenate([grad_w_in, small], axis=1).reshape(-1, 2 * width)
     grads_in, grad_w_in, own_out = tied((grads_in, grad_w_in, own_out))
     own_in = owned(grad_w_in, 0)
-    grad_tokens, gain_mix_part, output, own_gate, own_up, own_out = plane_sum(
-        "back", False, grads_in, full_in, grad_resid, own, gain_mix, 4, 5 << 33, (output, own_gu, own_out)
-    )
-    own_in, own_gate, own_up, own_out, own_down = tied((own_in, own_gate, own_up, own_out, own_down))
-    other_in = flip(own_in, 4)
-    own_in, other_in = tied((own_in, other_in))
-    smalls, gains = last(own_in, gain_mix_part, gain_mlp_part, model_width // fsdp_size, fsdp_size, 5)
+    grad_tokens, gain_mix_part, output, own_gate = plane_sum(
+        "back", False, grads_in, full_in, grad_resid, own, gain_mix, 4, 5 << 33, (output, output_along, own_gu)
+    )
+    other_in, smalls, gains, grad_tokens, own_up, own_out = last(
+        own_in, gain_mix_part, gain_mlp_part, grad_tokens, own_gu, own_out, model_width // fsdp_size, fsdp_size, 5
+    )
 
     def both_halves(x, other, axis):
         low = jnp.where(half_at == 0, x, other)
         high = jnp.where(half_at == 0, other, x)
         return jnp.concatenate([low, high], axis=axis).astype(F32)
 
-    own_in, other_in = [x[: model_width // fsdp_size] for x in (own_in, other_in)]
+    own_in = own_in[: model_width // fsdp_size]
     own_down = both_halves(own_down, other_down, 0)
     smalls = jnp.stack([smalls[..., :width], smalls[..., width:]], axis=2).reshape(2, fsdp_size * part_rows, width)
     smalls = jnp.concatenate([smalls[0], smalls[1]], axis=1).astype(F32)

time: 657 us -> 663 us (level)
  Pallas kernels: 426 us -> 439 us
    pallas_call x1, Pallas kernels: 21.2 us -> 61.2 us  [last(): pl.pallas_call(functools.partial(last_kernel, size, deep), in_specs=[anyw...]
    pallas_call x3, Pallas kernels: 279 us -> 251 us  [plane_sum(): pl.pallas_call(functools.partial(plane_sum_kernel, epilogue, wide), in_sp...]
    ppermute x3, waiting for transfers between devices: 1.05 us -> 8.37 us  [exchange(): return lax.ppermute(block, GROUP, pairs)]
  transfers between devices with their start and end apart: 12 -> 12, of which waited for: 3 -> 3; matrix products, arithmetic and copies ran while one was open for 26% -> 25% of each run, Pallas kernels for 62% -> 57%
where the time goes in v4:
time: 663 us; the launch traced here: 660 us
  Pallas kernels  439 us (66%)
  matrix products  118 us (18%)
  other arithmetic  38.3 us (6%)
  local copies, waits for them, and re-layouts  33.6 us (5%)
  between operations  15.1 us (2%)
  waiting for transfers between devices  12.5 us (2%)
    pallas_call x3, Pallas kernels, plane_sum(): pl.pallas_call(functools.partial(plane_sum_kernel, epilogue, wide), in_sp...  251 us
    pallas_call x1, Pallas kernels, head(): pl.pallas_call(head_kernel, in_specs=[anywhere, anywhere, pl.BlockSpec(me...  79.9 us
    pallas_call x1, Pallas kernels, last(): pl.pallas_call(functools.partial(last_kernel, size, deep), in_specs=[anyw...  61.2 us
    dot_general x6, matrix products, matmul(): return jnp.dot(left, right, preferred_element_type=F32)  55.8 us
    dot_general x4, matrix products, left_inner(): lax.dot_general(left, right, (((0,), (0,)), ((), ())), preferred_element_...  45.4 us
    pallas_call x1, Pallas kernels, mixer_back(): pl.pallas_call(mixer_back_kernel, grid_spec=pltpu.PrefetchScalarGridSpec(...  27.6 us
    pallas_call x1, Pallas kernels, mixer(): pl.pallas_call(mixer_kernel, grid_spec=pltpu.PrefetchScalarGridSpec(num_s...  19.1 us
    dot_general x1, matrix products, right_inner(): lax.dot_general(left, right, (((1,), (1,)), ((), ())), preferred_element_...  17 us
  transfers between devices with their start and end apart: 12, of which 3 were waited for; matrix products, arithmetic and copies ran while one was open for 25% of the time, Pallas kernels for 57%

profile of v4, /device:TPU:0, one launch (start us, length us, event | category | flops | bytes accessed | tf_op | source)
XLA Modules:
  0.0 660.0 jit_solution(8048783715827151291)
XLA Ops:
  8.6 1.5 constant_dynamic-slice_fusion.4
  10.1 1.3 pad_maximum_fusion.2
  11.5 1.5 constant_dynamic-slice_fusion
  13.1 1.3 pad_maximum_fusion.1
  17.9 2.3 dynamic-slice_bitcast_fusion.1.base.source
  20.2 2.4 dynamic-slice_bitcast_fusion.base
  23.8 1.8 dynamic_update_slice.13.gate_a
  25.6 1.6 dynamic_update_slice.15.gate_x
  27.2 79.9 %head.1 = (bf16[8,256,2048]{2,1,0:T(8,128)(2,1)}, bf16[8,256,2048]{2,1,0:T(8,128)(2,1)}) custom-call(bf16[1024,2048]{1,0:T(8,128)(2,1)} %bitcast.91, bf16[1024,2048]{1,0:T(8,128)(2,1)} %bitcast.92, f32[1,2048]{1,0:T(1,128)} %bitcast.98), custom_call_target="tpu_custom_call" | custom-call | flops 42949672960 | bytes 67108864 | tf_op jit(solution)/shard_map/head/pallas_call | solution.py:210
  107.8 11.3 %fusion.42.pre.pre_tail = f32[2048,640]{1,0:T(8,128)} fusion(bf16[2048,2048]{1,0:T(8,128)(2,1)} %bitcast.100, bf16[2048,960]{1,0:T(8,128)(2,1)} %all-gather.6.cloned.1.call-done), kind=kOutput, calls=%fused_computation.118 | convolution fusion | flops 5368709120 | bytes 16252928 | tf_op jit(solution)/shard_map/dot_general | solution.py:21
  119.1 19.1 %mixer.1 = (bf16[2048,320]{1,0:T(8,128)(2,1)}, f32[2048,320]{1,0:T(8,128)}, f32[2048,320]{1,0:T(8,128)}, f32[2048,320]{1,0:T(8,128)}, bf16[2048,320]{1,0:T(8,128)(2,1)}) custom-call(s32[8]{0:T(128)} %fusion.39.place, f32[2048,640]{1,0:T(8,128)} %fusion.42.pre.pre_tail, f32[2048,8]{1,0:T(8,128)} %convert_element_type.77.masks, f32[8,320]{1,0:T(8,128)} %concatenate.35.params, ...), custom_call_target="tpu_custom_call" | custom-call | flops 917504000 | bytes 15728640 | tf_op jit(solution)/shard_map/mixer/pallas_call | solution.py:673
  138.2 2.7 slice.230.right
  140.9 89.8 %plane_sum.3 = (bf16[8,256,2048]{2,1,0:T(8,128)(2,1)}, f32[256,2048]{1,0:T(8,128)}) custom-call(bf16[2048,320]{1,0:T(8,128)(2,1)} %get-tuple-element.71.left, bf16[2048,320]{1,0:T(8,128)(2,1)} %slice.230.right, bf16[256,2048]{1,0:T(8,128)(2,1)} %dynamic-slice_bitcast_fusion.1.base.source, bf16[256,2048]{1,0:T(8,128)(2,1)} %dynamic-slice_bitcast_fusion.1.base.source, ...), custom_call_target="tpu_custom_call" | custom-call | flops 77309411328 | bytes 4194304 | tf_op jit(solution)/shard_map/plane_sum/pallas_call | solution.py:389
  230.7 3.4 slice.229.right
  234.1 17.4 %fusion.45 = f32[2048,1536]{1,0:T(8,128)S(1)} fusion(bf16[2048,2048]{1,0:T(8,128)(2,1)} %bitcast.106, bf16[2048,1536]{1,0:T(8,128)(2,1)} %all-gather.8.cloned.1.call-done.right), kind=kOutput, calls=%fused_computation.121 | convolution fusion | flops 12884901888 | bytes 27262976 | tf_op jit(solution)/shard_map/dot_general | solution.py:21
  251.5 4.6 copy-done.8
  256.1 2.6 multiply_convert_fusion.1
  258.7 11.5 %convolution_convert_fusion.2 = bf16[768,2048]{1,0:T(8,128)(2,1)} fusion(bf16[2048,768]{1,0:T(8,128)(2,1)S(1)} %multiply_convert_fusion.1, bf16[2048,2048]{1,0:T(8,128)(2,1)} %bitcast.104), kind=kOutput, calls=%fused_computation.21 | convolution fusion | flops 6444023808 | bytes 14680064 | tf_op jit(solution)/shard_map/dot_general | solution.py:25
  270.3 3.9 all-gather.4.cloned.1.call-done
  274.3 7.0 %convolution_convert_fusion.1 = bf16[1024,2048]{1,0:T(8,128)(2,1)} fusion(bf16[768,2048]{1,0:T(8,128)(2,1)} %all-gather.4.cloned.1.call-done, bf16[2048,768]{1,0:T(8,128)(2,1)S(1)} %multiply_convert_fusion.1), kind=kOutput, calls=%fused_computation.20 | convolution fusion | flops 3223322624 | bytes 8912896 | tf_op jit(solution)/shard_map/dot_general | solution.py:21
  281.3 17.0 %fusion.9 = (bf16[2048,768]{1,0:T(8,128)(2,1)S(1)}, bf16[2048,768]{1,0:T(8,128)(2,1)}) fusion(f32[2048,1536]{1,0:T(8,128)} %copy-done.8, bf16[2048,2048]{1,0:T(8,128)(2,1)} %bitcast.105, bf16[768,2048]{1,0:T(8,128)(2,1)S(1)} %copy-done.26), kind=kOutput, calls=%fused_computation.12 | convolution fusion | flops 6478626816 | bytes 30408704 | tf_op jit(solution)/shard_map/dot_general | solution.py:29
  298.3 16.0 %convolution_convert_fusion = bf16[2048,1536]{1,0:T(8,128)(2,1)} fusion(bf16[2048,2048]{1,0:T(8,128)(2,1)S(1)} %bitcast.109, bf16[2048,768]{1,0:T(8,128)(2,1)} %get-tuple-element.126, bf16[2048,768]{1,0:T(8,128)(2,1)S(1)} %get-tuple-element.125), kind=kOutput, calls=%fused_computation.2 | convolution fusion | flops 12900630528 | bytes 20971520 | tf_op jit(solution)/shard_map/dot_general | solution.py:25
  314.7 5.2 pad_maximum_fusion.left
  319.9 2.0 collective-permute-done
  321.9 4.8 add_convert_fusion
  326.6 1.5 collective-permute-start.1
  328.2 5.4 convert_add_fusion
  333.6 98.5 %plane_sum.4 = (bf16[8,256,2048]{2,1,0:T(8,128)(2,1)}, f32[256,2048]{1,0:T(8,128)}, f32[8,2048]{1,0:T(8,128)}) custom-call(bf16[2048,1536]{1,0:T(8,128)(2,1)} %pad_maximum_fusion.left, bf16[2048,1536]{1,0:T(8,128)(2,1)} %all-gather.8.cloned.1.call-done.right, bf16[256,2048]{1,0:T(8,128)(2,1)} %dynamic-slice_bitcast_fusion.base, ...), custom_call_target="tpu_custom_call" | custom-call | flops 77309411328 | bytes 4194304 | tf_op jit(solution)/shard_map/plane_sum/pallas_call | solution.py:389
  432.1 2.3 add_convert_fusion.2
  435.2 7.5 %convolution_convert_fusion.4 = bf16[320,2048]{1,0:T(8,128)(2,1)} fusion(bf16[2048,320]{1,0:T(8,128)(2,1)S(1)} %copy-done.29, bf16[2048,2048]{1,0:T(8,128)(2,1)} %bitcast.102), kind=kOutput, calls=%fused_computation.24 | convolution fusion | flops 2685009920 | bytes 11010048 | tf_op jit(solution)/shard_map/dot_general | solution.py:25
  442.9 6.4 collective-permute-done.2
  449.3 2.8 add_convert_fusion.1.refs_0_
  452.9 10.0 %fusion.40.grad_mixed = f32[2048,320]{1,0:T(8,128)} fusion(bf16[2048,2048]{1,0:T(8,128)(2,1)} %bitcast.103, bf16[2048,960]{1,0:T(8,128)(2,1)} %all-gather.6.cloned.1.call-done), kind=kOutput, calls=%fused_computation.116 | convolution fusion | flops 2684354560 | bytes 12582912 | tf_op jit(solution)/shard_map/dot_general | solution.py:21
  462.9 27.6 %mixer_back.1 = (bf16[2048,640]{1,0:T(8,128)(2,1)}, f32[64,320]{1,0:T(8,128)}, f32[320,320]{1,0:T(8,128)}, f32[320,320]{1,0:T(8,128)}) custom-call(s32[8]{0:T(128)} %fusion.39.place, f32[2048,320]{1,0:T(8,128)} %fusion.40.grad_mixed, f32[2048,640]{1,0:T(8,128)} %fusion.42.pre.pre_tail, f32[2048,640]{1,0:T(8,128)} %fusion.42.pre.pre_tail, ...), custom_call_target="tpu_custom_call" | custom-call | flops 1808793600 | bytes 22282240 | tf_op jit(solution)/shard_map/mixer_back/pallas_call | solution.py:711
  490.5 1.4 fusion.26
  493.0 10.4 %convolution_convert_fusion.3 = bf16[2048,640]{1,0:T(8,128)(2,1)S(1)} fusion(bf16[2048,2048]{1,0:T(8,128)(2,1)} %bitcast.101, bf16[2048,640]{1,0:T(8,128)(2,1)} %get-tuple-element.102.left), kind=kOutput, calls=%fused_computation.22 | convolution fusion | flops 5370019840 | bytes 13631488 | tf_op jit(solution)/shard_map/dot_general | solution.py:25
  503.4 1.9 maximum_maximum_fusion
  505.3 62.6 %plane_sum.5 = (bf16[256,2048]{1,0:T(8,128)(2,1)}, f32[8,2048]{1,0:T(8,128)}, bf16[4,256,2048]{2,1,0:T(8,128)(2,1)}, bf16[512,1536]{1,0:T(8,128)(2,1)}) custom-call(bf16[2048,640]{1,0:T(8,128)(2,1)} %get-tuple-element.102.left, bf16[2048,640]{1,0:T(8,128)(2,1)} %slice.229.right, f32[256,2048]{1,0:T(8,128)} %get-tuple-element.104.base, ...), custom_call_target="tpu_custom_call" | custom-call | flops 42949672960 | bytes 4194304 | tf_op jit(solution)/shard_map/plane_sum/pallas_call | solution.py:389
  567.9 3.6 convert_element_type.99
  571.5 1.5 broadcast_select_fusion.1
  573.0 2.1 maximum_convert_fusion
  576.2 61.2 %last.1 = (bf16[512,640]{1,0:T(8,128)(2,1)S(1)}, bf16[2,4,48,640]{3,2,1,0:T(8,128)(2,1)S(1)}, f32[8,2048]{1,0:T(8,128)S(1)}, bf16[4,256,2048]{2,1,0:T(8,128)(2,1...) custom-call(bf16[560,640]{1,0:T(8,128)(2,1)S(1)} %copy-done.2, f32[8,2048]{1,0:T(8,128)S(1)} %copy-done.7, ...), custom_call_target="tpu_custom_call" | custom-call | flops 8589934592 | bytes 4194304 | tf_op jit(solution)/shard_map/last/pallas_call | solution.py:504
  640.9 1.2 convert_element_type.98
  642.1 2.1 convert_element_type.100
  644.5 1.3 maximum_convert_fusion.1
  645.8 1.3 maximum_convert_fusion.2
  648.9 2.0 copy.81
  650.9 2.0 copy.82
  (140 shorter events, 16.7 us)
Async XLA Ops:
  7.2 7.2 %copy-start = (bf16[1536,512]{1,0:T(8,128)(2,1)S(1)}, bf16[1536,512]{1,0:T(8,128)(2,1)}, u32[]{:S(2)}) copy-start(bf16[1536,512]{1,0:T(8,128)(2,1)} %param.36) | copy-start | bytes 4718596
  7.2 100.6 %all-gather.6.cloned.1.call-start = ((), (), s32[]{:S(2)}) async-start(), calls=%async_computation.5 | async-start | bytes 5242880 | tf_op jit(solution)/shard_map/all_gather | solution.py:768
  11.4 222.7 %all-gather.8.cloned.1.call-start = ((), (), s32[]{:S(2)}) async-start(), calls=%async_computation.6 | async-start | bytes 7864320 | tf_op jit(solution)/shard_map/all_gather | solution.py:770
  13.0 2.5 copy-start.21
  13.0 4.3 copy-start.22
  13.0 4.4 copy-start.23
  13.0 4.5 copy-start.24
  13.0 4.5 copy-start.25
  13.0 4.6 copy-start.19
  13.0 4.7 copy-start.17
  13.1 4.7 copy-start.18
  14.4 259.8 %all-gather.4.cloned.1.call-start = ((), (), s32[]{:S(2)}) async-start(), calls=%async_computation.4 | async-start | bytes 3932160 | tf_op jit(solution)/shard_map/all_gather | solution.py:771
  15.4 427.3 %reduce-scatter.5.cloned.1.call-start = ((), (), s32[]{:S(2)}) async-start(), calls=%async_computation.7 | async-start | bytes 3932160 | tf_op jit(solution)/shard_map/reduce_scatter | solution.py:762
  25.6 81.6 %copy-start.15 = (bf16[320,320]{1,0:T(8,128)(2,1)}, bf16[320,320]{1,0:T(8,128)(2,1)S(1)}, u32[]{:S(2)}) copy-start(bf16[320,320]{1,0:T(8,128)(2,1)S(1)} %dynamic_update_slice.13.gate_a) | copy-start | bytes 614404
  27.2 79.9 %copy-start.14 = (bf16[320,320]{1,0:T(8,128)(2,1)}, bf16[320,320]{1,0:T(8,128)(2,1)S(1)}, u32[]{:S(2)}) copy-start(bf16[320,320]{1,0:T(8,128)(2,1)S(1)} %dynamic_update_slice.15.gate_x) | copy-start | bytes 614404
  251.5 4.6 copy-start.8
  258.7 15.6 %copy-start.10 = (bf16[2048,768]{1,0:T(8,128)(2,1)}, bf16[2048,768]{1,0:T(8,128)(2,1)S(1)}, u32[]{:S(2)}) copy-start(bf16[2048,768]{1,0:T(8,128)(2,1)S(1)} %multiply_convert_fusion.1) | copy-start | bytes 9437188
  274.2 218.8 %reduce-scatter.7.cloned.1.call-start = ((), (), s32[]{:S(2)}) async-start(), calls=%async_computation.8 | async-start | bytes 7864320 | tf_op jit(solution)/shard_map/reduce_scatter | solution.py:762
  274.3 7.0 %copy-start.26 = (bf16[768,2048]{1,0:T(8,128)(2,1)S(1)}, bf16[768,2048]{1,0:T(8,128)(2,1)}, u32[]{:S(2)}) copy-start(bf16[768,2048]{1,0:T(8,128)(2,1)} %all-gather.4.cloned.1.call-done) | copy-start | bytes 9437188
  274.3 24.0 %slice-start = ((s8[8388608]{0:T(1024)(128)(4,1)}), s8[4194304]{0:T(1024)(128)(4,1)S(1)}, s32[]{:S(2)}) async-start(s8[8388608]{0:T(1024)(128)(4,1)} %bitcast.107), calls=%async_computation.11 | async-start | bytes 8388608
  281.3 17.0 %slice-start.1 = ((s8[8388608]{0:T(1024)(128)(4,1)}), s8[4194304]{0:T(1024)(128)(4,1)S(1)}, s32[]{:S(2)}) async-start(s8[8388608]{0:T(1024)(128)(4,1)} %bitcast.107), calls=%async_computation.12 | async-start | bytes 8388608
  314.3 7.5 %collective-permute-start = (bf16[1024,2048]{1,0:T(8,128)(2,1)}, bf16[1024,2048]{1,0:T(8,128)(2,1)}, u32[]{:S(2)}, u32[]{:S(2)}) collective-permute-start(bf16[1024,2048]{1,0:T(8,128)(2,1)} %convolution_convert_fusion.1), channel_id=1, source_target_pairs={{0,1},{1,0},{2,3},{3,2},{4,5},{5,4},{6,7},{7,6},{8,9},{9,8},{10,11... | collective-permute-start | bytes 12582920 | tf_op jit(solution)/shard_map/ppermute | solution.py:70
  314.4 190.9 %reduce-scatter.9.cloned.1.call-start = ((), (), s32[]{:S(2)}) async-start(), calls=%async_computation.9 | async-start | bytes 1638400 | tf_op jit(solution)/shard_map/reduce_scatter | solution.py:762
  314.7 7.2 %copy-start.11 = (bf16[2048,768]{1,0:T(8,128)(2,1)S(1)}, bf16[2048,768]{1,0:T(8,128)(2,1)}, u32[]{:S(2)}) copy-start(bf16[2048,768]{1,0:T(8,128)(2,1)} %copy-done.10) | copy-start | bytes 9437188
  314.7 7.2 %copy-start.27 = (bf16[768,2048]{1,0:T(8,128)(2,1)S(1)}, bf16[768,2048]{1,0:T(8,128)(2,1)}, u32[]{:S(2)}) copy-start(bf16[768,2048]{1,0:T(8,128)(2,1)} %all-gather.4.cloned.1.call-done) | copy-start | bytes 9437188
  326.6 105.5 %collective-permute-start.1 = (bf16[512,2048]{1,0:T(8,128)(2,1)}, bf16[512,2048]{1,0:T(8,128)(2,1)}, u32[]{:S(2)}, u32[]{:S(2)}) collective-permute-start(bf16[512,2048]{1,0:T(8,128)(2,1)} %add_convert_fusion), channel_id=1, source_target_pairs={{0,4},{1,3},{2,6},{3,1},{4,0},{5,7},{6,2},{7,5},{8,12},{9,11},{10,... | collective-permute-start | bytes 6291464 | tf_op jit(solution)/shard_map/ppermute | solution.py:70
  432.1 3.1 copy-start.29
  434.4 15.0 %collective-permute-start.2 = (bf16[256,2048]{1,0:T(8,128)(2,1)S(1)}, bf16[256,2048]{1,0:T(8,128)(2,1)}, u32[]{:S(2)}, u32[]{:S(2)}) collective-permute-start(bf16[256,2048]{1,0:T(8,128)(2,1)S(1)} %add_convert_fusion.2), channel_id=1, source_target_pairs={{0,2},{1,5},{2,0},{3,7},{4,6},{5,1},{6,4},{7,3},{8,10},{9,13},{10,... | collective-permute-start | bytes 3145736 | tf_op jit(solution)/shard_map/ppermute | solution.py:70
  435.2 14.1 %copy-start.12 = (f32[256,2048]{1,0:T(8,128)S(1)}, f32[256,2048]{1,0:T(8,128)}, u32[]{:S(2)}) copy-start(f32[256,2048]{1,0:T(8,128)} %get-tuple-element.81.source) | copy-start | bytes 6291460
  442.7 50.3 %collective-permute-start.4 = (bf16[768,512]{1,0:T(8,128)(2,1)}, bf16[768,512]{1,0:T(8,128)(2,1)}, u32[]{:S(2)}, u32[]{:S(2)}) collective-permute-start(bf16[768,512]{1,0:T(8,128)(2,1)} %reduce-scatter.5.cloned.1.call-done), channel_id=1, source_target_pairs={{0,4},{1,5},{2,6},{3,7},{4,0},{5,1},{6,2},{7,3},{8,12},{9,13},{10,... | collective-permute-start | bytes 2359304 | tf_op jit(solution)/shard_map/ppermute | solution.py:74
  442.9 132.2 %reduce-scatter.11.cloned.1.call-start = ((), (), s32[]{:S(2)}) async-start(), calls=%async_computation.10 | async-start | bytes 3584000 | tf_op jit(solution)/shard_map/reduce_scatter | solution.py:762
  452.1 10.8 %copy-start.13 = (bf16[256,2048]{1,0:T(8,128)(2,1)}, bf16[256,2048]{1,0:T(8,128)(2,1)S(1)}, u32[]{:S(2)}) copy-start(bf16[256,2048]{1,0:T(8,128)(2,1)S(1)} %add_convert_fusion.1.refs_0_) | copy-start | bytes 3145732
  452.1 40.9 %collective-permute-start.3 = (bf16[256,2048]{1,0:T(8,128)(2,1)S(1)}, bf16[256,2048]{1,0:T(8,128)(2,1)S(1)}, u32[]{:S(2)}, u32[]{:S(2)}) collective-permute-start(bf16[256,2048]{1,0:T(8,128)(2,1)S(1)} %add_convert_fusion.1.refs_0_), channel_id=1, source_target_pairs={{0,2},{1,3},{2,0},{3,1},{4,6},{5,7},{6,4},{7,5},{8,10},{9,11},{10,... | collective-permute-start | bytes 3145736 | tf_op jit(solution)/shard_map/ppermute | solution.py:74
  493.0 10.4 %copy-start.28 = (bf16[256,2048]{1,0:T(8,128)(2,1)}, bf16[256,2048]{1,0:T(8,128)(2,1)S(1)}, u32[]{:S(2)}) copy-start(bf16[256,2048]{1,0:T(8,128)(2,1)S(1)} %collective-permute-done.3.refs_1_) | copy-start | bytes 3145732
  567.9 3.6 copy-start.16
  571.4 3.6 copy-start.3
  571.4 3.6 copy-start.4
  571.4 3.6 copy-start.5
  571.5 3.6 copy-start.6
  571.5 3.6 copy-start.7
  575.1 1.1 copy-start.2
  637.6 2.7 copy-start.20
  644.5 4.4 copy-start.9
  648.9 4.0 copy-start.1
Sparse Core Ops, SparseCore 0:
  11.6 83.3 all-gather.5
  97.1 113.8 all-gather.7
  212.5 61.6 all-gather.3
  276.4 59.0 reduce-scatter.4
  337.6 110.6 reduce-scatter.6
  451.1 31.8 reduce-scatter.8
  505.4 55.7 reduce-scatter.10

commit v5 on v4

--- a/solution.py
+++ b/solution.py
@@ -235,8 +235,8 @@
     elif wide:
         out, kept_out, gain_out, refs = refs[0], refs[1], refs[2], refs[3:]
     else:
-        rows_in, rows_along, pair, out, gain_out, rows_out, pair_a = refs[:7]
-        refs = refs[7:]
+        rows_in, rows_along, pair, pair_far, stack, stack_far, out, gain_out, rows_out, pair_a, pair_b, stack_out = refs[:12]
+        refs = refs[12:]
     to_core, from_core, acc, to_far, from_far, to_near, from_near, own, store, send, recv, gsend, grecv = refs
     rows, width = own.shape
     if not wide:
@@ -266,20 +266,19 @@
     local, carried = [], []
     if not wide:
         came = (1 - line) * 2 + core
-        units = pair.shape[1] // 2
-        cols = pl.ds(pl.multiple_of(lax.axis_index("ctx") * units, 128), units)
-        mine = pair.at[:, pl.ds(0, units)]
+        half_at = lax.axis_index("ctx")
+        units, tall = pair.shape[1] // 2, stack.shape[0]
         carried = [
             remote(rows_in, rows_out.at[tp], gsend.at[0], grecv.at[0], same),
             remote(rows_along, rows_out.at[came], gsend.at[1], grecv.at[1], same),
-            remote(mine, pair_a.at[:, cols], gsend.at[2], grecv.at[2], across),
         ]
-        local = [
-            pltpu.make_async_copy(rows_in, rows_out.at[tp], store.at[0]),
-            pltpu.make_async_copy(rows_along, rows_out.at[came], store.at[1]),
-            pltpu.make_async_copy(mine, pair_a.at[:, cols], store.at[2]),
-        ]
-        carried[2].start()
+        places = [(rows_in, rows_out.at[tp]), (rows_along, rows_out.at[came])]
+        for at, halves, block in ((half_at, pair, stack), (1 - half_at, pair_far, stack_far)):
+            cols = pl.ds(pl.multiple_of(at * units, 128), units)
+            places.append((halves.at[:, pl.ds(0, units)], pair_a.at[:, cols]))
+            places.append((halves.at[:, pl.ds(units, units)], pair_b.at[:, cols]))
+            places.append((block, stack_out.at[pl.ds(pl.multiple_of(at * tall, 16), tall), :]))
+        local = [pltpu.make_async_copy(src, dst, store.at[i]) for i, (src, dst) in enumerate(places)]
         for copy in local:
             copy.start()
 
@@ -384,7 +383,9 @@
     carried = []
     result = jax.ShapeDtypeStruct((8, rows, width), BF16)
     if not wide:
-        carried = [jax.ShapeDtypeStruct((4, rows, width), BF16), jax.ShapeDtypeStruct(extra_in[2].shape, BF16)]
+        _, _, pair, _, stack, _ = extra_in
+        carried = [(4, rows, width), pair.shape, pair.shape, (2 * stack.shape[0], stack.shape[1])]
+        carried = [jax.ShapeDtypeStruct(shape, BF16) for shape in carried]
         result = jax.ShapeDtypeStruct((rows, width), BF16)
     return pl.pallas_call(
         functools.partial(plane_sum_kernel, epilogue, wide),
@@ -400,11 +401,11 @@
             pltpu.VMEM((rows, width), BF16),
             pltpu.VMEM((rows, width), BF16),
             pltpu.VMEM((rows, width), BF16),
+            pltpu.SemaphoreType.DMA((8,)),
             pltpu.SemaphoreType.DMA((5,)),
             pltpu.SemaphoreType.DMA((5,)),
-            pltpu.SemaphoreType.DMA((5,)),
-            pltpu.SemaphoreType.DMA((9,)),
-            pltpu.SemaphoreType.DMA((9,)),
+            pltpu.SemaphoreType.DMA((8,)),
+            pltpu.SemaphoreType.DMA((8,)),
         ],
         compiler_params=pltpu.CompilerParams(
             collective_id=collective_id, has_side_effects=True, vmem_limit_bytes=62 << 20
@@ -415,8 +416,8 @@
 
 
 def last_kernel(
-    size, deep, own_in, gain_a, gain_b, rows_in, pair, single, other_in, smalls, gains, rows_out, pair_b, single_out,
-    plane, mine, lines, store, send, recv, small_send, small_recv, plane_send, plane_recv, line_send, line_recv,
+    size, deep, own_in, gain_a, gain_b, rows_in, single, other_in, smalls, gains, rows_out, single_out, plane,
+    mine, lines, store, send, recv, small_send, small_recv, plane_send, plane_recv, line_send, line_recv,
 ):
     thin = smalls.shape[2]
     fsdp, ctx, tp = lax.axis_index("fsdp"), lax.axis_index("ctx"), lax.axis_index("tp")
@@ -430,32 +431,32 @@
     meet(*[away(*d) for d in in_plane + [d for d in across_line if d not in in_plane]])
     core, row, _, across, along, same, _, _ = partners()
     came = (1 - row) * 2 + core
-    units, tall = pair.shape[1] // 2, single.shape[0]
-    cols = pl.ds(pl.multiple_of(ctx * units, 128), units)
+    tall = single.shape[0]
     tall_rows = pl.ds(pl.multiple_of(ctx * tall, 16), tall)
-    high = pair.at[:, pl.ds(units, units)]
     copies = [
         remote(own_in.at[pl.ds(0, deep), :], other_in, send.at[0], recv.at[0], across),
         remote(rows_in, rows_out.at[tp], send.at[1], recv.at[1], along),
         remote(rows_in, rows_out.at[tp], send.at[2], recv.at[2], same),
         remote(rows_out.at[came], rows_out.at[came], send.at[3], recv.at[3], same),
-        remote(high, pair_b.at[:, cols], send.at[4], recv.at[4], across),
-        remote(single, single_out.at[tall_rows, :], send.at[5], recv.at[5], across),
+        remote(single, single_out.at[tall_rows, :], send.at[4], recv.at[4], across),
     ]
     local = [
         pltpu.make_async_copy(rows_in, rows_out.at[tp], store.at[1]),
-        pltpu.make_async_copy(high, pair_b.at[:, cols], store.at[2]),
-        pltpu.make_async_copy(single, single_out.at[tall_rows, :], store.at[3]),
+        pltpu.make_async_copy(single, single_out.at[tall_rows, :], store.at[2]),
     ]
-    for i in (1, 0, 2, 4, 5):
+    for i in (1, 0, 2, 4):
         copies[i].start()
     for copy in local:
         copy.start()
     at = lax.broadcasted_iota(jnp.int32, gains.shape, 0)
-    sum_a = jnp.sum(gain_a[...], axis=0, keepdims=True)
-    sum_b = jnp.sum(gain_b[...], axis=0, keepdims=True)
+    part = jnp.zeros(gains.shape, F32)
+    quarter = gains.shape[1]
+    for k, gain in enumerate((gain_a, gain_b)):
+        for i in range(4):
+            line = jnp.sum(gain[:, i * quarter : (i + 1) * quarter], axis=0, keepdims=True)
+            part = jnp.where(at == 4 * k + i, line, part)
     place = ctx * 4 + tp
-    plane[place] = jnp.where(at == 0, sum_a, jnp.where(at == 1, sum_b, 0.0))
+    plane[place] = part
     sent = [
         remote(plane.at[place], plane.at[place], plane_send.at[i], plane_recv.at[i], away(*d))
         for i, d in enumerate(in_plane)
@@ -496,27 +497,27 @@
         copy.wait()
 
 
-def last(own_in, gain_a, gain_b, rows, pair, single, deep, size, collective_id):
+def last(own_in, gain_a, gain_b, rows, single, deep, size, collective_id):
     width, thin = own_in.shape[1], own_in.shape[0] - deep
+    gains = (8, gain_a.shape[1] // 4)
     vmem = pl.BlockSpec(memory_space=pltpu.VMEM)
     anywhere = pl.BlockSpec(memory_space=pl.ANY)
-    sems = [pltpu.SemaphoreType.DMA((n,)) for n in (4, 6, 6, 2 * size, 2 * size, 8, 8, size, size)]
+    sems = [pltpu.SemaphoreType.DMA((n,)) for n in (3, 5, 5, 2 * size, 2 * size, 8, 8, size, size)]
     return pl.pallas_call(
         functools.partial(last_kernel, size, deep),
-        in_specs=[anywhere] + [vmem] * 5,
-        out_specs=[anywhere, anywhere, vmem, anywhere, anywhere, anywhere],
+        in_specs=[anywhere] + [vmem] * 4,
+        out_specs=[anywhere, anywhere, vmem, anywhere, anywhere],
         out_shape=[
             jax.ShapeDtypeStruct((deep, width), BF16),
             jax.ShapeDtypeStruct((2, size, thin, width), BF16),
-            jax.ShapeDtypeStruct(gain_a.shape, F32),
+            jax.ShapeDtypeStruct(gains, F32),
             jax.ShapeDtypeStruct((4,) + rows.shape, BF16),
-            jax.ShapeDtypeStruct(pair.shape, BF16),
             jax.ShapeDtypeStruct((2 * single.shape[0], single.shape[1]), BF16),
         ],
         scratch_shapes=[
-            pltpu.VMEM((8,) + gain_a.shape, F32),
-            pltpu.VMEM(gain_a.shape, F32),
-            pltpu.VMEM((size,) + gain_a.shape, F32),
+            pltpu.VMEM((8,) + gains, F32),
+            pltpu.VMEM(gains, F32),
+            pltpu.VMEM((size,) + gains, F32),
         ]
         + sems,
         compiler_params=pltpu.CompilerParams(
@@ -524,7 +525,7 @@
         ),
         cost_estimate=pl.CostEstimate(flops=1 << 33, bytes_accessed=4 << 20, transcendentals=0),
         name="last",
-    )(own_in, gain_a, gain_b, rows, pair, single)
+    )(own_in, gain_a, gain_b, rows, single)
 
 
 def scan_rows(a_ref, b_ref, carry, reverse):
@@ -585,7 +586,7 @@
 
 
 def mixer_back_kernel(
-    place, grad_mixed, pre, pre_tail, states, states_tail, recur_in, input_in, conv_in, masks, params, gate_a, gate_x,
+    place, grad_proj, w_out, pre, pre_tail, states, states_tail, recur_in, input_in, conv_in, masks, params, gate_a, gate_x,
     grads, sums, sum_a, sum_x, ext, grad_ext, a_buf, b_buf, carry,
 ):
     rows, width = states.shape
@@ -602,7 +603,7 @@
 
     inside = jnp.where(first, 0.0, 1.0)
     branch, slope = gelu_parts(pre[:, :width])
-    above = grad_mixed[...]
+    above = matmul(grad_proj[...], w_out[...])
     state = states[...]
     grads[:, :width] = (above * state * slope).astype(BF16)
     recur, opened = recur_in[...], input_in[...]
@@ -694,7 +695,7 @@
     )(place, pre, masks, params, gate_a, gate_x)
 
 
-def mixer_back(grad_mixed, pre, states, recur, opened, conv, masks, params, gate_a, gate_x, place, rows):
+def mixer_back(grad_proj, w_out, pre, states, recur, opened, conv, masks, params, gate_a, gate_x, place, rows):
     count, width = states.shape
     steps = count // rows
     last = steps - 1
@@ -714,7 +715,8 @@
             num_scalar_prefetch=1,
             grid=(steps,),
             in_specs=[
-                one, wide, pl.BlockSpec((8, 2 * width), tail), one, pl.BlockSpec((8, width), tail), one, one, one,
+                pl.BlockSpec((rows, grad_proj.shape[1]), spot), pl.BlockSpec(w_out.shape, fixed),
+                wide, pl.BlockSpec((8, 2 * width), tail), one, pl.BlockSpec((8, width), tail), one, one, one,
                 pl.BlockSpec((rows, 8), inorder), pl.BlockSpec((8, width), fixed), gate, gate,
             ],
             out_specs=[wide, pl.BlockSpec((64, width), fixed), gate, gate],
@@ -733,10 +735,10 @@
             jax.ShapeDtypeStruct((width, width), F32),
         ],
         cost_estimate=pl.CostEstimate(
-            flops=count * width * (8 * width + 200), bytes_accessed=count * width * 34, transcendentals=count * width * 4
+            flops=count * width * (8 * width + 2 * grad_proj.shape[1] + 200), bytes_accessed=count * width * 34, transcendentals=count * width * 4
         ),
         name="mixer_back",
-    )(place, grad_mixed, pre, pre, states, states, recur, opened, conv, masks, params, gate_a, gate_x)
+    )(place, grad_proj, w_out, pre, pre, states, states, recur, opened, conv, masks, params, gate_a, gate_x)
 
 
 def on_diagonal(blocks):
@@ -842,15 +844,16 @@
     grad_w_out = left_inner(mixed, grad_proj).astype(BF16)
     grad_proj, own_down, grad_w_out = tied((grad_proj, own_down, grad_w_out))
     own_out = owned(grad_w_out, 1)
-    grad_mixed = matmul(grad_proj, full_out)
     other_down = flip(own_down, 4)
+    low, own_gu, grad_w_out = tied((low, own_gu, grad_w_out))
+    other_gu = flip(own_gu, 4)
     output = (resid + low[:rows] + got_far[:rows].astype(F32) + got_near.astype(F32)).astype(BF16)
     states, output = tied((states, output))
     output_along = flip(output, 2)
     grads_in, sums, sum_a, sum_x = mixer_back(
-        grad_mixed, pre, states, recur, opened, conv, masks, params, diag_a, diag_x, place, rows
-    )
-    grads_in, output_along, other_down, own_gu = tied((grads_in, output_along, other_down, own_gu))
+        grad_proj, full_out, pre, states, recur, opened, conv, masks, params, diag_a, diag_x, place, rows
+    )
+    grads_in, output_along, other_down = tied((grads_in, output_along, other_down))
     lines = jnp.sum(sums.reshape(8, 8, width), axis=1)
     head_at = lax.broadcasted_iota(jnp.int32, (head_width, width), 1) // head_width
     squares = [
@@ -867,13 +870,14 @@
     small = jnp.concatenate([small[:, 0], small[:, 1]], axis=2)
     grad_w_in = left_inner(normed, grads_in).astype(BF16).reshape(fsdp_size, -1, 2 * width)
     grad_w_in = jnp.concatenate([grad_w_in, small], axis=1).reshape(-1, 2 * width)
-    grads_in, grad_w_in, own_out = tied((grads_in, grad_w_in, own_out))
+    grads_in, grad_w_in, own_out, other_gu = tied((grads_in, grad_w_in, own_out, other_gu))
     own_in = owned(grad_w_in, 0)
-    grad_tokens, gain_mix_part, output, own_gate = plane_sum(
-        "back", False, grads_in, full_in, grad_resid, own, gain_mix, 4, 5 << 33, (output, output_along, own_gu)
-    )
-    other_in, smalls, gains, grad_tokens, own_up, own_out = last(
-        own_in, gain_mix_part, gain_mlp_part, grad_tokens, own_gu, own_out, model_width // fsdp_size, fsdp_size, 5
+    moved = (output, output_along, own_gu, other_gu, own_down, other_down)
+    grad_tokens, gain_mix_part, output, own_gate, own_up, own_down = plane_sum(
+        "back", False, grads_in, full_in, grad_resid, own, gain_mix, 4, 5 << 33, moved
+    )
+    other_in, smalls, gains, grad_tokens, own_out = last(
+        own_in, gain_mix_part, gain_mlp_part, grad_tokens, own_out, model_width // fsdp_size, fsdp_size, 5
     )
 
     def both_halves(x, other, axis):
@@ -882,7 +886,6 @@
         return jnp.concatenate([low, high], axis=axis).astype(F32)
 
     own_in = own_in[: model_width // fsdp_size]
-    own_down = both_halves(own_down, other_down, 0)
     smalls = jnp.stack([smalls[..., :width], smalls[..., width:]], axis=2).reshape(2, fsdp_size * part_rows, width)
     smalls = jnp.concatenate([smalls[0], smalls[1]], axis=1).astype(F32)
     lines = smalls[:8]
@@ -897,7 +900,7 @@
     return (
         output.reshape(1, tok_count, model_width),
         grad_tokens.reshape(1, tok_count, model_width),
-        gains[0],
+        gains[:4].reshape(model_width),
         own_branch,
         own_input,
         lines[4:8],
@@ -908,10 +911,10 @@
         lines[2],
         RATE_SCALE * jax.nn.sigmoid(-decay_param) * lines[0],
         own_out.astype(F32),
-        gains[1],
+        gains[4:].reshape(model_width),
         own_gate.astype(F32),
         own_up.astype(F32),
-        own_down,
+        own_down.astype(F32),
     )
 
 

time: 663 us -> 630 us (0.950)
  Pallas kernels: 439 us -> 411 us
  matrix products: 118 us -> 109 us
    pallas_call x1, Pallas kernels: 61.2 us -> 38.4 us  [last(): pl.pallas_call(functools.partial(last_kernel, size, deep), in_specs=[anyw...]
    dot_general x6 -> x5, matrix products: 55.8 us -> 46.8 us  [matmul(): return jnp.dot(left, right, preferred_element_type=F32)]
    pallas_call x3, Pallas kernels: 251 us -> 242 us  [plane_sum(): pl.pallas_call(functools.partial(plane_sum_kernel, epilogue, wide), in_sp...]
  transfers between devices with their start and end apart: 12 -> 13, of which waited for: 3 -> 4; matrix products, arithmetic and copies ran while one was open for 25% -> 25% of each run, Pallas kernels for 57% -> 59%
where the time goes in v5:
time: 630 us; the launch traced here: 627 us
  Pallas kernels  411 us (65%)
  matrix products  109 us (17%)
  other arithmetic  38.1 us (6%)
  local copies, waits for them, and re-layouts  35.9 us (6%)
  between operations  15 us (2%)
  waiting for transfers between devices  13.9 us (2%)
    pallas_call x3, Pallas kernels, plane_sum(): pl.pallas_call(functools.partial(plane_sum_kernel, epilogue, wide), in_sp...  242 us
    pallas_call x1, Pallas kernels, head(): pl.pallas_call(head_kernel, in_specs=[anywhere, anywhere, pl.BlockSpec(me...  79.9 us
    dot_general x5, matrix products, matmul(): return jnp.dot(left, right, preferred_element_type=F32)  46.8 us
    dot_general x4, matrix products, left_inner(): lax.dot_general(left, right, (((0,), (0,)), ((), ())), preferred_element_...  46.3 us
    pallas_call x1, Pallas kernels, last(): pl.pallas_call(functools.partial(last_kernel, size, deep), in_specs=[anyw...  38.4 us
    pallas_call x1, Pallas kernels, mixer_back(): pl.pallas_call(mixer_back_kernel, grid_spec=pltpu.PrefetchScalarGridSpec(...  31.7 us
    pallas_call x1, Pallas kernels, mixer(): pl.pallas_call(mixer_kernel, grid_spec=pltpu.PrefetchScalarGridSpec(num_s...  19 us
    dot_general x1, matrix products, right_inner(): lax.dot_general(left, right, (((1,), (1,)), ((), ())), preferred_element_...  15.9 us
  transfers between devices with their start and end apart: 13, of which 4 were waited for; matrix products, arithmetic and copies ran while one was open for 25% of the time, Pallas kernels for 59%

profile of v5, /device:TPU:0, one launch (start us, length us, event | category | flops | bytes accessed | tf_op | source)
XLA Modules:
  0.0 627.1 jit_solution(3039252730710825307)
XLA Ops:
  8.6 1.7 constant_dynamic-slice_fusion.4
  10.3 1.3 pad_maximum_fusion.2
  11.6 1.2 constant_dynamic-slice_fusion
  13.0 1.3 pad_maximum_fusion.1
  17.7 2.3 dynamic-slice_bitcast_fusion.1.base.source
  20.0 2.4 dynamic-slice_bitcast_fusion.base
  22.5 1.2 fusion.39.place
  23.7 1.8 dynamic_update_slice.13.gate_a
  25.5 1.6 dynamic_update_slice.15.gate_x
  27.1 79.9 %head.1 = (bf16[8,256,2048]{2,1,0:T(8,128)(2,1)}, bf16[8,256,2048]{2,1,0:T(8,128)(2,1)}) custom-call(bf16[1024,2048]{1,0:T(8,128)(2,1)} %bitcast.96, bf16[1024,2048]{1,0:T(8,128)(2,1)} %bitcast.97, f32[1,2048]{1,0:T(1,128)} %bitcast.103), custom_call_target="tpu_custom_call" | custom-call | flops 42949672960 | bytes 67108864 | tf_op jit(solution)/shard_map/head/pallas_call | solution.py:210
  107.7 11.3 %fusion.40.pre.pre_tail = f32[2048,640]{1,0:T(8,128)} fusion(bf16[2048,2048]{1,0:T(8,128)(2,1)} %bitcast.105, bf16[2048,960]{1,0:T(8,128)(2,1)} %all-gather.6.cloned.1.call-done), kind=kOutput, calls=%fused_computation.115 | convolution fusion | flops 5368709120 | bytes 16252928 | tf_op jit(solution)/shard_map/dot_general | solution.py:21
  119.0 19.0 %mixer.1 = (bf16[2048,320]{1,0:T(8,128)(2,1)}, f32[2048,320]{1,0:T(8,128)}, f32[2048,320]{1,0:T(8,128)}, f32[2048,320]{1,0:T(8,128)}, bf16[2048,320]{1,0:T(8,128)(2,1)}) custom-call(s32[8]{0:T(128)} %fusion.39.place, f32[2048,640]{1,0:T(8,128)} %fusion.40.pre.pre_tail, f32[2048,8]{1,0:T(8,128)} %convert_element_type.77.masks, f32[8,320]{1,0:T(8,128)} %concatenate.32.params, ...), custom_call_target="tpu_custom_call" | custom-call | flops 917504000 | bytes 15728640 | tf_op jit(solution)/shard_map/mixer/pallas_call | solution.py:674
  138.0 2.7 slice.230.right.w_out
  140.8 90.0 %plane_sum.3 = (bf16[8,256,2048]{2,1,0:T(8,128)(2,1)}, f32[256,2048]{1,0:T(8,128)}) custom-call(bf16[2048,320]{1,0:T(8,128)(2,1)} %get-tuple-element.74.left, bf16[2048,320]{1,0:T(8,128)(2,1)} %slice.230.right.w_out, bf16[256,2048]{1,0:T(8,128)(2,1)} %dynamic-slice_bitcast_fusion.1.base.source, bf16[256,2048]{1,0:T(8,128)(2,1)} %dynamic-slice_bitcast_fusion.1.base.source, ...), custom_call_target="tpu_custom_call" | custom-call | flops 77309411328 | bytes 4194304 | tf_op jit(solution)/shard_map/plane_sum/pallas_call | solution.py:390
  230.7 3.5 slice.229.right
  234.2 17.4 %fusion.42 = f32[2048,1536]{1,0:T(8,128)S(1)} fusion(bf16[2048,2048]{1,0:T(8,128)(2,1)} %bitcast.109, bf16[2048,1536]{1,0:T(8,128)(2,1)} %all-gather.8.cloned.1.call-done.right), kind=kOutput, calls=%fused_computation.117 | convolution fusion | flops 12884901888 | bytes 27262976 | tf_op jit(solution)/shard_map/dot_general | solution.py:21
  251.6 2.6 multiply_convert_fusion.1
  254.3 1.9 copy-done.7
  256.2 1.7 copy-done.11
  257.9 10.5 %convolution_convert_fusion.2 = bf16[768,2048]{1,0:T(8,128)(2,1)} fusion(bf16[2048,768]{1,0:T(8,128)(2,1)S(1)} %multiply_convert_fusion.1, bf16[2048,2048]{1,0:T(8,128)(2,1)} %bitcast.107), kind=kOutput, calls=%fused_computation.21 | convolution fusion | flops 6444023808 | bytes 14680064 | tf_op jit(solution)/shard_map/dot_general | solution.py:25
  268.3 6.6 %all-gather.4.cloned.1.call-done = bf16[768,2048]{1,0:T(8,128)(2,1)} async-done(((bf16[768,512]{1,0:T(8,128)(2,1)}), bf16[768,2048]{1,0:T(8,128)(2,1)}) %all-gather.4.cloned.1.call-update) | async-done | bytes 3145744 | tf_op jit(solution)/shard_map/all_gather | solution.py:773
  275.0 7.9 %convolution_convert_fusion.1 = bf16[1024,2048]{1,0:T(8,128)(2,1)} fusion(bf16[768,2048]{1,0:T(8,128)(2,1)} %all-gather.4.cloned.1.call-done, bf16[2048,768]{1,0:T(8,128)(2,1)} %copy-done.11), kind=kOutput, calls=%fused_computation.20 | convolution fusion | flops 3223322624 | bytes 8912896 | tf_op jit(solution)/shard_map/dot_general | solution.py:21
  282.9 15.9 %fusion.9 = (bf16[2048,768]{1,0:T(8,128)(2,1)S(1)}, bf16[2048,768]{1,0:T(8,128)(2,1)S(1)}) fusion(f32[2048,1536]{1,0:T(8,128)} %copy-done.7, bf16[2048,2048]{1,0:T(8,128)(2,1)} %bitcast.108, bf16[768,2048]{1,0:T(8,128)(2,1)S(1)} %copy-done.28), kind=kOutput, calls=%fused_computation.12 | convolution fusion | flops 6478626816 | bytes 30408704 | tf_op jit(solution)/shard_map/dot_general | solution.py:29
  298.8 1.6 copy-done.9
  301.5 17.7 %convolution_convert_fusion = bf16[2048,1536]{1,0:T(8,128)(2,1)} fusion(bf16[2048,2048]{1,0:T(8,128)(2,1)} %bitcast.110, bf16[2048,768]{1,0:T(8,128)(2,1)S(1)} %get-tuple-element.132, bf16[2048,768]{1,0:T(8,128)(2,1)S(1)} %get-tuple-element.131), kind=kOutput, calls=%fused_computation.2 | convolution fusion | flops 12900630528 | bytes 20971520 | tf_op jit(solution)/shard_map/dot_general | solution.py:25
  319.6 6.1 pad_maximum_fusion.left
  326.7 4.8 add_convert_fusion
  331.5 1.5 collective-permute-start.1
  333.0 5.4 convert_add_fusion
  338.4 98.5 %plane_sum.4 = (bf16[8,256,2048]{2,1,0:T(8,128)(2,1)}, f32[256,2048]{1,0:T(8,128)}, f32[8,2048]{1,0:T(8,128)}) custom-call(bf16[2048,1536]{1,0:T(8,128)(2,1)} %pad_maximum_fusion.left, bf16[2048,1536]{1,0:T(8,128)(2,1)} %all-gather.8.cloned.1.call-done.right, bf16[256,2048]{1,0:T(8,128)(2,1)} %dynamic-slice_bitcast_fusion.base, ...), custom_call_target="tpu_custom_call" | custom-call | flops 77309411328 | bytes 4194304 | tf_op jit(solution)/shard_map/plane_sum/pallas_call | solution.py:390
  436.9 2.3 add_convert_fusion.2
  439.9 7.5 %convolution_convert_fusion.4 = bf16[320,2048]{1,0:T(8,128)(2,1)} fusion(bf16[2048,320]{1,0:T(8,128)(2,1)S(1)} %copy-done.32, bf16[2048,2048]{1,0:T(8,128)(2,1)} %bitcast.84), kind=kOutput, calls=%fused_computation.24 | convolution fusion | flops 2685009920 | bytes 11010048 | tf_op jit(solution)/shard_map/dot_general | solution.py:25
  449.0 5.0 collective-permute-done.2
  454.1 3.1 add_convert_fusion.1.refs_0_
  458.1 31.7 %mixer_back.1 = (bf16[2048,640]{1,0:T(8,128)(2,1)}, f32[64,320]{1,0:T(8,128)}, f32[320,320]{1,0:T(8,128)}, f32[320,320]{1,0:T(8,128)}) custom-call(s32[8]{0:T(128)} %fusion.39.place, bf16[2048,2048]{1,0:T(8,128)(2,1)} %bitcast.85, bf16[2048,320]{1,0:T(8,128)(2,1)} %slice.230.right.w_out, f32[2048,640]{1,0:T(8,128)} %fusion.40.pre.pre_tail, ...), custom_call_target="tpu_custom_call" | custom-call | flops 4493148160 | bytes 22282240 | tf_op jit(solution)/shard_map/mixer_back/pallas_call | solution.py:712
  489.9 1.4 fusion.26
  492.4 10.6 %convolution_convert_fusion.3 = bf16[2048,640]{1,0:T(8,128)(2,1)S(1)} fusion(bf16[2048,2048]{1,0:T(8,128)(2,1)} %bitcast.106, bf16[2048,640]{1,0:T(8,128)(2,1)} %get-tuple-element.107.left), kind=kOutput, calls=%fused_computation.22 | convolution fusion | flops 5370019840 | bytes 13631488 | tf_op jit(solution)/shard_map/dot_general | solution.py:25
  503.1 1.9 maximum_maximum_fusion
  505.0 53.6 %plane_sum.5 = (bf16[256,2048]{1,0:T(8,128)(2,1)}, f32[8,2048]{1,0:T(8,128)}, bf16[4,256,2048]{2,1,0:T(8,128)(2,1)}, bf16[512,1536]{1,0:T(8,128)(2,1)}, bf16[512...) custom-call(bf16[2048,640]{1,0:T(8,128)(2,1)} %get-tuple-element.107.left, bf16[2048,640]{1,0:T(8,128)(2,1)} %slice.229.right, ...), custom_call_target="tpu_custom_call" | custom-call | flops 42949672960 | bytes 4194304 | tf_op jit(solution)/shard_map/plane_sum/pallas_call | solution.py:390
  558.6 3.6 convert_element_type.99
  562.3 2.1 convert_element_type.100
  564.3 2.1 convert_element_type.101
  567.6 38.4 %last.1 = (bf16[512,640]{1,0:T(8,128)(2,1)S(1)}, bf16[2,4,48,640]{3,2,1,0:T(8,128)(2,1)S(1)}, f32[8,512]{1,0:T(8,128)S(1)}, bf16[4,256,2048]{2,1,0:T(8,128)(2,1)S(1)}, bf16[640,512]{1,0:T(8,128)(2,1)S(1)}) custom-call(bf16[560,640]{1,0:T(8,128)(2,1)S(1)} %copy-done.2, f32[8,2048]{1,0:T(8,128)S(1)} %copy-done.6, f32[8,2048]{1,0:T(8,128)S(1)} %copy-done.5, ...), custom_call_target="tpu_custom_call" | custom-call | flops 8589934592 | bytes 4194304 | tf_op jit(solution)/shard_map/last/pallas_call | solution.py:506
  609.5 1.2 convert_element_type.98
  611.7 1.3 maximum_convert_fusion
  613.0 1.3 maximum_convert_fusion.1
  616.0 2.0 copy.79
  618.0 2.0 copy.80
  (143 shorter events, 19.6 us)
Async XLA Ops:
  7.2 7.1 %copy-start = (bf16[1536,512]{1,0:T(8,128)(2,1)S(1)}, bf16[1536,512]{1,0:T(8,128)(2,1)}, u32[]{:S(2)}) copy-start(bf16[1536,512]{1,0:T(8,128)(2,1)} %param.36) | copy-start | bytes 4718596
  7.2 100.5 %all-gather.6.cloned.1.call-start = ((), (), s32[]{:S(2)}) async-start(), calls=%async_computation.5 | async-start | bytes 5242880 | tf_op jit(solution)/shard_map/all_gather | solution.py:770
  8.6 3.0 copy-start.18
  11.6 222.6 %all-gather.8.cloned.1.call-start = ((), (), s32[]{:S(2)}) async-start(), calls=%async_computation.6 | async-start | bytes 7864320 | tf_op jit(solution)/shard_map/all_gather | solution.py:772
  12.9 2.5 copy-start.23
  12.9 4.3 copy-start.24
  12.9 4.4 copy-start.25
  12.9 4.4 copy-start.26
  12.9 4.5 copy-start.27
  12.9 4.6 copy-start.21
  12.9 4.7 copy-start.19
  13.0 4.7 copy-start.20
  14.3 260.6 %all-gather.4.cloned.1.call-start = ((), (), s32[]{:S(2)}) async-start(), calls=%async_computation.4 | async-start | bytes 3932160 | tf_op jit(solution)/shard_map/all_gather | solution.py:773
  15.3 432.1 %reduce-scatter.5.cloned.1.call-start = ((), (), s32[]{:S(2)}) async-start(), calls=%async_computation.7 | async-start | bytes 3932160 | tf_op jit(solution)/shard_map/reduce_scatter | solution.py:764
  25.4 81.6 %copy-start.17 = (bf16[320,320]{1,0:T(8,128)(2,1)}, bf16[320,320]{1,0:T(8,128)(2,1)S(1)}, u32[]{:S(2)}) copy-start(bf16[320,320]{1,0:T(8,128)(2,1)S(1)} %dynamic_update_slice.13.gate_a) | copy-start | bytes 614404
  27.1 80.0 %copy-start.16 = (bf16[320,320]{1,0:T(8,128)(2,1)}, bf16[320,320]{1,0:T(8,128)(2,1)S(1)}, u32[]{:S(2)}) copy-start(bf16[320,320]{1,0:T(8,128)(2,1)S(1)} %dynamic_update_slice.15.gate_x) | copy-start | bytes 614404
  251.6 4.6 copy-start.7
  256.2 1.7 copy-start.11
  274.9 174.1 %reduce-scatter.7.cloned.1.call-start = ((), (), s32[]{:S(2)}) async-start(), calls=%async_computation.8 | async-start | bytes 7864320 | tf_op jit(solution)/shard_map/reduce_scatter | solution.py:764
  275.0 8.0 %copy-start.28 = (bf16[768,2048]{1,0:T(8,128)(2,1)S(1)}, bf16[768,2048]{1,0:T(8,128)(2,1)}, u32[]{:S(2)}) copy-start(bf16[768,2048]{1,0:T(8,128)(2,1)} %all-gather.4.cloned.1.call-done) | copy-start | bytes 9437188
  298.8 1.6 copy-start.9
  298.8 2.7 copy-start.10
  319.2 7.5 %collective-permute-start = (bf16[1024,2048]{1,0:T(8,128)(2,1)}, bf16[1024,2048]{1,0:T(8,128)(2,1)}, u32[]{:S(2)}, u32[]{:S(2)}) collective-permute-start(bf16[1024,2048]{1,0:T(8,128)(2,1)} %convolution_convert_fusion.1), channel_id=1, source_target_pairs={{0,1},{1,0},{2,3},{3,2},{4,5},{5,4},{6,7},{7,6},{8,9},{9,8},{10,11... | collective-permute-start | bytes 12582920 | tf_op jit(solution)/shard_map/ppermute | solution.py:70
  319.3 185.7 %reduce-scatter.9.cloned.1.call-start = ((), (), s32[]{:S(2)}) async-start(), calls=%async_computation.9 | async-start | bytes 1638400 | tf_op jit(solution)/shard_map/reduce_scatter | solution.py:764
  319.6 7.2 %copy-start.12 = (bf16[2048,768]{1,0:T(8,128)(2,1)S(1)}, bf16[2048,768]{1,0:T(8,128)(2,1)}, u32[]{:S(2)}) copy-start(bf16[2048,768]{1,0:T(8,128)(2,1)} %copy-done.11) | copy-start | bytes 9437188
  319.6 7.2 %copy-start.29 = (bf16[768,2048]{1,0:T(8,128)(2,1)S(1)}, bf16[768,2048]{1,0:T(8,128)(2,1)}, u32[]{:S(2)}) copy-start(bf16[768,2048]{1,0:T(8,128)(2,1)} %all-gather.4.cloned.1.call-done) | copy-start | bytes 9437188
  331.5 105.4 %collective-permute-start.1 = (bf16[512,2048]{1,0:T(8,128)(2,1)}, bf16[512,2048]{1,0:T(8,128)(2,1)}, u32[]{:S(2)}, u32[]{:S(2)}) collective-permute-start(bf16[512,2048]{1,0:T(8,128)(2,1)} %add_convert_fusion), channel_id=1, source_target_pairs={{0,4},{1,3},{2,6},{3,1},{4,0},{5,7},{6,2},{7,5},{8,12},{9,11},{10,... | collective-permute-start | bytes 6291464 | tf_op jit(solution)/shard_map/ppermute | solution.py:70
  436.9 2.9 copy-start.32
  439.2 14.9 %collective-permute-start.2 = (bf16[256,2048]{1,0:T(8,128)(2,1)S(1)}, bf16[256,2048]{1,0:T(8,128)(2,1)S(1)}, u32[]{:S(2)}, u32[]{:S(2)}) collective-permute-start(bf16[256,2048]{1,0:T(8,128)(2,1)S(1)} %add_convert_fusion.2), channel_id=1, source_target_pairs={{0,2},{1,5},{2,0},{3,7},{4,6},{5,1},{6,4},{7,3},{8,10},{9,13},{10,... | collective-permute-start | bytes 3145736 | tf_op jit(solution)/shard_map/ppermute | solution.py:70
  447.3 45.0 %collective-permute-start.4 = (bf16[768,512]{1,0:T(8,128)(2,1)}, bf16[768,512]{1,0:T(8,128)(2,1)S(1)}, u32[]{:S(2)}, u32[]{:S(2)}) collective-permute-start(bf16[768,512]{1,0:T(8,128)(2,1)} %reduce-scatter.5.cloned.1.call-done.refs_4_), channel_id=1, source_target_pairs={{0,4},{1,5},{2,6},{3,7},{4,0},{5,1},{6,2},{7,3},{8,12},{9,13},{10,... | collective-permute-start | bytes 2359304 | tf_op jit(solution)/shard_map/ppermute | solution.py:74
  447.7 118.7 %reduce-scatter.11.cloned.1.call-start = ((), (), s32[]{:S(2)}) async-start(), calls=%async_computation.10 | async-start | bytes 3584000 | tf_op jit(solution)/shard_map/reduce_scatter | solution.py:764
  457.2 32.7 %copy-start.15 = (bf16[256,2048]{1,0:T(8,128)(2,1)}, bf16[256,2048]{1,0:T(8,128)(2,1)S(1)}, u32[]{:S(2)}) copy-start(bf16[256,2048]{1,0:T(8,128)(2,1)S(1)} %add_convert_fusion.1.refs_0_) | copy-start | bytes 3145732
  457.2 35.2 %collective-permute-start.3 = (bf16[256,2048]{1,0:T(8,128)(2,1)S(1)}, bf16[256,2048]{1,0:T(8,128)(2,1)S(1)}, u32[]{:S(2)}, u32[]{:S(2)}) collective-permute-start(bf16[256,2048]{1,0:T(8,128)(2,1)S(1)} %add_convert_fusion.1.refs_0_), channel_id=1, source_target_pairs={{0,2},{1,3},{2,0},{3,1},{4,6},{5,7},{6,4},{7,5},{8,10},{9,11},{10,... | collective-permute-start | bytes 3145736 | tf_op jit(solution)/shard_map/ppermute | solution.py:74
  457.8 47.1 %collective-permute-start.5 = (bf16[512,1536]{1,0:T(8,128)(2,1)}, bf16[512,1536]{1,0:T(8,128)(2,1)}, u32[]{:S(2)}, u32[]{:S(2)}) collective-permute-start(bf16[512,1536]{1,0:T(8,128)(2,1)} %reduce-scatter.7.cloned.1.call-done.refs_2_), channel_id=1, source_target_pairs={{0,4},{1,5},{2,6},{3,7},{4,0},{5,1},{6,2},{7,3},{8,12},{9,13},{10,... | collective-permute-start | bytes 4718600 | tf_op jit(solution)/shard_map/ppermute | solution.py:74
  492.4 10.7 %copy-start.31 = (bf16[768,512]{1,0:T(8,128)(2,1)}, bf16[768,512]{1,0:T(8,128)(2,1)S(1)}, u32[]{:S(2)}) copy-start(bf16[768,512]{1,0:T(8,128)(2,1)S(1)} %collective-permute-done.4.refs_5_) | copy-start | bytes 2359300
  492.4 10.7 %copy-start.30 = (bf16[256,2048]{1,0:T(8,128)(2,1)}, bf16[256,2048]{1,0:T(8,128)(2,1)S(1)}, u32[]{:S(2)}) copy-start(bf16[256,2048]{1,0:T(8,128)(2,1)S(1)} %collective-permute-done.3.refs_1_) | copy-start | bytes 3145732
  558.6 3.7 copy-start.14
  558.6 5.7 copy-start.13
  562.2 4.2 copy-start.3
  562.2 4.2 copy-start.4
  562.3 4.2 copy-start.5
  562.3 4.2 copy-start.6
  566.5 1.1 copy-start.2
  606.2 2.7 copy-start.22
  611.7 4.4 copy-start.8
  616.0 4.0 copy-start.1
Sparse Core Ops, SparseCore 0:
  11.7 83.3 all-gather.5
  97.2 113.8 all-gather.7
  213.2 61.6 all-gather.3
  277.1 59.0 reduce-scatter.4
  338.3 110.6 reduce-scatter.6
  451.8 31.8 reduce-scatter.8
  505.1 56.3 reduce-scatter.10

commit v6 on v5

--- a/solution.py
+++ b/solution.py
@@ -228,15 +228,17 @@
 
 
 def plane_sum_kernel(
-    epilogue, wide, left, right, base, source, gain, *refs
+    epilogue, wide, parts, *refs
 ):
+    lefts, (right, base, source, gain), refs = refs[:parts], refs[parts : parts + 4], refs[parts + 4 :]
     if epilogue == "norm":
         out, kept_out, refs = refs[0], refs[1], refs[2:]
     elif wide:
         out, kept_out, gain_out, refs = refs[0], refs[1], refs[2], refs[3:]
     else:
-        rows_in, rows_along, pair, pair_far, stack, stack_far, out, gain_out, rows_out, pair_a, pair_b, stack_out = refs[:12]
-        refs = refs[12:]
+        rows_in, rows_along, pair, pair_far, stack, stack_far, single = refs[:7]
+        out, gain_out, rows_out, pair_a, pair_b, stack_out, single_out = refs[7:14]
+        refs = refs[14:]
     to_core, from_core, acc, to_far, from_far, to_near, from_near, own, store, send, recv, gsend, grecv = refs
     rows, width = own.shape
     if not wide:
@@ -248,7 +250,10 @@
     def products(row, ref, at):
         def turn(i, _):
             cols = pl.ds(pl.multiple_of(i * tile, tile), tile)
-            part = right_inner(left[pl.ds(row, 2 * rows), :], right[cols, :])
+            part, start = 0.0, 0
+            for left in lefts:
+                part = part + right_inner(left[pl.ds(row, 2 * rows), :], right[cols, start : start + left.shape[1]])
+                start += left.shape[1]
             ref[pl.ds(at, 2 * rows), cols] = part.astype(ref.dtype)
             return 0
 
@@ -272,7 +277,10 @@
             remote(rows_in, rows_out.at[tp], gsend.at[0], grecv.at[0], same),
             remote(rows_along, rows_out.at[came], gsend.at[1], grecv.at[1], same),
         ]
-        places = [(rows_in, rows_out.at[tp]), (rows_along, rows_out.at[came])]
+        single_rows = pl.ds(pl.multiple_of(half_at * single.shape[0], 16), single.shape[0])
+        carried.append(remote(single, single_out.at[single_rows, :], gsend.at[2], grecv.at[2], across))
+        carried[2].start()
+        places = [(rows_in, rows_out.at[tp]), (rows_along, rows_out.at[came]), (single, single_out.at[single_rows, :])]
         for at, halves, block in ((half_at, pair, stack), (1 - half_at, pair_far, stack_far)):
             cols = pl.ds(pl.multiple_of(at * units, 128), units)
             places.append((halves.at[:, pl.ds(0, units)], pair_a.at[:, cols]))
@@ -372,8 +380,8 @@
         copy.wait()
 
 
-def plane_sum(epilogue, wide, left, right, base, source, gain, collective_id, cost, extra_in=()):
-    count, width = left.shape[0], right.shape[0]
+def plane_sum(epilogue, wide, lefts, right, base, source, gain, collective_id, cost, extra_in=()):
+    count, width = lefts[0].shape[0], right.shape[0]
     rows = count // 8
     vmem = pl.BlockSpec(memory_space=pltpu.VMEM)
     anywhere = pl.BlockSpec(memory_space=pl.ANY)
@@ -383,13 +391,14 @@
     carried = []
     result = jax.ShapeDtypeStruct((8, rows, width), BF16)
     if not wide:
-        _, _, pair, _, stack, _ = extra_in
-        carried = [(4, rows, width), pair.shape, pair.shape, (2 * stack.shape[0], stack.shape[1])]
+        _, _, pair, _, stack, _, single = extra_in
+        carried = [(4, rows, width), pair.shape, pair.shape]
+        carried += [(2 * block.shape[0], block.shape[1]) for block in (stack, single)]
         carried = [jax.ShapeDtypeStruct(shape, BF16) for shape in carried]
         result = jax.ShapeDtypeStruct((rows, width), BF16)
     return pl.pallas_call(
-        functools.partial(plane_sum_kernel, epilogue, wide),
-        in_specs=[vmem] * (5 + len(extra_in)),
+        functools.partial(plane_sum_kernel, epilogue, wide, len(lefts)),
+        in_specs=[vmem] * (len(lefts) + 4 + len(extra_in)),
         out_specs=[anywhere if wide else vmem] + [vmem] * len(extra) + [anywhere] * len(carried),
         out_shape=[result] + extra + carried,
         scratch_shapes=[
@@ -401,7 +410,7 @@
             pltpu.VMEM((rows, width), BF16),
             pltpu.VMEM((rows, width), BF16),
             pltpu.VMEM((rows, width), BF16),
-            pltpu.SemaphoreType.DMA((8,)),
+            pltpu.SemaphoreType.DMA((9,)),
             pltpu.SemaphoreType.DMA((5,)),
             pltpu.SemaphoreType.DMA((5,)),
             pltpu.SemaphoreType.DMA((8,)),
@@ -412,11 +421,11 @@
         ),
         cost_estimate=pl.CostEstimate(flops=cost, bytes_accessed=count * width, transcendentals=0),
         name="plane_sum",
-    )(left, right, base, source, gain, *extra_in)
+    )(*lefts, right, base, source, gain, *extra_in)
 
 
 def last_kernel(
-    size, deep, own_in, gain_a, gain_b, rows_in, single, other_in, smalls, gains, rows_out, single_out, plane,
+    size, deep, own_in, gain_a, gain_b, rows_in, other_in, smalls, gains, rows_out, plane,
     mine, lines, store, send, recv, small_send, small_recv, plane_send, plane_recv, line_send, line_recv,
 ):
     thin = smalls.shape[2]
@@ -431,20 +440,16 @@
     meet(*[away(*d) for d in in_plane + [d for d in across_line if d not in in_plane]])
     core, row, _, across, along, same, _, _ = partners()
     came = (1 - row) * 2 + core
-    tall = single.shape[0]
-    tall_rows = pl.ds(pl.multiple_of(ctx * tall, 16), tall)
     copies = [
         remote(own_in.at[pl.ds(0, deep), :], other_in, send.at[0], recv.at[0], across),
         remote(rows_in, rows_out.at[tp], send.at[1], recv.at[1], along),
         remote(rows_in, rows_out.at[tp], send.at[2], recv.at[2], same),
         remote(rows_out.at[came], rows_out.at[came], send.at[3], recv.at[3], same),
-        remote(single, single_out.at[tall_rows, :], send.at[4], recv.at[4], across),
     ]
     local = [
         pltpu.make_async_copy(rows_in, rows_out.at[tp], store.at[1]),
-        pltpu.make_async_copy(single, single_out.at[tall_rows, :], store.at[2]),
     ]
-    for i in (1, 0, 2, 4):
+    for i in (1, 0, 2):
         copies[i].start()
     for copy in local:
         copy.start()
@@ -497,22 +502,21 @@
         copy.wait()
 
 
-def last(own_in, gain_a, gain_b, rows, single, deep, size, collective_id):
+def last(own_in, gain_a, gain_b, rows, deep, size, collective_id):
     width, thin = own_in.shape[1], own_in.shape[0] - deep
     gains = (8, gain_a.shape[1] // 4)
     vmem = pl.BlockSpec(memory_space=pltpu.VMEM)
     anywhere = pl.BlockSpec(memory_space=pl.ANY)
-    sems = [pltpu.SemaphoreType.DMA((n,)) for n in (3, 5, 5, 2 * size, 2 * size, 8, 8, size, size)]
+    sems = [pltpu.SemaphoreType.DMA((n,)) for n in (2, 4, 4, 2 * size, 2 * size, 8, 8, size, size)]
     return pl.pallas_call(
         functools.partial(last_kernel, size, deep),
-        in_specs=[anywhere] + [vmem] * 4,
-        out_specs=[anywhere, anywhere, vmem, anywhere, anywhere],
+        in_specs=[anywhere] + [vmem] * 3,
+        out_specs=[anywhere, anywhere, vmem, anywhere],
         out_shape=[
             jax.ShapeDtypeStruct((deep, width), BF16),
             jax.ShapeDtypeStruct((2, size, thin, width), BF16),
             jax.ShapeDtypeStruct(gains, F32),
             jax.ShapeDtypeStruct((4,) + rows.shape, BF16),
-            jax.ShapeDtypeStruct((2 * single.shape[0], single.shape[1]), BF16),
         ],
         scratch_shapes=[
             pltpu.VMEM((8,) + gains, F32),
@@ -525,7 +529,7 @@
         ),
         cost_estimate=pl.CostEstimate(flops=1 << 33, bytes_accessed=4 << 20, transcendentals=0),
         name="last",
-    )(own_in, gain_a, gain_b, rows, single)
+    )(own_in, gain_a, gain_b, rows)
 
 
 def scan_rows(a_ref, b_ref, carry, reverse):
@@ -803,7 +807,7 @@
 
     pre = matmul(normed, full_in)
     mixed, states, recur, opened, conv = mixer(pre, masks, params, diag_a, diag_x, place, rows)
-    normed_mlp, resid = plane_sum("norm", True, mixed, full_out, own, own, gain_mlp, 2, 9 << 33)
+    normed_mlp, resid = plane_sum("norm", True, [mixed], full_out, own, own, gain_mlp, 2, 9 << 33)
     normed_mlp = normed_mlp.reshape(length, model_width)
 
     both = matmul(normed_mlp, full_gu)
@@ -815,17 +819,12 @@
     own_down = owned(grad_w_down, 1)
 
     grad_hidden = right_inner(cot, full_down)
-    grad_both = jnp.concatenate(
-        [
-            (grad_hidden * up_pre * gate_slope).astype(BF16),
-            (grad_hidden * gate_act).astype(BF16),
-        ],
-        axis=1,
-    )
-    grad_w_gu = left_inner(normed_mlp, grad_both).astype(BF16)
+    grad_both = [(grad_hidden * up_pre * gate_slope).astype(BF16), (grad_hidden * gate_act).astype(BF16)]
+    grad_both, hidden = tied((grad_both, hidden))
     half = length // 2
     sent = matmul(hidden[half:], full_down).astype(BF16)
-    grad_w_gu, sent = tied((grad_w_gu, sent))
+    grad_both, sent = tied((grad_both, sent))
+    grad_w_gu = left_inner(normed_mlp, jnp.concatenate(grad_both, axis=1)).astype(BF16)
     own_gu = owned(grad_w_gu, 0)
     got = exchange(sent, "core")
     grad_both, got, grad_w_gu = tied((grad_both, got, grad_w_gu))
@@ -872,12 +871,12 @@
     grad_w_in = jnp.concatenate([grad_w_in, small], axis=1).reshape(-1, 2 * width)
     grads_in, grad_w_in, own_out, other_gu = tied((grads_in, grad_w_in, own_out, other_gu))
     own_in = owned(grad_w_in, 0)
-    moved = (output, output_along, own_gu, other_gu, own_down, other_down)
-    grad_tokens, gain_mix_part, output, own_gate, own_up, own_down = plane_sum(
-        "back", False, grads_in, full_in, grad_resid, own, gain_mix, 4, 5 << 33, moved
-    )
-    other_in, smalls, gains, grad_tokens, own_out = last(
-        own_in, gain_mix_part, gain_mlp_part, grad_tokens, own_out, model_width // fsdp_size, fsdp_size, 5
+    moved = (output, output_along, own_gu, other_gu, own_down, other_down, own_out)
+    grad_tokens, gain_mix_part, output, own_gate, own_up, own_down, own_out = plane_sum(
+        "back", False, [grads_in], full_in, grad_resid, own, gain_mix, 4, 5 << 33, moved
+    )
+    other_in, smalls, gains, grad_tokens = last(
+        own_in, gain_mix_part, gain_mlp_part, grad_tokens, model_width // fsdp_size, fsdp_size, 5
     )
 
     def both_halves(x, other, axis):

time: 630 us -> 623 us (0.989)
    reduce_scatter x4, waiting for transfers between devices: 1.06 us -> 11.5 us  [owned(): return lax.psum_scatter(x, 'fsdp', scatter_dimension=axis, tiled=True)]
  transfers between devices with their start and end apart: 13 -> 13, of which waited for: 4 -> 2; matrix products, arithmetic and copies ran while one was open for 25% -> 24% of each run, Pallas kernels for 59% -> 60%
where the time goes in v6:
time: 623 us; the launch traced here: 619 us
  Pallas kernels  407 us (65%)
  matrix products  108 us (17%)
  local copies, waits for them, and re-layouts  33.2 us (5%)
  other arithmetic  32 us (5%)
  waiting for transfers between devices  18.2 us (3%)
  between operations  15 us (2%)
  starting transfers between devices  6.27 us (1%)
    pallas_call x3, Pallas kernels, plane_sum(): pl.pallas_call(functools.partial(plane_sum_kernel, epilogue, wide, len(le...  242 us
    pallas_call x1, Pallas kernels, head(): pl.pallas_call(head_kernel, in_specs=[anywhere, anywhere, pl.BlockSpec(me...  79.9 us
    dot_general x4, matrix products, left_inner(): lax.dot_general(left, right, (((0,), (0,)), ((), ())), preferred_element_...  46.3 us
    dot_general x5, matrix products, matmul(): return jnp.dot(left, right, preferred_element_type=F32)  45.4 us
    pallas_call x1, Pallas kernels, last(): pl.pallas_call(functools.partial(last_kernel, size, deep), in_specs=[anyw...  34.3 us
    pallas_call x1, Pallas kernels, mixer_back(): pl.pallas_call(mixer_back_kernel, grid_spec=pltpu.PrefetchScalarGridSpec(...  31.9 us
    pallas_call x1, Pallas kernels, mixer(): pl.pallas_call(mixer_kernel, grid_spec=pltpu.PrefetchScalarGridSpec(num_s...  19 us
    dot_general x1, matrix products, right_inner(): lax.dot_general(left, right, (((1,), (1,)), ((), ())), preferred_element_...  16.2 us
  transfers between devices with their start and end apart: 13, of which 2 were waited for; matrix products, arithmetic and copies ran while one was open for 24% of the time, Pallas kernels for 60%

profile of v6, /device:TPU:0, one launch (start us, length us, event | category | flops | bytes accessed | tf_op | source)
XLA Modules:
  0.0 619.4 jit_solution(1726265781367985347)
XLA Ops:
  8.6 1.7 constant_dynamic-slice_fusion.4
  10.3 1.3 pad_maximum_fusion.1
  11.6 1.2 constant_dynamic-slice_fusion
  13.0 1.3 pad_maximum_fusion
  17.7 2.3 dynamic-slice_bitcast_fusion.1.refs_2_.refs_3_
  20.0 2.4 dynamic-slice_bitcast_fusion.refs_3_
  22.5 1.8 dynamic_update_slice.13.gate_a
  24.2 1.6 dynamic_update_slice.15.gate_x
  25.9 1.3 fusion.42.place
  27.1 79.9 %head.1 = (bf16[8,256,2048]{2,1,0:T(8,128)(2,1)}, bf16[8,256,2048]{2,1,0:T(8,128)(2,1)}) custom-call(bf16[1024,2048]{1,0:T(8,128)(2,1)} %bitcast.96, bf16[1024,2048]{1,0:T(8,128)(2,1)} %bitcast.97, f32[1,2048]{1,0:T(1,128)} %bitcast.103), custom_call_target="tpu_custom_call" | custom-call | flops 42949672960 | bytes 67108864 | tf_op jit(solution)/shard_map/head/pallas_call | solution.py:210
  107.7 11.3 %fusion.44.pre.pre_tail = f32[2048,640]{1,0:T(8,128)} fusion(bf16[2048,2048]{1,0:T(8,128)(2,1)} %bitcast.105, bf16[2048,960]{1,0:T(8,128)(2,1)} %all-gather.6.cloned.1.call-done), kind=kOutput, calls=%fused_computation.118 | convolution fusion | flops 5368709120 | bytes 16252928 | tf_op jit(solution)/shard_map/dot_general | solution.py:21
  119.0 19.0 %mixer.1 = (bf16[2048,320]{1,0:T(8,128)(2,1)}, f32[2048,320]{1,0:T(8,128)}, f32[2048,320]{1,0:T(8,128)}, f32[2048,320]{1,0:T(8,128)}, bf16[2048,320]{1,0:T(8,128)(2,1)}) custom-call(s32[8]{0:T(128)} %fusion.42.place, f32[2048,640]{1,0:T(8,128)} %fusion.44.pre.pre_tail, f32[2048,8]{1,0:T(8,128)} %convert_element_type.77.masks, f32[8,320]{1,0:T(8,128)} %concatenate.32.params, ...), custom_call_target="tpu_custom_call" | custom-call | flops 917504000 | bytes 15728640 | tf_op jit(solution)/shard_map/mixer/pallas_call | solution.py:678
  138.0 2.7 slice.230.refs_1_.w_out
  140.7 90.0 %plane_sum.3 = (bf16[8,256,2048]{2,1,0:T(8,128)(2,1)}, f32[256,2048]{1,0:T(8,128)}) custom-call(bf16[2048,320]{1,0:T(8,128)(2,1)} %get-tuple-element.80.refs_0_, bf16[2048,320]{1,0:T(8,128)(2,1)} %slice.230.refs_1_.w_out, bf16[256,2048]{1,0:T(8,128)(2,1)} %dynamic-slice_bitcast_fusion.1.refs_2_.refs_3_, ...), custom_call_target="tpu_custom_call" | custom-call | flops 77309411328 | bytes 4194304 | tf_op jit(solution)/shard_map/plane_sum/pallas_call | solution.py:399
  230.7 3.5 slice.229.refs_1_
  234.2 17.4 %fusion.46 = f32[2048,1536]{1,0:T(8,128)S(1)} fusion(bf16[2048,2048]{1,0:T(8,128)(2,1)} %bitcast.109, bf16[2048,1536]{1,0:T(8,128)(2,1)} %all-gather.8.cloned.1.call-done.refs_2_), kind=kOutput, calls=%fused_computation.120 | convolution fusion | flops 12884901888 | bytes 27262976 | tf_op jit(solution)/shard_map/dot_general | solution.py:21
  251.6 2.6 multiply_convert_fusion.1
  254.3 1.9 copy-done.6
  256.2 1.7 copy-done.8
  257.9 10.5 %convolution_convert_fusion.2 = bf16[768,2048]{1,0:T(8,128)(2,1)} fusion(bf16[2048,768]{1,0:T(8,128)(2,1)S(1)} %multiply_convert_fusion.1, bf16[2048,2048]{1,0:T(8,128)(2,1)} %bitcast.107), kind=kOutput, calls=%fused_computation.23 | convolution fusion | flops 6444023808 | bytes 14680064 | tf_op jit(solution)/shard_map/dot_general | solution.py:25
  268.3 6.6 %all-gather.4.cloned.1.call-done = bf16[768,2048]{1,0:T(8,128)(2,1)} async-done(((bf16[768,512]{1,0:T(8,128)(2,1)}), bf16[768,2048]{1,0:T(8,128)(2,1)}) %all-gather.4.cloned.1.call-update) | async-done | bytes 3145744 | tf_op jit(solution)/shard_map/all_gather | solution.py:777
  275.0 16.2 %multiply_convert_fusion = (bf16[2048,768]{1,0:T(8,128)(2,1)S(1)}, bf16[2048,768]{1,0:T(8,128)(2,1)S(1)}) fusion(f32[2048,1536]{1,0:T(8,128)} %copy-done.6, bf16[2048,2048]{1,0:T(8,128)(2,1)} %bitcast.108, bf16[768,2048]{1,0:T(8,128)(2,1)} %all-gather.4.cloned.1.call-done), kind=kOutput, calls=%fused_computation.16 | convolution fusion | flops 6478626816 | bytes 30408704 | tf_op jit(solution)/shard_map/dot_general | solution.py:29
  291.3 4.9 convolution_convert_fusion.1
  296.2 17.8 %convolution_convert_fusion = bf16[2048,1536]{1,0:T(8,128)(2,1)} fusion(bf16[2048,2048]{1,0:T(8,128)(2,1)} %bitcast.110, bf16[2048,768]{1,0:T(8,128)(2,1)S(1)} %get-tuple-element.94.refs_1_, bf16[2048,768]{1,0:T(8,128)(2,1)S(1)} %get-tuple-element.93.refs_0_), kind=kOutput, calls=%fused_computation.2 | convolution fusion | flops 12900630528 | bytes 20971520 | tf_op jit(solution)/shard_map/dot_general | solution.py:25
  314.3 6.1 add_convert_fusion
  320.4 1.4 collective-permute-start.1
  321.8 5.7 convert_add_fusion
  327.5 98.9 %plane_sum.4 = (bf16[8,256,2048]{2,1,0:T(8,128)(2,1)}, f32[256,2048]{1,0:T(8,128)}, f32[8,2048]{1,0:T(8,128)}) custom-call(bf16[2048,768]{1,0:T(8,128)(2,1)} %copy-done.32, bf16[2048,768]{1,0:T(8,128)(2,1)} %copy-done.31, bf16[2048,1536]{1,0:T(8,128)(2,1)} %all-gather.8.cloned.1.call-done.refs_2_, bf16[256,2048]{1,0:T(8,128)(2,1)} %dynamic-slice_bitcast_fusion.refs_3_, ...), custom_call_target="tpu_custom_call" | custom-call | flops 77309411328 | bytes 4194304 | tf_op jit(solution)/shard_map/plane_sum/pallas_call | solution.py:399
  426.4 2.3 add_convert_fusion.2
  429.3 7.4 %convolution_convert_fusion.4 = bf16[320,2048]{1,0:T(8,128)(2,1)} fusion(bf16[2048,320]{1,0:T(8,128)(2,1)S(1)} %copy-done.30, bf16[2048,2048]{1,0:T(8,128)(2,1)} %bitcast.84), kind=kOutput, calls=%fused_computation.26 | convolution fusion | flops 2685009920 | bytes 11010048 | tf_op jit(solution)/shard_map/dot_general | solution.py:25
  437.6 11.5 %reduce-scatter.7.cloned.1.call-done.refs_7_ = bf16[512,1536]{1,0:T(8,128)(2,1)} async-done(((bf16[2048,1536]{1,0:T(8,128)(2,1)}), bf16[512,1536]{1,0:T(8,128)(2,1)}) %reduce-scatter.7.cloned.1.call-update) | async-done | bytes 1572880 | tf_op jit(solution)/shard_map/reduce_scatter | solution.py:768
  449.0 3.1 add_convert_fusion.1.refs_5_
  452.1 1.5 collective-permute-start.3
  453.7 1.5 collective-permute-start.5
  455.2 31.9 %mixer_back.1 = (bf16[2048,640]{1,0:T(8,128)(2,1)}, f32[64,320]{1,0:T(8,128)}, f32[320,320]{1,0:T(8,128)}, f32[320,320]{1,0:T(8,128)}) custom-call(s32[8]{0:T(128)} %fusion.42.place, bf16[2048,2048]{1,0:T(8,128)(2,1)} %bitcast.85, bf16[2048,320]{1,0:T(8,128)(2,1)} %slice.230.refs_1_.w_out, f32[2048,640]{1,0:T(8,128)} %fusion.44.pre.pre_tail, ...), custom_call_target="tpu_custom_call" | custom-call | flops 4493148160 | bytes 22282240 | tf_op jit(solution)/shard_map/mixer_back/pallas_call | solution.py:716
  487.1 1.4 fusion.29
  489.6 10.6 %convolution_convert_fusion.3 = bf16[2048,640]{1,0:T(8,128)(2,1)S(1)} fusion(bf16[2048,2048]{1,0:T(8,128)(2,1)} %bitcast.106, bf16[2048,640]{1,0:T(8,128)(2,1)} %get-tuple-element.119.refs_0_), kind=kOutput, calls=%fused_computation.24 | convolution fusion | flops 5370019840 | bytes 13631488 | tf_op jit(solution)/shard_map/dot_general | solution.py:25
  500.3 1.9 maximum_maximum_fusion
  502.2 52.8 %plane_sum.5 = (bf16[256,2048]{1,0:T(8,128)(2,1)}, f32[8,2048]{1,0:T(8,128)}, bf16[4,256,2048]{2,1,0:T(8,128)(2,1)}, bf16[512,1536]{1,0:T(8,128)(2,1)}, bf16[512...) custom-call(bf16[2048,640]{1,0:T(8,128)(2,1)} %get-tuple-element.119.refs_0_, ...), custom_call_target="tpu_custom_call" | custom-call | flops 42949672960 | bytes 4194304 | tf_op jit(solution)/shard_map/plane_sum/pallas_call | solution.py:399
  555.1 3.6 convert_element_type.100
  558.7 2.1 convert_element_type.101
  560.8 2.1 convert_element_type.99
  562.9 1.2 convert_element_type.98
  565.2 34.3 %last.1 = (bf16[512,640]{1,0:T(8,128)(2,1)S(1)}, bf16[2,4,48,640]{3,2,1,0:T(8,128)(2,1)S(1)}, f32[8,512]{1,0:T(8,128)S(1)}, bf16[4,256,2048]{2,1,0:T(8,128)(2,1)S(1)}) custom-call(bf16[560,640]{1,0:T(8,128)(2,1)S(1)} %copy-done.2, f32[8,2048]{1,0:T(8,128)S(1)} %copy-done.5, f32[8,2048]{1,0:T(8,128)S(1)} %copy-done.4, bf16[256,2048]{1,0:T(8,128)(2,1)S(1)} %copy-done.3), custom_call_target="tpu_custom_call" | custom-call | flops 8589934592 | bytes 4194304 | tf_op jit(solution)/shard_map/last/pallas_call | solution.py:511
  603.9 1.3 maximum_convert_fusion.1
  605.2 1.3 maximum_convert_fusion
  608.3 2.0 copy.65
  610.3 2.0 copy.66
  (142 shorter events, 15.6 us)
Async XLA Ops:
  7.2 7.1 %copy-start = (bf16[1536,512]{1,0:T(8,128)(2,1)S(1)}, bf16[1536,512]{1,0:T(8,128)(2,1)}, u32[]{:S(2)}) copy-start(bf16[1536,512]{1,0:T(8,128)(2,1)} %param.36) | copy-start | bytes 4718596
  7.2 100.4 %all-gather.6.cloned.1.call-start = ((), (), s32[]{:S(2)}) async-start(), calls=%async_computation.5 | async-start | bytes 5242880 | tf_op jit(solution)/shard_map/all_gather | solution.py:774
  8.6 3.0 copy-start.16
  11.6 222.7 %all-gather.8.cloned.1.call-start = ((), (), s32[]{:S(2)}) async-start(), calls=%async_computation.6 | async-start | bytes 7864320 | tf_op jit(solution)/shard_map/all_gather | solution.py:776
  12.9 2.5 copy-start.19
  12.9 2.6 copy-start.22
  12.9 2.6 copy-start.23
  12.9 2.7 copy-start.24
  12.9 2.8 copy-start.25
  12.9 2.8 copy-start.17
  12.9 2.8 copy-start.18
  13.0 2.9 copy-start.21
  14.3 260.7 %all-gather.4.cloned.1.call-start = ((), (), s32[]{:S(2)}) async-start(), calls=%async_computation.4 | async-start | bytes 3932160 | tf_op jit(solution)/shard_map/all_gather | solution.py:777
  15.3 421.5 %reduce-scatter.5.cloned.1.call-start = ((), (), s32[]{:S(2)}) async-start(), calls=%async_computation.7 | async-start | bytes 3932160 | tf_op jit(solution)/shard_map/reduce_scatter | solution.py:768
  24.2 82.8 %copy-start.14 = (bf16[320,320]{1,0:T(8,128)(2,1)}, bf16[320,320]{1,0:T(8,128)(2,1)S(1)}, u32[]{:S(2)}) copy-start(bf16[320,320]{1,0:T(8,128)(2,1)S(1)} %dynamic_update_slice.13.gate_a) | copy-start | bytes 614404
  25.9 81.2 %copy-start.13 = (bf16[320,320]{1,0:T(8,128)(2,1)}, bf16[320,320]{1,0:T(8,128)(2,1)S(1)}, u32[]{:S(2)}) copy-start(bf16[320,320]{1,0:T(8,128)(2,1)S(1)} %dynamic_update_slice.15.gate_x) | copy-start | bytes 614404
  251.6 4.6 copy-start.6
  256.2 1.7 copy-start.8
  274.9 174.1 %reduce-scatter.7.cloned.1.call-start = ((), (), s32[]{:S(2)}) async-start(), calls=%async_computation.8 | async-start | bytes 7864320 | tf_op jit(solution)/shard_map/reduce_scatter | solution.py:768
  275.0 16.3 %copy-start.9 = (bf16[2048,768]{1,0:T(8,128)(2,1)S(1)}, bf16[2048,768]{1,0:T(8,128)(2,1)}, u32[]{:S(2)}) copy-start(bf16[2048,768]{1,0:T(8,128)(2,1)} %copy-done.8) | copy-start | bytes 9437188
  275.0 16.3 %copy-start.26 = (bf16[768,2048]{1,0:T(8,128)(2,1)S(1)}, bf16[768,2048]{1,0:T(8,128)(2,1)}, u32[]{:S(2)}) copy-start(bf16[768,2048]{1,0:T(8,128)(2,1)} %all-gather.4.cloned.1.call-done) | copy-start | bytes 9437188
  291.2 5.0 copy-start.31
  291.2 5.0 copy-start.32
  296.2 18.1 %collective-permute-start = (bf16[1024,2048]{1,0:T(8,128)(2,1)}, bf16[1024,2048]{1,0:T(8,128)(2,1)}, u32[]{:S(2)}, u32[]{:S(2)}) collective-permute-start(bf16[1024,2048]{1,0:T(8,128)(2,1)} %convolution_convert_fusion.1), channel_id=1, source_target_pairs={{0,1},{1,0},{2,3},{3,2},{4,5},{5,4},{6,7},{7,6},{8,9},{9,8},{10,11... | collective-permute-start | bytes 12582920 | tf_op jit(solution)/shard_map/ppermute | solution.py:70
  314.0 188.2 %reduce-scatter.9.cloned.1.call-start = ((), (), s32[]{:S(2)}) async-start(), calls=%async_computation.9 | async-start | bytes 1638400 | tf_op jit(solution)/shard_map/reduce_scatter | solution.py:768
  314.3 7.5 %copy-start.27 = (bf16[768,2048]{1,0:T(8,128)(2,1)S(1)}, bf16[768,2048]{1,0:T(8,128)(2,1)}, u32[]{:S(2)}) copy-start(bf16[768,2048]{1,0:T(8,128)(2,1)} %all-gather.4.cloned.1.call-done) | copy-start | bytes 9437188
  320.4 106.0 %collective-permute-start.1 = (bf16[512,2048]{1,0:T(8,128)(2,1)}, bf16[512,2048]{1,0:T(8,128)(2,1)}, u32[]{:S(2)}, u32[]{:S(2)}) collective-permute-start(bf16[512,2048]{1,0:T(8,128)(2,1)} %add_convert_fusion), channel_id=1, source_target_pairs={{0,4},{1,3},{2,6},{3,1},{4,0},{5,7},{6,2},{7,5},{8,12},{9,11},{10,... | collective-permute-start | bytes 6291464 | tf_op jit(solution)/shard_map/ppermute | solution.py:70
  426.4 2.9 copy-start.30
  428.7 20.4 %collective-permute-start.2 = (bf16[256,2048]{1,0:T(8,128)(2,1)S(1)}, bf16[256,2048]{1,0:T(8,128)(2,1)S(1)}, u32[]{:S(2)}, u32[]{:S(2)}) collective-permute-start(bf16[256,2048]{1,0:T(8,128)(2,1)S(1)} %add_convert_fusion.2), channel_id=1, source_target_pairs={{0,2},{1,5},{2,0},{3,7},{4,6},{5,1},{6,4},{7,3},{8,10},{9,13},{10,... | collective-permute-start | bytes 3145736 | tf_op jit(solution)/shard_map/ppermute | solution.py:70
  436.7 52.8 %collective-permute-start.4 = (bf16[768,512]{1,0:T(8,128)(2,1)}, bf16[768,512]{1,0:T(8,128)(2,1)S(1)}, u32[]{:S(2)}, u32[]{:S(2)}) collective-permute-start(bf16[768,512]{1,0:T(8,128)(2,1)} %reduce-scatter.5.cloned.1.call-done.refs_9_), channel_id=1, source_target_pairs={{0,4},{1,5},{2,6},{3,7},{4,0},{5,1},{6,2},{7,3},{8,12},{9,13},{10,... | collective-permute-start | bytes 2359304 | tf_op jit(solution)/shard_map/ppermute | solution.py:74
  437.3 126.8 %reduce-scatter.11.cloned.1.call-start = ((), (), s32[]{:S(2)}) async-start(), calls=%async_computation.10 | async-start | bytes 3584000 | tf_op jit(solution)/shard_map/reduce_scatter | solution.py:768
  452.1 34.9 %copy-start.12 = (bf16[256,2048]{1,0:T(8,128)(2,1)}, bf16[256,2048]{1,0:T(8,128)(2,1)S(1)}, u32[]{:S(2)}) copy-start(bf16[256,2048]{1,0:T(8,128)(2,1)S(1)} %add_convert_fusion.1.refs_5_) | copy-start | bytes 3145732
  452.1 37.4 %collective-permute-start.3 = (bf16[256,2048]{1,0:T(8,128)(2,1)S(1)}, bf16[256,2048]{1,0:T(8,128)(2,1)S(1)}, u32[]{:S(2)}, u32[]{:S(2)}) collective-permute-start(bf16[256,2048]{1,0:T(8,128)(2,1)S(1)} %add_convert_fusion.1.refs_5_), channel_id=1, source_target_pairs={{0,2},{1,3},{2,0},{3,1},{4,6},{5,7},{6,4},{7,5},{8,10},{9,11},{10,... | collective-permute-start | bytes 3145736 | tf_op jit(solution)/shard_map/ppermute | solution.py:74
  453.7 48.5 %collective-permute-start.5 = (bf16[512,1536]{1,0:T(8,128)(2,1)}, bf16[512,1536]{1,0:T(8,128)(2,1)}, u32[]{:S(2)}, u32[]{:S(2)}) collective-permute-start(bf16[512,1536]{1,0:T(8,128)(2,1)} %reduce-scatter.7.cloned.1.call-done.refs_7_), channel_id=1, source_target_pairs={{0,4},{1,5},{2,6},{3,7},{4,0},{5,1},{6,2},{7,3},{8,12},{9,13},{10,... | collective-permute-start | bytes 4718600 | tf_op jit(solution)/shard_map/ppermute | solution.py:74
  489.6 10.7 %copy-start.29 = (bf16[768,512]{1,0:T(8,128)(2,1)}, bf16[768,512]{1,0:T(8,128)(2,1)S(1)}, u32[]{:S(2)}) copy-start(bf16[768,512]{1,0:T(8,128)(2,1)S(1)} %collective-permute-done.4.refs_10_) | copy-start | bytes 2359300
  489.6 10.7 %copy-start.28 = (bf16[256,2048]{1,0:T(8,128)(2,1)}, bf16[256,2048]{1,0:T(8,128)(2,1)S(1)}, u32[]{:S(2)}) copy-start(bf16[256,2048]{1,0:T(8,128)(2,1)S(1)} %collective-permute-done.3.refs_6_) | copy-start | bytes 3145732
  555.0 3.7 copy-start.11
  555.0 5.8 copy-start.10
  558.7 4.2 copy-start.15
  560.8 3.3 copy-start.3
  560.8 3.3 copy-start.4
  560.8 3.3 copy-start.5
  564.1 1.1 copy-start.2
  599.5 2.2 copy-start.20
  603.9 4.3 copy-start.7
  608.3 4.0 copy-start.1
Sparse Core Ops, SparseCore 0:
  11.7 83.3 all-gather.5
  97.2 113.8 all-gather.7
  213.3 61.6 all-gather.3
  277.1 59.0 reduce-scatter.4
  338.3 110.6 reduce-scatter.6
  451.8 31.8 reduce-scatter.8
  502.3 54.9 reduce-scatter.10

commit v7 on v6

--- a/solution.py
+++ b/solution.py
@@ -844,9 +844,10 @@
     grad_proj, own_down, grad_w_out = tied((grad_proj, own_down, grad_w_out))
     own_out = owned(grad_w_out, 1)
     other_down = flip(own_down, 4)
-    low, own_gu, grad_w_out = tied((low, own_gu, grad_w_out))
+    low, grad_w_out = tied((low, grad_w_out))
+    output = (resid + low[:rows] + got_far[:rows].astype(F32) + got_near.astype(F32)).astype(BF16)
+    output, own_gu = tied((output, own_gu))
     other_gu = flip(own_gu, 4)
-    output = (resid + low[:rows] + got_far[:rows].astype(F32) + got_near.astype(F32)).astype(BF16)
     states, output = tied((states, output))
     output_along = flip(output, 2)
     grads_in, sums, sum_a, sum_x = mixer_back(

time: 623 us -> 619 us (level)
    reduce_scatter x4, waiting for transfers between devices: 11.5 us -> 2.39 us  [owned(): return lax.psum_scatter(x, 'fsdp', scatter_dimension=axis, tiled=True)]
  transfers between devices with their start and end apart: 13 -> 13, of which waited for: 2 -> 3; matrix products, arithmetic and copies ran while one was open for 24% -> 25% of each run, Pallas kernels for 60% -> 60%
where the time goes in v7:
time: 619 us; the launch traced here: 616 us
  Pallas kernels  407 us (66%)
  matrix products  108 us (17%)
  local copies, waits for them, and re-layouts  33.2 us (5%)
  other arithmetic  32 us (5%)
  waiting for transfers between devices  15.1 us (2%)
  between operations  15 us (2%)
  starting transfers between devices  6.2 us (1%)
    pallas_call x3, Pallas kernels, plane_sum(): pl.pallas_call(functools.partial(plane_sum_kernel, epilogue, wide, len(le...  242 us
    pallas_call x1, Pallas kernels, head(): pl.pallas_call(head_kernel, in_specs=[anywhere, anywhere, pl.BlockSpec(me...  79.9 us
    dot_general x4, matrix products, left_inner(): lax.dot_general(left, right, (((0,), (0,)), ((), ())), preferred_element_...  46.3 us
    dot_general x5, matrix products, matmul(): return jnp.dot(left, right, preferred_element_type=F32)  45.4 us
    pallas_call x1, Pallas kernels, last(): pl.pallas_call(functools.partial(last_kernel, size, deep), in_specs=[anyw...  34.3 us
    pallas_call x1, Pallas kernels, mixer_back(): pl.pallas_call(mixer_back_kernel, grid_spec=pltpu.PrefetchScalarGridSpec(...  31.7 us
    pallas_call x1, Pallas kernels, mixer(): pl.pallas_call(mixer_kernel, grid_spec=pltpu.PrefetchScalarGridSpec(num_s...  19 us
    dot_general x1, matrix products, right_inner(): lax.dot_general(left, right, (((1,), (1,)), ((), ())), preferred_element_...  16.2 us
  transfers between devices with their start and end apart: 13, of which 3 were waited for; matrix products, arithmetic and copies ran while one was open for 25% of the time, Pallas kernels for 60%

profile of v7, /device:TPU:0, one launch (start us, length us, event | category | flops | bytes accessed | tf_op | source)
XLA Modules:
  0.0 616.0 jit_solution(5223612752311534348)
XLA Ops:
  8.6 1.7 constant_dynamic-slice_fusion.4
  10.3 1.3 pad_maximum_fusion.1
  11.6 1.2 constant_dynamic-slice_fusion
  13.0 1.3 pad_maximum_fusion
  17.7 2.3 dynamic-slice_bitcast_fusion.1.refs_2_.refs_3_
  20.0 2.4 dynamic-slice_bitcast_fusion.refs_3_
  22.5 1.8 dynamic_update_slice.13.gate_a
  24.2 1.6 dynamic_update_slice.15.gate_x
  25.9 1.3 fusion.42.place
  27.1 79.9 %head.1 = (bf16[8,256,2048]{2,1,0:T(8,128)(2,1)}, bf16[8,256,2048]{2,1,0:T(8,128)(2,1)}) custom-call(bf16[1024,2048]{1,0:T(8,128)(2,1)} %bitcast.96, bf16[1024,2048]{1,0:T(8,128)(2,1)} %bitcast.97, f32[1,2048]{1,0:T(1,128)} %bitcast.103), custom_call_target="tpu_custom_call" | custom-call | flops 42949672960 | bytes 67108864 | tf_op jit(solution)/shard_map/head/pallas_call | solution.py:210
  107.7 11.3 %fusion.44.pre.pre_tail = f32[2048,640]{1,0:T(8,128)} fusion(bf16[2048,2048]{1,0:T(8,128)(2,1)} %bitcast.105, bf16[2048,960]{1,0:T(8,128)(2,1)} %all-gather.6.cloned.1.call-done), kind=kOutput, calls=%fused_computation.118 | convolution fusion | flops 5368709120 | bytes 16252928 | tf_op jit(solution)/shard_map/dot_general | solution.py:21
  119.0 19.0 %mixer.1 = (bf16[2048,320]{1,0:T(8,128)(2,1)}, f32[2048,320]{1,0:T(8,128)}, f32[2048,320]{1,0:T(8,128)}, f32[2048,320]{1,0:T(8,128)}, bf16[2048,320]{1,0:T(8,128)(2,1)}) custom-call(s32[8]{0:T(128)} %fusion.42.place, f32[2048,640]{1,0:T(8,128)} %fusion.44.pre.pre_tail, f32[2048,8]{1,0:T(8,128)} %convert_element_type.77.masks, f32[8,320]{1,0:T(8,128)} %concatenate.32.params, ...), custom_call_target="tpu_custom_call" | custom-call | flops 917504000 | bytes 15728640 | tf_op jit(solution)/shard_map/mixer/pallas_call | solution.py:678
  138.0 2.7 slice.230.refs_1_.w_out
  140.7 90.0 %plane_sum.3 = (bf16[8,256,2048]{2,1,0:T(8,128)(2,1)}, f32[256,2048]{1,0:T(8,128)}) custom-call(bf16[2048,320]{1,0:T(8,128)(2,1)} %get-tuple-element.81.refs_0_, bf16[2048,320]{1,0:T(8,128)(2,1)} %slice.230.refs_1_.w_out, bf16[256,2048]{1,0:T(8,128)(2,1)} %dynamic-slice_bitcast_fusion.1.refs_2_.refs_3_, ...), custom_call_target="tpu_custom_call" | custom-call | flops 77309411328 | bytes 4194304 | tf_op jit(solution)/shard_map/plane_sum/pallas_call | solution.py:399
  230.7 3.5 slice.229.refs_1_
  234.2 17.4 %fusion.46 = f32[2048,1536]{1,0:T(8,128)S(1)} fusion(bf16[2048,2048]{1,0:T(8,128)(2,1)} %bitcast.109, bf16[2048,1536]{1,0:T(8,128)(2,1)} %all-gather.8.cloned.1.call-done.refs_2_), kind=kOutput, calls=%fused_computation.120 | convolution fusion | flops 12884901888 | bytes 27262976 | tf_op jit(solution)/shard_map/dot_general | solution.py:21
  251.6 2.6 multiply_convert_fusion.1
  254.3 1.9 copy-done.6
  256.2 1.7 copy-done.8
  257.9 10.5 %convolution_convert_fusion.2 = bf16[768,2048]{1,0:T(8,128)(2,1)} fusion(bf16[2048,768]{1,0:T(8,128)(2,1)S(1)} %multiply_convert_fusion.1, bf16[2048,2048]{1,0:T(8,128)(2,1)} %bitcast.107), kind=kOutput, calls=%fused_computation.23 | convolution fusion | flops 6444023808 | bytes 14680064 | tf_op jit(solution)/shard_map/dot_general | solution.py:25
  268.3 6.6 %all-gather.4.cloned.1.call-done = bf16[768,2048]{1,0:T(8,128)(2,1)} async-done(((bf16[768,512]{1,0:T(8,128)(2,1)}), bf16[768,2048]{1,0:T(8,128)(2,1)}) %all-gather.4.cloned.1.call-update) | async-done | bytes 3145744 | tf_op jit(solution)/shard_map/all_gather | solution.py:777
  275.0 16.2 %multiply_convert_fusion = (bf16[2048,768]{1,0:T(8,128)(2,1)S(1)}, bf16[2048,768]{1,0:T(8,128)(2,1)S(1)}) fusion(f32[2048,1536]{1,0:T(8,128)} %copy-done.6, bf16[2048,2048]{1,0:T(8,128)(2,1)} %bitcast.108, bf16[768,2048]{1,0:T(8,128)(2,1)} %all-gather.4.cloned.1.call-done), kind=kOutput, calls=%fused_computation.16 | convolution fusion | flops 6478626816 | bytes 30408704 | tf_op jit(solution)/shard_map/dot_general | solution.py:29
  291.3 4.9 convolution_convert_fusion.1
  296.2 17.8 %convolution_convert_fusion = bf16[2048,1536]{1,0:T(8,128)(2,1)} fusion(bf16[2048,2048]{1,0:T(8,128)(2,1)} %bitcast.110, bf16[2048,768]{1,0:T(8,128)(2,1)S(1)} %get-tuple-element.95.refs_1_, bf16[2048,768]{1,0:T(8,128)(2,1)S(1)} %get-tuple-element.94.refs_0_), kind=kOutput, calls=%fused_computation.2 | convolution fusion | flops 12900630528 | bytes 20971520 | tf_op jit(solution)/shard_map/dot_general | solution.py:25
  314.3 6.1 add_convert_fusion
  320.4 1.4 collective-permute-start.1
  321.8 5.7 convert_add_fusion
  327.5 98.9 %plane_sum.4 = (bf16[8,256,2048]{2,1,0:T(8,128)(2,1)}, f32[256,2048]{1,0:T(8,128)}, f32[8,2048]{1,0:T(8,128)}) custom-call(bf16[2048,768]{1,0:T(8,128)(2,1)} %copy-done.32, bf16[2048,768]{1,0:T(8,128)(2,1)} %copy-done.31, bf16[2048,1536]{1,0:T(8,128)(2,1)} %all-gather.8.cloned.1.call-done.refs_2_, bf16[256,2048]{1,0:T(8,128)(2,1)} %dynamic-slice_bitcast_fusion.refs_3_, ...), custom_call_target="tpu_custom_call" | custom-call | flops 77309411328 | bytes 4194304 | tf_op jit(solution)/shard_map/plane_sum/pallas_call | solution.py:399
  426.4 2.3 add_convert_fusion.2
  429.3 7.4 %convolution_convert_fusion.4 = bf16[320,2048]{1,0:T(8,128)(2,1)} fusion(bf16[2048,320]{1,0:T(8,128)(2,1)S(1)} %copy-done.30, bf16[2048,2048]{1,0:T(8,128)(2,1)} %bitcast.84), kind=kOutput, calls=%fused_computation.26 | convolution fusion | flops 2685009920 | bytes 11010048 | tf_op jit(solution)/shard_map/dot_general | solution.py:25
  437.6 6.0 collective-permute-done.2
  443.5 3.1 add_convert_fusion.1.refs_5_
  446.6 2.4 reduce-scatter.7.cloned.1.call-done.refs_7_
  449.0 1.5 collective-permute-start.3
  450.5 1.5 collective-permute-start.5
  452.0 31.7 %mixer_back.1 = (bf16[2048,640]{1,0:T(8,128)(2,1)}, f32[64,320]{1,0:T(8,128)}, f32[320,320]{1,0:T(8,128)}, f32[320,320]{1,0:T(8,128)}) custom-call(s32[8]{0:T(128)} %fusion.42.place, bf16[2048,2048]{1,0:T(8,128)(2,1)} %bitcast.85, bf16[2048,320]{1,0:T(8,128)(2,1)} %slice.230.refs_1_.w_out, f32[2048,640]{1,0:T(8,128)} %fusion.44.pre.pre_tail, ...), custom_call_target="tpu_custom_call" | custom-call | flops 4493148160 | bytes 22282240 | tf_op jit(solution)/shard_map/mixer_back/pallas_call | solution.py:716
  483.7 1.4 fusion.29
  486.2 10.6 %convolution_convert_fusion.3 = bf16[2048,640]{1,0:T(8,128)(2,1)S(1)} fusion(bf16[2048,2048]{1,0:T(8,128)(2,1)} %bitcast.106, bf16[2048,640]{1,0:T(8,128)(2,1)} %get-tuple-element.121.refs_0_), kind=kOutput, calls=%fused_computation.24 | convolution fusion | flops 5370019840 | bytes 13631488 | tf_op jit(solution)/shard_map/dot_general | solution.py:25
  496.9 1.9 maximum_maximum_fusion
  498.8 52.8 %plane_sum.5 = (bf16[256,2048]{1,0:T(8,128)(2,1)}, f32[8,2048]{1,0:T(8,128)}, bf16[4,256,2048]{2,1,0:T(8,128)(2,1)}, bf16[512,1536]{1,0:T(8,128)(2,1)}, bf16[512...) custom-call(bf16[2048,640]{1,0:T(8,128)(2,1)} %get-tuple-element.121.refs_0_, ...), custom_call_target="tpu_custom_call" | custom-call | flops 42949672960 | bytes 4194304 | tf_op jit(solution)/shard_map/plane_sum/pallas_call | solution.py:399
  551.7 3.6 convert_element_type.100
  555.3 2.1 convert_element_type.101
  557.4 2.1 convert_element_type.99
  561.8 34.3 %last.1 = (bf16[512,640]{1,0:T(8,128)(2,1)S(1)}, bf16[2,4,48,640]{3,2,1,0:T(8,128)(2,1)S(1)}, f32[8,512]{1,0:T(8,128)S(1)}, bf16[4,256,2048]{2,1,0:T(8,128)(2,1)S(1)}) custom-call(bf16[560,640]{1,0:T(8,128)(2,1)S(1)} %copy-done.2, f32[8,2048]{1,0:T(8,128)S(1)} %copy-done.5, f32[8,2048]{1,0:T(8,128)S(1)} %copy-done.4, bf16[256,2048]{1,0:T(8,128)(2,1)S(1)} %copy-done.3), custom_call_target="tpu_custom_call" | custom-call | flops 8589934592 | bytes 4194304 | tf_op jit(solution)/shard_map/last/pallas_call | solution.py:511
  600.5 1.3 maximum_convert_fusion.1
  601.8 1.3 maximum_convert_fusion
  604.9 2.0 copy.65
  606.9 2.0 copy.66
  (142 shorter events, 16.9 us)
Async XLA Ops:
  7.2 7.1 %copy-start = (bf16[1536,512]{1,0:T(8,128)(2,1)S(1)}, bf16[1536,512]{1,0:T(8,128)(2,1)}, u32[]{:S(2)}) copy-start(bf16[1536,512]{1,0:T(8,128)(2,1)} %param.36) | copy-start | bytes 4718596
  7.2 100.4 %all-gather.6.cloned.1.call-start = ((), (), s32[]{:S(2)}) async-start(), calls=%async_computation.5 | async-start | bytes 5242880 | tf_op jit(solution)/shard_map/all_gather | solution.py:774
  8.6 3.0 copy-start.16
  11.6 222.7 %all-gather.8.cloned.1.call-start = ((), (), s32[]{:S(2)}) async-start(), calls=%async_computation.6 | async-start | bytes 7864320 | tf_op jit(solution)/shard_map/all_gather | solution.py:776
  12.9 2.5 copy-start.19
  12.9 2.6 copy-start.22
  12.9 2.6 copy-start.23
  12.9 2.7 copy-start.24
  12.9 2.8 copy-start.25
  12.9 2.8 copy-start.17
  12.9 2.8 copy-start.18
  13.0 2.9 copy-start.21
  14.3 260.7 %all-gather.4.cloned.1.call-start = ((), (), s32[]{:S(2)}) async-start(), calls=%async_computation.4 | async-start | bytes 3932160 | tf_op jit(solution)/shard_map/all_gather | solution.py:777
  15.3 421.5 %reduce-scatter.5.cloned.1.call-start = ((), (), s32[]{:S(2)}) async-start(), calls=%async_computation.7 | async-start | bytes 3932160 | tf_op jit(solution)/shard_map/reduce_scatter | solution.py:768
  24.2 82.8 %copy-start.14 = (bf16[320,320]{1,0:T(8,128)(2,1)}, bf16[320,320]{1,0:T(8,128)(2,1)S(1)}, u32[]{:S(2)}) copy-start(bf16[320,320]{1,0:T(8,128)(2,1)S(1)} %dynamic_update_slice.13.gate_a) | copy-start | bytes 614404
  25.9 81.2 %copy-start.13 = (bf16[320,320]{1,0:T(8,128)(2,1)}, bf16[320,320]{1,0:T(8,128)(2,1)S(1)}, u32[]{:S(2)}) copy-start(bf16[320,320]{1,0:T(8,128)(2,1)S(1)} %dynamic_update_slice.15.gate_x) | copy-start | bytes 614404
  251.6 4.6 copy-start.6
  256.2 1.7 copy-start.8
  274.9 174.1 %reduce-scatter.7.cloned.1.call-start = ((), (), s32[]{:S(2)}) async-start(), calls=%async_computation.8 | async-start | bytes 7864320 | tf_op jit(solution)/shard_map/reduce_scatter | solution.py:768
  275.0 16.3 %copy-start.9 = (bf16[2048,768]{1,0:T(8,128)(2,1)S(1)}, bf16[2048,768]{1,0:T(8,128)(2,1)}, u32[]{:S(2)}) copy-start(bf16[2048,768]{1,0:T(8,128)(2,1)} %copy-done.8) | copy-start | bytes 9437188
  275.0 16.3 %copy-start.26 = (bf16[768,2048]{1,0:T(8,128)(2,1)S(1)}, bf16[768,2048]{1,0:T(8,128)(2,1)}, u32[]{:S(2)}) copy-start(bf16[768,2048]{1,0:T(8,128)(2,1)} %all-gather.4.cloned.1.call-done) | copy-start | bytes 9437188
  291.2 5.0 copy-start.31
  291.2 5.0 copy-start.32
  296.2 18.1 %collective-permute-start = (bf16[1024,2048]{1,0:T(8,128)(2,1)}, bf16[1024,2048]{1,0:T(8,128)(2,1)}, u32[]{:S(2)}, u32[]{:S(2)}) collective-permute-start(bf16[1024,2048]{1,0:T(8,128)(2,1)} %convolution_convert_fusion.1), channel_id=1, source_target_pairs={{0,1},{1,0},{2,3},{3,2},{4,5},{5,4},{6,7},{7,6},{8,9},{9,8},{10,11... | collective-permute-start | bytes 12582920 | tf_op jit(solution)/shard_map/ppermute | solution.py:70
  314.0 184.8 %reduce-scatter.9.cloned.1.call-start = ((), (), s32[]{:S(2)}) async-start(), calls=%async_computation.9 | async-start | bytes 1638400 | tf_op jit(solution)/shard_map/reduce_scatter | solution.py:768
  314.3 7.5 %copy-start.27 = (bf16[768,2048]{1,0:T(8,128)(2,1)S(1)}, bf16[768,2048]{1,0:T(8,128)(2,1)}, u32[]{:S(2)}) copy-start(bf16[768,2048]{1,0:T(8,128)(2,1)} %all-gather.4.cloned.1.call-done) | copy-start | bytes 9437188
  320.4 106.0 %collective-permute-start.1 = (bf16[512,2048]{1,0:T(8,128)(2,1)}, bf16[512,2048]{1,0:T(8,128)(2,1)}, u32[]{:S(2)}, u32[]{:S(2)}) collective-permute-start(bf16[512,2048]{1,0:T(8,128)(2,1)} %add_convert_fusion), channel_id=1, source_target_pairs={{0,4},{1,3},{2,6},{3,1},{4,0},{5,7},{6,2},{7,5},{8,12},{9,11},{10,... | collective-permute-start | bytes 6291464 | tf_op jit(solution)/shard_map/ppermute | solution.py:70
  426.4 2.9 copy-start.30
  428.7 14.9 %collective-permute-start.2 = (bf16[256,2048]{1,0:T(8,128)(2,1)S(1)}, bf16[256,2048]{1,0:T(8,128)(2,1)S(1)}, u32[]{:S(2)}, u32[]{:S(2)}) collective-permute-start(bf16[256,2048]{1,0:T(8,128)(2,1)S(1)} %add_convert_fusion.2), channel_id=1, source_target_pairs={{0,2},{1,5},{2,0},{3,7},{4,6},{5,1},{6,4},{7,3},{8,10},{9,13},{10,... | collective-permute-start | bytes 3145736 | tf_op jit(solution)/shard_map/ppermute | solution.py:70
  436.7 49.4 %collective-permute-start.4 = (bf16[768,512]{1,0:T(8,128)(2,1)}, bf16[768,512]{1,0:T(8,128)(2,1)S(1)}, u32[]{:S(2)}, u32[]{:S(2)}) collective-permute-start(bf16[768,512]{1,0:T(8,128)(2,1)} %reduce-scatter.5.cloned.1.call-done.refs_9_), channel_id=1, source_target_pairs={{0,4},{1,5},{2,6},{3,7},{4,0},{5,1},{6,2},{7,3},{8,12},{9,13},{10,... | collective-permute-start | bytes 2359304 | tf_op jit(solution)/shard_map/ppermute | solution.py:74
  437.3 123.4 %reduce-scatter.11.cloned.1.call-start = ((), (), s32[]{:S(2)}) async-start(), calls=%async_computation.10 | async-start | bytes 3584000 | tf_op jit(solution)/shard_map/reduce_scatter | solution.py:768
  446.6 37.1 %copy-start.12 = (bf16[256,2048]{1,0:T(8,128)(2,1)}, bf16[256,2048]{1,0:T(8,128)(2,1)S(1)}, u32[]{:S(2)}) copy-start(bf16[256,2048]{1,0:T(8,128)(2,1)S(1)} %add_convert_fusion.1.refs_5_) | copy-start | bytes 3145732
  449.0 37.2 %collective-permute-start.3 = (bf16[256,2048]{1,0:T(8,128)(2,1)S(1)}, bf16[256,2048]{1,0:T(8,128)(2,1)S(1)}, u32[]{:S(2)}, u32[]{:S(2)}) collective-permute-start(bf16[256,2048]{1,0:T(8,128)(2,1)S(1)} %add_convert_fusion.1.refs_5_), channel_id=1, source_target_pairs={{0,2},{1,3},{2,0},{3,1},{4,6},{5,7},{6,4},{7,5},{8,10},{9,11},{10,... | collective-permute-start | bytes 3145736 | tf_op jit(solution)/shard_map/ppermute | solution.py:74
  450.5 48.3 %collective-permute-start.5 = (bf16[512,1536]{1,0:T(8,128)(2,1)}, bf16[512,1536]{1,0:T(8,128)(2,1)}, u32[]{:S(2)}, u32[]{:S(2)}) collective-permute-start(bf16[512,1536]{1,0:T(8,128)(2,1)} %reduce-scatter.7.cloned.1.call-done.refs_7_), channel_id=1, source_target_pairs={{0,4},{1,5},{2,6},{3,7},{4,0},{5,1},{6,2},{7,3},{8,12},{9,13},{10,... | collective-permute-start | bytes 4718600 | tf_op jit(solution)/shard_map/ppermute | solution.py:74
  486.2 10.7 %copy-start.29 = (bf16[768,512]{1,0:T(8,128)(2,1)}, bf16[768,512]{1,0:T(8,128)(2,1)S(1)}, u32[]{:S(2)}) copy-start(bf16[768,512]{1,0:T(8,128)(2,1)S(1)} %collective-permute-done.4.refs_10_) | copy-start | bytes 2359300
  486.2 10.7 %copy-start.28 = (bf16[256,2048]{1,0:T(8,128)(2,1)}, bf16[256,2048]{1,0:T(8,128)(2,1)S(1)}, u32[]{:S(2)}) copy-start(bf16[256,2048]{1,0:T(8,128)(2,1)S(1)} %collective-permute-done.3.refs_6_) | copy-start | bytes 3145732
  551.7 3.7 copy-start.11
  551.7 5.8 copy-start.10
  555.3 4.2 copy-start.15
  557.4 3.3 copy-start.3
  557.4 3.3 copy-start.4
  557.4 3.3 copy-start.5
  560.7 1.1 copy-start.2
  596.1 2.2 copy-start.20
  600.5 4.3 copy-start.7
  604.9 4.0 copy-start.1
Sparse Core Ops, SparseCore 0:
  11.7 83.3 all-gather.5
  97.2 113.8 all-gather.7
  213.3 61.6 all-gather.3
  277.1 59.0 reduce-scatter.4
  338.3 110.6 reduce-scatter.6
  451.8 31.8 reduce-scatter.8
  498.9 54.9 reduce-scatter.10
